TPU v7x, 512 devices: a whole 4x8x8 slice. The times are simulated.
512 devices in a mesh: graph: 128 (over z, y, core), sample: 4 (over x).
Axes of the slice: x: 4, y: 8, z: 8, core: 2. Of those that a mesh axis runs over, the one named last changes fastest.
Arguments:
- grid_in: bfloat16 [4, 65536, 256], P('sample', 'graph'), may hold values from -6 to 6
- mesh_init: bfloat16 [4, 16384, 512], P('sample', 'graph'), may hold values from -24 to 24
- g2m_geometry: bfloat16 [4, 131072], P(None, 'graph'), may hold values from -6 to 6
- w_embed: bfloat16 [256, 512], replicated, may hold values from -0.375 to 0.375
- w_g2m: bfloat16 [512, 512], replicated, may hold values from -0.25 to 0.25
- w_geo: bfloat16 [4, 512], replicated, may hold values from -3 to 3
- a_send: bfloat16 [512, 512], replicated, may hold values from -0.25 to 0.25
- a_recv: bfloat16 [512, 512], replicated, may hold values from -0.25 to 0.25
- b_node: bfloat16 [512, 512], replicated, may hold values from -0.25 to 0.25
- cotangent: bfloat16 [4, 16384, 512], P('sample', 'graph'), may hold values from -6 to 6
- g2m_send_rows: int32 [128, 128, 8], P('graph'), may hold values from 0 to 511
- g2m_counts: int32 [128, 128], P('graph'), may hold values from 0 to 8, as said below
- g2m_senders: int32 [131072], P('graph'), may hold values from 0 to 1023
- g2m_receivers: int32 [131072], P('graph'), may hold values from 0 to 127
- mesh_send_rows: int32 [128, 128, 4], P('graph'), may hold values from 0 to 127
- mesh_senders: int32 [65536], P('graph'), may hold values from 0 to 639
- mesh_receivers: int32 [65536], P('graph'), may hold values from 0 to 127
Outputs:
- mesh_out: bfloat16 [4, 16384, 512], P('sample', 'graph')
- grad_mesh: float32 [4, 16384, 512], P('sample', 'graph')
- grad_weights: float32 [1536, 512], P('graph')
Inputs may be any that keep to these rules, and one draw needn't show every extreme that they name: `g2m_send_rows`: entry [b, g, j] is a row of band b's own 512 rows. `g2m_counts`: entry [b, g] is the number of live slots from band b to partition g; every band has some partition at 8, and some partition receives 8 from every band. `g2m_senders`: b * 8 + j names slot j from band b, for the partition that holds the edge. `g2m_receivers`: A node of the partition that holds the edge. `mesh_send_rows`: entry [b, g, j] is a row of partition b's own 128 rows. `mesh_senders`: A row of the holding partition's sender_table: below 512 a row received from another partition, else a local node. `mesh_receivers`: A node of the partition that holds the edge.
All inputs are finite; a program needn't handle non-finite values.
Results may differ from a plain program's by a relative error of at most 0.012.
The roundings to bfloat16 on the way count: a program that leaves them out, or rounds other values in their place, can miss the bound.
Values may be sent and summed in bfloat16 or wider, within the bound.
No kernel may reach another device: no remote copies, remote signals or barrier semaphores. Data moves between devices by JAX's collectives and lax.ppermute only.
A program may use at most 64 MiB of HBM per device.

v0:
```python
import jax
import jax.numpy as jnp
from jax import lax
from jax.sharding import Mesh
from jax.sharding import PartitionSpec as P

GRAPH = ("graph_0", "graph_1", "graph_2")


def split_up(x, dim, devices):
    before, after = (x.shape[:dim], x.shape[dim + 1 :])
    return jnp.moveaxis(x.reshape(*before, devices, -1, *after), dim, 0)


def summed_on_arrival(x, axis, dim):
    pieces = split_up(x, dim, lax.axis_size(axis))
    arrived = lax.all_to_all(pieces, axis, split_axis=0, concat_axis=0, tiled=True)
    return arrived.sum(axis=0)


def sum_by_axis(x, axes, dim):
    far, near = axes
    pieces = split_up(x, dim, lax.axis_size(far))
    nearer = summed_on_arrival(pieces, near, dim + 1)
    arrived = lax.all_to_all(nearer, far, split_axis=0, concat_axis=0, tiled=True)
    return arrived.sum(axis=0)


def copy_for_each(x, axis):
    copies = jnp.broadcast_to(x, (lax.axis_size(axis), *x.shape))
    return lax.all_to_all(copies, axis, split_axis=0, concat_axis=0, tiled=True)


def of_everyone(x, axis):
    return copy_for_each(x, axis).sum(axis=0)


def one_hot_rows(index_list, segments):
    return (
        lax.broadcasted_iota(jnp.int32, (segments, index_list.shape[0]), 0) == index_list[None, :]
    ).astype(jnp.bfloat16)


def silu_slope(values):
    sigmoid_v = jax.nn.sigmoid(values)
    return sigmoid_v * (1.0 + values * (1.0 - sigmoid_v))


def times_transposed(left, right):
    return lax.dot_general(
        left, right, (((1,), (1,)), ((), ())), preferred_element_type=jnp.float32
    )


def inner_rows(left, right):
    return lax.dot_general(
        left, right, (((0,), (0,)), ((), ())), preferred_element_type=jnp.float32
    )


def on_device(
    grid_in,
    mesh_init,
    g2m_geometry,
    w_embed,
    w_g2m,
    w_geo,
    a_send,
    a_recv,
    b_node,
    cotangent,
    g2m_send_rows,
    g2m_counts,
    g2m_senders,
    g2m_receivers,
    mesh_send_rows,
    mesh_senders,
    mesh_receivers,
):
    groups = lax.axis_size(GRAPH)
    slot_count = g2m_send_rows.shape[2]
    halo_count = mesh_send_rows.shape[2]
    width = w_g2m.shape[1]
    mesh_rows = mesh_init.shape[1]
    chosen = jnp.take(grid_in[0], g2m_send_rows[0].reshape(-1), axis=0).reshape(
        groups, slot_count, -1
    )
    live_slots = (
        lax.broadcasted_iota(jnp.int32, (groups, slot_count), 1) < g2m_counts[0][:, None]
    )[:, :, None]
    raw_rows = jnp.where(live_slots, chosen, jnp.zeros_like(chosen))
    pieces = lax.all_to_all(raw_rows, GRAPH, split_axis=0, concat_axis=0, tiled=True)
    flat_rows = pieces.reshape(-1, pieces.shape[-1])
    result = jax.nn.silu(jnp.dot(flat_rows, w_embed, preferred_element_type=jnp.float32)).astype(
        jnp.bfloat16
    )
    received = result.reshape(pieces.shape[0], pieces.shape[1], width)
    grid_proj = jnp.dot(
        received.reshape(groups * slot_count, width), w_g2m, preferred_element_type=jnp.float32
    )
    geo_part = inner_rows(g2m_geometry, w_geo)
    messages = jax.nn.silu(jnp.take(grid_proj, g2m_senders, axis=0) + geo_part).astype(jnp.bfloat16)
    gathered_sum = jnp.dot(
        one_hot_rows(g2m_receivers, mesh_rows), messages, preferred_element_type=jnp.float32
    )
    mesh_latent = (mesh_init[0].astype(jnp.float32) + gathered_sum).astype(jnp.bfloat16)
    own_send = mesh_send_rows[0].reshape(-1)
    halo_rows = jnp.take(mesh_latent, own_send, axis=0).reshape(groups, halo_count, width)
    halo_rows = lax.all_to_all(halo_rows, GRAPH, split_axis=0, concat_axis=0, tiled=True).reshape(
        groups * halo_count, width
    )
    sender_table = jnp.concatenate([halo_rows, mesh_latent], axis=0)
    table_size = sender_table.shape[0]
    send_proj = jnp.dot(sender_table, a_send, preferred_element_type=jnp.float32)
    recv_proj = jnp.dot(mesh_latent, a_recv, preferred_element_type=jnp.float32)
    pre_act = jnp.take(send_proj, mesh_senders, axis=0) + jnp.take(
        recv_proj, mesh_receivers, axis=0
    )
    edge_out = jax.nn.silu(pre_act).astype(jnp.bfloat16)
    recv_hot = one_hot_rows(mesh_receivers, mesh_rows)
    aggregate = jnp.dot(recv_hot, edge_out, preferred_element_type=jnp.float32).astype(jnp.bfloat16)
    update = jnp.dot(aggregate, b_node, preferred_element_type=jnp.float32)
    mesh_out = (mesh_latent.astype(jnp.float32) + jax.nn.silu(update)).astype(jnp.bfloat16)
    cot_value = cotangent[0].astype(jnp.float32)
    d_update = (cot_value * silu_slope(update)).astype(jnp.bfloat16)
    d_aggregate = times_transposed(d_update, b_node).astype(jnp.bfloat16)
    d_pre = (
        jnp.take(d_aggregate, mesh_receivers, axis=0).astype(jnp.float32) * silu_slope(pre_act)
    ).astype(jnp.bfloat16)
    recv_grad = jnp.dot(recv_hot, d_pre, preferred_element_type=jnp.float32).astype(jnp.bfloat16)
    send_grad = jnp.dot(
        one_hot_rows(mesh_senders, table_size), d_pre, preferred_element_type=jnp.float32
    ).astype(jnp.bfloat16)
    stacked = jnp.concatenate(
        [
            inner_rows(sender_table, send_grad),
            inner_rows(mesh_latent, recv_grad),
            inner_rows(aggregate, d_update),
        ],
        axis=0,
    )
    remote_grad = send_grad[: groups * halo_count].reshape(groups, halo_count, width)
    back_rows = lax.all_to_all(remote_grad, GRAPH, split_axis=0, concat_axis=0, tiled=True)
    returned = times_transposed(back_rows.reshape(groups * halo_count, width), a_send)
    grad_mesh = (
        cot_value
        + times_transposed(recv_grad, a_recv)
        + times_transposed(send_grad[groups * halo_count :], a_send)
    )
    grad_mesh = grad_mesh + jax.ops.segment_sum(returned, own_send, num_segments=mesh_rows)
    partial_rows = sum_by_axis(stacked, (("graph_0", "graph_1"), "graph_2"), 0)
    grad_weights = of_everyone(partial_rows, "sample")
    return (mesh_out[None], grad_mesh[None], grad_weights)


def solution(mesh):
    torus = Mesh(
        mesh.devices.reshape(8, 8, 2, mesh.shape["sample"]),
        ("graph_0", "graph_1", "graph_2", "sample"),
    )
    in_specs = (
        P("sample", GRAPH, None),
        P("sample", GRAPH, None),
        P(None, GRAPH),
        P(),
        P(),
        P(),
        P(),
        P(),
        P(),
        P("sample", GRAPH, None),
        P(GRAPH, None, None),
        P(GRAPH, None),
        P(GRAPH),
        P(GRAPH),
        P(GRAPH, None, None),
        P(GRAPH),
        P(GRAPH),
    )
    out_specs = (P("sample", GRAPH, None), P("sample", GRAPH, None), P(GRAPH, None))
    return jax.shard_map(
        on_device, mesh=torus, in_specs=in_specs, out_specs=out_specs, check_vma=False
    )
```

profile of v0, /device:TPU:24, one launch (start us, length us, event | category | flops | bytes accessed | tf_op | source)
XLA Modules:
  0.0 219.6 jit_solution(9041592598802157400)
XLA Ops:
  0.6 0.8 compare_and_fusion
  1.4 0.8 copy.43
  2.3 0.7 iota_compare_fusion.7
  3.2 4.4 %gather_fusion = bf16[1024,256]{1,0:T(8,128)(2,1)S(1)} fusion(bf16[512,256]{1,0:T(8,128)(2,1)} %bitcast.50, s32[1024]{0:T(1024)S(1)} %broadcast_clamp_fusion), kind=kCustom, calls=%fused_computation.2 | custom fusion | bytes 1052672 | tf_op jit(solution)/shard_map/jit(_take)/gather | solution.py:85
  7.7 1.1 fusion.11
  8.8 17.1 %all-to-all-start = ((bf16[128,8,256]{2,1,0:T(8,128)(2,1)}), bf16[128,8,256]{2,1,0:T(8,128)(2,1)S(1)}, u32[]{:S(2)}, u32[]{:S(2)}) async-start(bf16[128,8,256]{2,1,0:T(8,128)(2,1)} %fusion.11), calls=%async_computation | async-start | bytes 1048576 | tf_op jit(solution)/shard_map/all_to_all | solution.py:92
  26.3 18.2 %all-to-all-done = bf16[128,8,256]{2,1,0:T(8,128)(2,1)S(1)} async-done(((bf16[128,8,256]{2,1,0:T(8,128)(2,1)}), bf16[128,8,256]{2,1,0:T(8,128)(2,1)S(1)}, u32[]{:S(2)}, u32[]{:S(2)}) %all-to-all-start) | async-done | bytes 524320 | tf_op jit(solution)/shard_map/all_to_all | solution.py:92
  44.4 2.2 fusion
  46.7 4.9 %gather_fusion.1 = f32[1024,512]{1,0:T(8,128)} fusion(f32[1024,512]{1,0:T(8,128)S(1)} %fusion, s32[1024]{0:T(1024)S(1)} %fusion.20), kind=kCustom, calls=%fused_computation.3 | custom fusion | bytes 4198400 | tf_op jit(solution)/shard_map/jit(_take)/gather | solution.py:102
  51.6 2.6 %fusion.3 = bf16[128,512]{1,0:T(8,128)(2,1)S(1)} fusion(f32[1024,512]{1,0:T(8,128)} %gather_fusion.1, bf16[4,1024]{1,0:T(4,128)(2,1)S(1)} %copy-done.23, bf16[4,512]{1,0:T(4,128)(2,1)S(1)} %copy-done.24, pred[1024]{0:T(1024)(128)(4,1)S(1)} %compare_and_fusion.1, s32[1024]{0:T(1024)S(1)} %copy-done.25, bf16[1,128,512]{2,1,0:T(8,128)(2,1)S(1)} %copy-done.22), kind=kOutput, calls=%fused_computation.20 | convolution fusion | flops 142409728 | bytes 2376704 | tf_op jit(solution)/shard_map/dot_general | solution.py:103
  54.2 2.0 gather_fusion.4
  56.4 0.9 reshape.112
  57.3 7.5 %all-to-all-start.1 = ((bf16[128,4,512]{2,1,0:T(4,128)(2,1)}), bf16[128,4,512]{2,1,0:T(4,128)(2,1)S(1)}, u32[]{:S(2)}, u32[]{:S(2)}) async-start(bf16[128,4,512]{2,1,0:T(4,128)(2,1)} %reshape.112), calls=%async_computation.1 | async-start | bytes 1048576 | tf_op jit(solution)/shard_map/all_to_all | solution.py:109
  64.9 0.5 compare_and_fusion.3
  65.6 1.6 gather_fusion.3
  67.3 16.0 %all-to-all-done.1 = bf16[128,4,512]{2,1,0:T(4,128)(2,1)S(1)} async-done(((bf16[128,4,512]{2,1,0:T(4,128)(2,1)}), bf16[128,4,512]{2,1,0:T(4,128)(2,1)S(1)}, u32[]{:S(2)}, u32[]{:S(2)}) %all-to-all-start.1) | async-done | bytes 524320 | tf_op jit(solution)/shard_map/all_to_all | solution.py:109
  83.4 0.5 fusion.13
  83.9 2.3 %gather_fusion.2 = f32[512,512]{1,0:T(8,128)} fusion(f32[640,512]{1,0:T(8,128)S(1)} %fusion.13, s32[1024]{0:T(1024)S(1)} %pad_clamp_fusion.1), kind=kCustom, calls=%fused_computation.4 | custom fusion | bytes 2099200 | tf_op jit(solution)/shard_map/jit(_take)/gather | solution.py:116
  86.3 1.8 convolution_convert_fusion.3
  88.4 0.7 copy-done.8
  89.4 2.6 %gather_fusion.5 = bf16[512,512]{1,0:T(8,128)(2,1)} fusion(bf16[128,512]{1,0:T(8,128)(2,1)S(1)} %convolution_convert_fusion.2, s32[1024]{0:T(1024)S(1)} %pad_clamp_fusion), kind=kCustom, calls=%fused_computation.1.clone | custom fusion | bytes 1050624 | tf_op jit(solution)/shard_map/jit(_take)/gather | solution.py:128
  92.0 1.6 multiply_convert_fusion.2
  93.9 0.5 convolution_convert_fusion
  94.5 0.6 fusion.12
  95.7 1.4 fusion.27
  97.1 1.0 reshape.114
  98.0 0.3 fusion.33
  98.4 3.2 %pad_maximum_fusion = f32[1536,512]{1,0:T(8,128)} fusion(f32[512,512]{1,0:T(8,128)} %fusion.27, f32[512,512]{1,0:T(8,128)S(1)} %fusion.33, f32[512,512]{1,0:T(8,128)S(1)} %fusion.12), kind=kLoop, calls=%fused_computation.7 | loop fusion | flops 1572864 | bytes 6291456 | tf_op jit(solution)/shard_map/concatenate | solution.py:134
  101.6 4.5 %reshape_reshape.3 = f32[64,2,12,512]{3,2,1,0:T(8,128)} reshape(f32[1536,512]{1,0:T(8,128)} %pad_maximum_fusion) | data formatting | bytes 6291456 | tf_op jit(solution)/shard_map/reshape;reshape | solution.py:12
  106.1 4.0 %copy.45 = f32[2,64,12,512]{3,1,2,0:T(8,128)S(1)} copy(f32[2,64,12,512]{3,2,0,1:T(8,128)} %bitcast.51) | data formatting | bytes 6291456 | tf_op jit(solution)/shard_map/transpose | solution.py:12
  110.1 7.2 %all_to_all.30 = f32[2,64,12,512]{3,1,2,0:T(8,128)} all-to-all(f32[2,64,12,512]{3,1,2,0:T(8,128)S(1)} %copy.45), channel_id=1, replica_groups=mesh['graph_0'=8,'graph_1'=8,'graph_2'=2,'sample'=4] {'graph_2'}, dimensions={0} | all-to-all | bytes 6291456 | tf_op jit(solution)/shard_map/all_to_all | solution.py:17
  117.3 7.5 %all-to-all-start.2 = ((bf16[128,4,512]{2,1,0:T(4,128)(2,1)}), bf16[128,4,512]{2,1,0:T(4,128)(2,1)S(1)}, u32[]{:S(2)}, u32[]{:S(2)}) async-start(bf16[128,4,512]{2,1,0:T(4,128)(2,1)} %reshape.114), calls=%async_computation.2 | async-start | bytes 1048576 | tf_op jit(solution)/shard_map/all_to_all | solution.py:143
  124.8 2.4 %reduce_sum.27 = f32[64,12,512]{2,0,1:T(8,128)S(1)} reduce(f32[2,64,12,512]{3,1,2,0:T(8,128)} %all_to_all.30, f32[]{:T(128)} %constant.83.clone.1), dimensions={0}, to_apply=%region_1.3 | reduce | flops 393216 | bytes 4718596 | tf_op jit(solution)/shard_map/reduce_sum | solution.py:18
  127.2 2.3 %copy.46 = f32[64,12,512]{2,1,0:T(8,128)} copy(f32[64,12,512]{2,0,1:T(8,128)S(1)} %reduce_sum.27) | data formatting | bytes 3145728 | tf_op jit(solution)/shard_map/reduce_sum | solution.py:18
  129.5 13.8 %all-to-all-done.2 = bf16[128,4,512]{2,1,0:T(4,128)(2,1)S(1)} async-done(((bf16[128,4,512]{2,1,0:T(4,128)(2,1)}), bf16[128,4,512]{2,1,0:T(4,128)(2,1)S(1)}, u32[]{:S(2)}, u32[]{:S(2)}) %all-to-all-start.2) | async-done | bytes 524320 | tf_op jit(solution)/shard_map/all_to_all | solution.py:143
  143.3 0.8 copy-done.5
  144.1 6.7 %all-to-all-start.4 = ((f32[64,12,512]{2,1,0:T(8,128)}), f32[64,12,512]{2,1,0:T(8,128)S(1)}, u32[]{:S(2)}, u32[]{:S(2)}) async-start(f32[64,12,512]{2,1,0:T(8,128)} %copy.46), calls=%async_computation.4 | async-start | bytes 4194304 | tf_op jit(solution)/shard_map/all_to_all | solution.py:25
  150.8 1.7 fusion.19
  152.5 0.3 convolution_add_fusion.1
  152.9 1.2 convolution_add_fusion
  154.1 1.2 reshape.115
  155.2 52.6 %all-to-all-done.4 = f32[64,12,512]{2,1,0:T(8,128)S(1)} async-done(((f32[64,12,512]{2,1,0:T(8,128)}), f32[64,12,512]{2,1,0:T(8,128)S(1)}, u32[]{:S(2)}, u32[]{:S(2)}) %all-to-all-start.4) | async-done | bytes 1572896 | tf_op jit(solution)/shard_map/all_to_all | solution.py:25
  208.0 0.6 broadcast_in_dim.92
  208.6 4.3 %all-to-all-start.5 = ((f32[4,12,512]{2,1,0:T(8,128)}), f32[4,12,512]{2,1,0:T(8,128)S(1)}, u32[]{:S(2)}, u32[]{:S(2)}) async-start(f32[4,12,512]{2,1,0:T(8,128)} %broadcast_in_dim.92), calls=%async_computation.5 | async-start | bytes 262144 | tf_op jit(solution)/shard_map/all_to_all | solution.py:31
  213.0 0.5 fusion.32
  213.4 3.7 %scatter_fusion = f32[128,512]{1,0:T(8,128)S(1)} fusion(f32[128,512]{1,0:T(8,128)S(1)} %convolution_add_fusion, s32[512]{0:T(512)S(1)} %reshape_squeeze.10, f32[512,512]{1,0:T(8,128)S(1)} %fusion.32), kind=kCustom, calls=%fused_computation.6 | custom fusion | flops 262144 | bytes 3147776 | tf_op jit(solution)/shard_map/scatter-add | solution.py:150
  217.2 1.8 all-to-all-done.5
  218.9 0.6 reduce_sum.29
  (73 shorter events, 2.6 us)
Async XLA Ops:
  0.6 82.8 %copy-start = (bf16[512,512]{1,0:T(8,128)(2,1)S(1)}, bf16[512,512]{1,0:T(8,128)(2,1)}, u32[]{:S(2)}) copy-start(bf16[512,512]{1,0:T(8,128)(2,1)} %param.25) | copy-start | bytes 1572868
  7.6 18.3 %copy-start.20 = (s32[1,128,4]{1,2,0:T(4,128)S(1)}, s32[1,128,4]{1,2,0:T(4,128)}, u32[]{:S(2)}) copy-start(s32[1,128,4]{1,2,0:T(4,128)} %param.33) | copy-start | bytes 6148
  7.6 18.6 %copy-start.16 = (s32[1024]{0:T(1024)S(1)}, s32[1024]{0:T(1024)}, u32[]{:S(2)}) copy-start(s32[1024]{0:T(1024)} %param.31) | copy-start | bytes 12292
  7.7 36.8 %copy-start.21 = (bf16[256,512]{1,0:T(8,128)(2,1)S(1)}, bf16[256,512]{1,0:T(8,128)(2,1)}, u32[]{:S(2)}) copy-start(bf16[256,512]{1,0:T(8,128)(2,1)} %param.22) | copy-start | bytes 786436
  8.8 35.6 %all-to-all-start = ((bf16[128,8,256]{2,1,0:T(8,128)(2,1)}), bf16[128,8,256]{2,1,0:T(8,128)(2,1)S(1)}, u32[]{:S(2)}, u32[]{:S(2)}) async-start(bf16[128,8,256]{2,1,0:T(8,128)(2,1)} %fusion.11), calls=%async_computation | async-start | bytes 1048576 | tf_op jit(solution)/shard_map/all_to_all | solution.py:92
  46.6 4.9 %copy-start.22 = (bf16[1,128,512]{2,1,0:T(8,128)(2,1)S(1)}, bf16[1,128,512]{2,1,0:T(8,128)(2,1)}, u32[]{:S(2)}) copy-start(bf16[1,128,512]{2,1,0:T(8,128)(2,1)} %param.20) | copy-start | bytes 393220
  46.6 4.9 %copy-start.23 = (bf16[4,1024]{1,0:T(4,128)(2,1)S(1)}, bf16[4,1024]{1,0:T(4,128)(2,1)}, u32[]{:S(2)}) copy-start(bf16[4,1024]{1,0:T(4,128)(2,1)} %param.21) | copy-start | bytes 24580
  46.6 4.9 %copy-start.24 = (bf16[4,512]{1,0:T(4,128)(2,1)S(1)}, bf16[4,512]{1,0:T(4,128)(2,1)}, u32[]{:S(2)}) copy-start(bf16[4,512]{1,0:T(4,128)(2,1)} %param.24) | copy-start | bytes 12292
  46.7 4.9 %copy-start.25 = (s32[1024]{0:T(1024)S(1)}, s32[1024]{0:T(1024)}, u32[]{:S(2)}) copy-start(s32[1024]{0:T(1024)} %param.32) | copy-start | bytes 12292
  56.2 8.6 %copy-start.17 = (s32[512]{0:T(512)S(1)}, s32[512]{0:T(512)}, u32[]{:S(2)}) copy-start(s32[512]{0:T(512)} %param.34) | copy-start | bytes 6148
  56.2 8.7 %copy-start.15 = (s32[512]{0:T(512)S(1)}, s32[512]{0:T(512)}, u32[]{:S(2)}) copy-start(s32[512]{0:T(512)} %param.35) | copy-start | bytes 6148
  56.2 9.2 %copy-start.3 = (bf16[512,512]{1,0:T(8,128)(2,1)S(1)}, bf16[512,512]{1,0:T(8,128)(2,1)}, u32[]{:S(2)}) copy-start(bf16[512,512]{1,0:T(8,128)(2,1)} %param.26) | copy-start | bytes 1572868
  57.3 26.0 %all-to-all-start.1 = ((bf16[128,4,512]{2,1,0:T(4,128)(2,1)}), bf16[128,4,512]{2,1,0:T(4,128)(2,1)S(1)}, u32[]{:S(2)}, u32[]{:S(2)}) async-start(bf16[128,4,512]{2,1,0:T(4,128)(2,1)} %reshape.112), calls=%async_computation.1 | async-start | bytes 1048576 | tf_op jit(solution)/shard_map/all_to_all | solution.py:109
  86.3 1.9 copy-start.11
  86.3 2.8 %copy-start.12 = (bf16[1,128,512]{2,1,0:T(8,128)(2,1)S(1)}, bf16[1,128,512]{2,1,0:T(8,128)(2,1)}, u32[]{:S(2)}) copy-start(bf16[1,128,512]{2,1,0:T(8,128)(2,1)} %param.28) | copy-start | bytes 393220
  88.4 0.7 copy-start.8
  89.4 2.6 %copy-start.2 = (f32[512,512]{1,0:T(8,128)S(1)}, f32[512,512]{1,0:T(8,128)}, u32[]{:S(2)}) copy-start(f32[512,512]{1,0:T(8,128)} %gather_fusion.2) | copy-start | bytes 3145732
  89.4 2.6 %copy-start.19 = (pred[512]{0:T(512)(128)(4,1)S(1)}, pred[512]{0:T(512)(128)(4,1)}, u32[]{:S(2)}) copy-start(pred[512]{0:T(512)(128)(4,1)} %get-tuple-element.4) | copy-start | bytes 1540
  92.0 1.9 copy-start.18
  93.9 4.1 %copy-start.6 = (bf16[128,512]{1,0:T(8,128)(2,1)}, bf16[128,512]{1,0:T(8,128)(2,1)S(1)}, u32[]{:S(2)}) copy-start(bf16[128,512]{1,0:T(8,128)(2,1)S(1)} %convolution_convert_fusion.1) | copy-start | bytes 393220
  94.4 0.9 copy-start.10
  94.5 1.1 copy-start.9
  94.5 1.2 copy-start.13
  117.3 26.0 %all-to-all-start.2 = ((bf16[128,4,512]{2,1,0:T(4,128)(2,1)}), bf16[128,4,512]{2,1,0:T(4,128)(2,1)S(1)}, u32[]{:S(2)}, u32[]{:S(2)}) async-start(bf16[128,4,512]{2,1,0:T(4,128)(2,1)} %reshape.114), calls=%async_computation.2 | async-start | bytes 1048576 | tf_op jit(solution)/shard_map/all_to_all | solution.py:143
  129.5 23.0 %copy-start.4 = (bf16[512,512]{1,0:T(8,128)(2,1)S(1)}, bf16[512,512]{1,0:T(8,128)(2,1)}, u32[]{:S(2)}) copy-start(bf16[512,512]{1,0:T(8,128)(2,1)} %param.26) | copy-start | bytes 1572868
  129.5 23.0 %copy-start.7 = (bf16[128,512]{1,0:T(8,128)(2,1)S(1)}, bf16[128,512]{1,0:T(8,128)(2,1)}, u32[]{:S(2)}) copy-start(bf16[128,512]{1,0:T(8,128)(2,1)} %copy-done.6) | copy-start | bytes 393220
  129.5 23.0 %copy-start.14 = (bf16[1,128,512]{2,1,0:T(8,128)(2,1)S(1)}, bf16[1,128,512]{2,1,0:T(8,128)(2,1)}, u32[]{:S(2)}) copy-start(bf16[1,128,512]{2,1,0:T(8,128)(2,1)} %param.28) | copy-start | bytes 393220
  143.3 0.8 copy-start.5
  144.1 63.7 %all-to-all-start.4 = ((f32[64,12,512]{2,1,0:T(8,128)}), f32[64,12,512]{2,1,0:T(8,128)S(1)}, u32[]{:S(2)}, u32[]{:S(2)}) async-start(f32[64,12,512]{2,1,0:T(8,128)} %copy.46), calls=%async_computation.4 | async-start | bytes 4194304 | tf_op jit(solution)/shard_map/all_to_all | solution.py:25
  208.6 10.3 %all-to-all-start.5 = ((f32[4,12,512]{2,1,0:T(8,128)}), f32[4,12,512]{2,1,0:T(8,128)S(1)}, u32[]{:S(2)}, u32[]{:S(2)}) async-start(f32[4,12,512]{2,1,0:T(8,128)} %broadcast_in_dim.92), calls=%async_computation.5 | async-start | bytes 262144 | tf_op jit(solution)/shard_map/all_to_all | solution.py:31
  217.2 2.4 %copy-start.1 = (f32[128,512]{1,0:T(8,128)}, f32[128,512]{1,0:T(8,128)S(1)}, u32[]{:S(2)}) copy-start(f32[128,512]{1,0:T(8,128)S(1)} %scatter_fusion) | copy-start | bytes 786436
where the time goes:
time: 221 us; the launch traced here: 220 us
  waiting for transfers between devices  102 us (46%)
  starting transfers between devices  43.2 us (20%)
  local copies, waits for them, and re-layouts  35.9 us (16%)
  other arithmetic  16.8 us (8%)
  matrix products  12.9 us (6%)
  blocking collectives  7.24 us (3%)
    all_to_all x1, waiting for transfers between devices, sum_by_axis(): lax.all_to_all(nearer, far, split_axis=0, concat_axis=0, tiled=True)  52.6 us
    all_to_all x1, waiting for transfers between devices, on_device(): lax.all_to_all(raw_rows, GRAPH, split_axis=0, concat_axis=0, tiled=True)  18.2 us
    all_to_all x1, starting transfers between devices, on_device(): lax.all_to_all(raw_rows, GRAPH, split_axis=0, concat_axis=0, tiled=True)  17.1 us
    all_to_all x1, waiting for transfers between devices, on_device(): lax.all_to_all(halo_rows, GRAPH, split_axis=0, concat_axis=0, tiled=True)  16 us
    all_to_all x1, waiting for transfers between devices, on_device(): lax.all_to_all(remote_grad, GRAPH, split_axis=0, concat_axis=0, tiled=True)  13.8 us
    all_to_all x1, starting transfers between devices, on_device(): lax.all_to_all(halo_rows, GRAPH, split_axis=0, concat_axis=0, tiled=True)  7.52 us
    all_to_all x1, starting transfers between devices, on_device(): lax.all_to_all(remote_grad, GRAPH, split_axis=0, concat_axis=0, tiled=True)  7.51 us
    all_to_all x1, blocking collectives, summed_on_arrival(): lax.all_to_all(pieces, axis, split_axis=0, concat_axis=0, tiled=True)  7.24 us
  transfers between devices with their start and end apart: 5, of which 5 were waited for; matrix products, arithmetic and copies ran while one was open for 7% of the time, Pallas kernels for 0%

commit v1 on v0

v1 whole, which is shorter than its diff:
```python
import functools

import jax
import jax.numpy as jnp
from jax import lax
from jax.experimental import pallas as pl
from jax.experimental.pallas import tpu as pltpu
from jax.sharding import Mesh
from jax.sharding import PartitionSpec as P

GRAPH = ("graph_0", "graph_1", "graph_2")
LANES = 128
F32 = jnp.float32
BF16 = jnp.bfloat16


def dot(left, right):
    return jnp.dot(left, right, preferred_element_type=F32)


def times_transposed(left, right):
    return lax.dot_general(left, right, (((1,), (1,)), ((), ())), preferred_element_type=F32)


def inner_rows(left, right):
    return lax.dot_general(left, right, (((0,), (0,)), ((), ())), preferred_element_type=F32)


def logistic(v):
    return 0.5 * jnp.tanh(0.5 * v) + 0.5


def silu(v):
    return v * logistic(v)


def slope_from(v, s):
    return s * (1.0 + v * (1.0 - s))


def columns_of(row):
    return jnp.transpose(jnp.broadcast_to(row, (LANES, row.shape[1])))


def select_rows(column, size):
    lane = lax.broadcasted_iota(jnp.int32, column.shape, 1)
    blocks = [
        jnp.where(column == lane + LANES * k, 1.0, 0.0).astype(BF16) for k in range(size // LANES)
    ]
    return blocks[0] if len(blocks) == 1 else jnp.concatenate(blocks, axis=1)


def select_columns(row, size):
    segment = lax.broadcasted_iota(jnp.int32, (size, row.shape[1]), 0)
    return jnp.where(segment == row, 1.0, 0.0).astype(BF16)


def strided_store(spread, start, stride, value):
    rows, width = value.shape
    for k in range(width // LANES):
        spread[k, pl.ds(start, rows, stride=stride), :] = value[:, k * LANES : (k + 1) * LANES]


def gather_blocks(spread, out_ref):
    for k in range(spread.shape[0]):
        out_ref[:, k * LANES : (k + 1) * LANES] = spread[k].astype(out_ref.dtype)


def scatter_blocks(spread, in_ref):
    for k in range(spread.shape[0]):
        spread[k] = in_ref[:, k * LANES : (k + 1) * LANES].astype(spread.dtype)


def pick_grid(rows_ref, counts_ref, grid_ref, out_ref, spread):
    groups, slots = rows_ref.shape[1:]
    counts = columns_of(counts_ref[...])
    wanted = rows_ref[0]
    for j in range(slots):
        row_ids = jnp.where(counts > j, wanted[:, j : j + 1], -1)
        chosen = dot(select_rows(row_ids, grid_ref.shape[1]), grid_ref[0])
        strided_store(spread, j, slots, chosen)
    gather_blocks(spread, out_ref)


def encode(
    pieces_ref, senders_ref, receivers_ref, geometry_ref, w_embed_ref, w_g2m_ref, w_geo_ref,
    init_ref, send_rows_ref, latent_ref, halo_ref, spread,
):
    edges = senders_ref.shape[1]
    nodes, width = latent_ref.shape
    step = 256
    total = init_ref[0].astype(F32)
    for start in range(0, edges, step):
        span = slice(start, start + step)
        chosen = select_rows(columns_of(senders_ref[:, span]), pieces_ref.shape[0])
        raw = dot(chosen, pieces_ref[...]).astype(BF16)
        embedded = silu(dot(raw, w_embed_ref[...])).astype(BF16)
        geo_part = inner_rows(geometry_ref[:, span], w_geo_ref[...])
        message = silu(dot(embedded, w_g2m_ref[...]) + geo_part).astype(BF16)
        total = total + dot(select_columns(receivers_ref[:, span], nodes), message)
    latent = total.astype(BF16)
    latent_ref[...] = latent
    groups, slots = send_rows_ref.shape[1:]
    wanted = send_rows_ref[0]
    for j in range(slots):
        row_ids = jnp.broadcast_to(wanted[:, j : j + 1], (groups, LANES))
        split_store(spread, j, slots, dot(select_rows(row_ids, nodes), latent))
    gather_blocks(spread, halo_ref)


def split_store(spread, j, slots, value):
    groups, width = value.shape
    strided_store(spread, j, 2 * slots, value[:, : width // 2])
    strided_store(spread, slots + j, 2 * slots, value[:, width // 2 :])


def split_load(spread, j, slots, groups):
    blocks = [
        spread[k, pl.ds(start, groups, stride=2 * slots), :]
        for start in (j, slots + j)
        for k in range(spread.shape[0])
    ]
    return jnp.concatenate(blocks, axis=1)


def process(
    slots, halo_ref, latent_ref, senders_ref, receivers_ref, a_send_ref, a_recv_ref, b_node_ref, cot_ref,
    out_ref, back_ref, table_ref, send_grad_ref, recv_grad_ref, aggregate_ref, d_update_ref, spread,
):
    nodes, width = latent_ref.shape
    rows = table_ref.shape[0]
    remote = rows - nodes
    groups = remote // slots
    scatter_blocks(spread, halo_ref)
    for j in range(slots):
        table_ref[j * groups : (j + 1) * groups, :] = split_load(spread, j, slots, groups).astype(BF16)
    latent = latent_ref[...]
    table_ref[remote:, :] = latent
    ids = senders_ref[...]
    ids = jnp.where(ids < remote, lax.rem(ids, slots) * groups + lax.div(ids, slots), ids)
    receivers = receivers_ref[...]
    receive = select_rows(columns_of(receivers), nodes)
    gather = select_columns(receivers, nodes)
    sent = dot(select_rows(columns_of(ids), rows), table_ref[...]).astype(BF16)
    own = dot(receive, latent).astype(BF16)
    pre_act = dot(sent, a_send_ref[...]) + dot(own, a_recv_ref[...])
    gate = logistic(pre_act)
    aggregate = dot(gather, (pre_act * gate).astype(BF16)).astype(BF16)
    aggregate_ref[...] = aggregate
    update = dot(aggregate, b_node_ref[...])
    update_gate = logistic(update)
    out_ref[0] = (latent.astype(F32) + update * update_gate).astype(BF16)
    d_update = (cot_ref[0].astype(F32) * slope_from(update, update_gate)).astype(BF16)
    d_update_ref[...] = d_update
    d_aggregate = times_transposed(d_update, b_node_ref[...]).astype(BF16)
    d_pre = (dot(receive, d_aggregate) * slope_from(pre_act, gate)).astype(BF16)
    recv_grad_ref[...] = dot(gather, d_pre).astype(BF16)
    send_grad = dot(select_columns(ids, rows), d_pre)
    send_grad_ref[...] = send_grad.astype(BF16)
    for j in range(slots):
        split_store(spread, j, slots, send_grad[j * groups : (j + 1) * groups])
    gather_blocks(spread, back_ref)


def weight_grads(
    half_ref, table_ref, send_grad_ref, latent_ref, recv_grad_ref, aggregate_ref, d_update_ref, out_ref
):
    half = out_ref.shape[1]
    width = latent_ref.shape[1]
    columns = pl.ds(pl.multiple_of(half_ref[0] * half, half), half)
    pairs = ((table_ref, send_grad_ref), (latent_ref, recv_grad_ref), (aggregate_ref, d_update_ref))
    for i, (left, right) in enumerate(pairs):
        product = inner_rows(left[...], right[:, columns])
        out_ref[i * width : (i + 1) * width, :] = product.astype(out_ref.dtype)


def pack(keep_ref, other_ref, back_ref, out_ref):
    half = keep_ref.shape[2]
    mid = half // 2
    tile = back_ref.shape[2]
    out_ref[:, :, :, :half] = back_ref[...]
    for i in range(3):
        rows = slice(i * tile, (i + 1) * tile)
        total = (keep_ref[:, rows, :] + other_ref[:, rows, :].astype(F32)).astype(BF16)
        if i == 1:
            out_ref[:, 0, :, 2 * half :] = total[:, :, :mid]
            out_ref[:, 1, :, 2 * half :] = total[:, :, mid:]
        else:
            out_ref[:, i // 2, :, half : 2 * half] = total


def add_chips(arrived_ref, out_ref):
    chips = arrived_ref.shape[0]
    skip = arrived_ref.shape[3] - out_ref.shape[3]
    total = arrived_ref[0, :, :, skip:].astype(F32)
    for i in range(1, chips):
        total = total + arrived_ref[i, :, :, skip:].astype(F32)
    for i in range(out_ref.shape[0]):
        out_ref[i] = total


def add_samples(core_ref, arrived_ref, out_ref):
    samples, _, _, tile, lanes = arrived_ref.shape
    half = out_ref.shape[1] // 2
    mid = half // 2
    total = arrived_ref[0]
    for i in range(1, samples):
        total = total + arrived_ref[i]
    extra = tile // 2

    def middle(rows):
        parts = [total[core, h, rows, half:] for h in range(2) for core in range(2)]
        return jnp.concatenate(parts, axis=1)

    def whole(core):
        return jnp.concatenate([total[core, h, :, :half] for h in range(2)], axis=1)

    @pl.when(core_ref[0] == 0)
    def _():
        out_ref[:tile, :] = whole(0)
        out_ref[tile:, :] = middle(slice(0, extra))

    @pl.when(core_ref[0] == 1)
    def _():
        out_ref[:extra, :] = middle(slice(extra, tile))
        out_ref[extra:, :] = whole(1)


def return_grads(
    back_ref, send_rows_ref, send_grad_ref, recv_grad_ref, a_send_ref, a_recv_ref, cot_ref,
    out_ref, spread,
):
    nodes = recv_grad_ref.shape[0]
    groups, slots = send_rows_ref.shape[1:]
    scatter_blocks(spread, back_ref)
    total = send_grad_ref[...].astype(F32)
    wanted = send_rows_ref[0]
    for j in range(slots):
        row_ids = jnp.broadcast_to(wanted[:, j : j + 1], (groups, LANES))
        arrived = split_load(spread, j, slots, groups).astype(BF16)
        total = total + inner_rows(select_rows(row_ids, nodes), arrived)
    high = total.astype(BF16)
    rest = total - high.astype(F32)
    low = rest.astype(BF16)
    a_send = a_send_ref[...]
    out_ref[0] = (
        cot_ref[0].astype(F32)
        + times_transposed(recv_grad_ref[...], a_recv_ref[...])
        + (times_transposed(high, a_send) + times_transposed(low, a_send))
    )


def shape(dims, dtype):
    return jax.ShapeDtypeStruct(dims, dtype)


def kernel(body, outs, scratch, flops, smem_first=False):
    def call(*operands):
        specs = [pl.BlockSpec(memory_space=pltpu.VMEM) for _ in operands]
        if smem_first:
            specs[0] = pl.BlockSpec(memory_space=pltpu.SMEM)
        moved = sum(x.size * x.dtype.itemsize for x in operands)
        return pl.pallas_call(
            body,
            out_shape=outs,
            in_specs=specs,
            out_specs=jax.tree.map(lambda _: pl.BlockSpec(memory_space=pltpu.VMEM), outs),
            scratch_shapes=scratch,
            compiler_params=pltpu.CompilerParams(vmem_limit_bytes=24 << 20),
            cost_estimate=pl.CostEstimate(flops=flops, bytes_accessed=moved, transcendentals=0),
        )(*operands)

    return call


def exchange(x, axis):
    return lax.all_to_all(x, axis, split_axis=0, concat_axis=0, tiled=True)


def share(keep, send, back, core):
    half = keep.shape[1]
    tile = 8
    chips = lax.axis_size("graph_0") * lax.axis_size("graph_1")
    samples = lax.axis_size("sample")
    lanes = 2 * half + half // 2
    other = lax.ppermute(send, "graph_2", [(0, 1), (1, 0)])
    packed = kernel(pack, shape((chips, 2, tile, lanes), BF16), [], 10**7)(
        keep.reshape(chips, -1, half),
        other.reshape(chips, -1, half),
        back.reshape(chips, 2, tile, half),
    )
    arrived = exchange(packed.reshape(2 * chips, tile, lanes), GRAPH)
    copies = kernel(add_chips, shape((2 * samples, 2, tile, lanes - half), F32), [], 10**7)(
        arrived.reshape(chips, 2, tile, lanes)
    )
    copies = exchange(copies, ("sample", "graph_2"))
    rows = keep.shape[0] // (2 * chips)
    grad_weights = kernel(add_samples, shape((rows, 2 * half), F32), [], 10**6, True)(
        core, copies.reshape(samples, 2, 2, tile, lanes - half)
    )
    return arrived.reshape(2 * chips * tile, lanes), grad_weights


def on_device(
    grid_in,
    mesh_init,
    g2m_geometry,
    w_embed,
    w_g2m,
    w_geo,
    a_send,
    a_recv,
    b_node,
    cotangent,
    g2m_send_rows,
    g2m_counts,
    g2m_senders,
    g2m_receivers,
    mesh_send_rows,
    mesh_senders,
    mesh_receivers,
):
    groups, slots = g2m_send_rows.shape[1:]
    halo_slots = mesh_send_rows.shape[2]
    features = grid_in.shape[2]
    width = w_g2m.shape[1]
    half = width // 2
    nodes = mesh_init.shape[1]
    table_rows = groups * halo_slots + nodes
    halves = 2 * groups * halo_slots

    raw_rows = kernel(
        pick_grid,
        shape((groups * slots, features), BF16),
        [pltpu.VMEM((features // LANES, groups * slots, LANES), F32)],
        10**8,
    )(g2m_send_rows, g2m_counts, grid_in)
    pieces = exchange(raw_rows.reshape(groups, slots, features), GRAPH)

    latent, halo = kernel(
        encode,
        (shape((nodes, width), BF16), shape((halves, half), BF16)),
        [pltpu.VMEM((half // LANES, halves, LANES), F32)],
        2 * 10**9,
    )(
        pieces.reshape(groups * slots, features),
        g2m_senders[None],
        g2m_receivers[None],
        g2m_geometry,
        w_embed,
        w_g2m,
        w_geo,
        mesh_init,
        mesh_send_rows,
    )
    halo = exchange(halo.reshape(groups, 2 * halo_slots, half), GRAPH)

    mesh_out, back, table, send_grad, recv_grad, aggregate, d_update = kernel(
        functools.partial(process, halo_slots),
        (
            shape((1, nodes, width), BF16),
            shape((halves, half), BF16),
            shape((table_rows, width), BF16),
            shape((table_rows, width), BF16),
            shape((nodes, width), BF16),
            shape((nodes, width), BF16),
            shape((nodes, width), BF16),
        ),
        [pltpu.VMEM((half // LANES, halves, LANES), F32)],
        3 * 10**9,
    )(
        halo.reshape(halves, half),
        latent,
        mesh_senders[None],
        mesh_receivers[None],
        a_send,
        a_recv,
        b_node,
        cotangent,
    )
    core = lax.axis_index("graph_2").astype(jnp.int32)[None]
    operands = (table, send_grad, latent, recv_grad, aggregate, d_update)
    send = kernel(weight_grads, shape((3 * width, half), BF16), [], 5 * 10**8, True)(1 - core, *operands)
    keep = kernel(weight_grads, shape((3 * width, half), F32), [], 5 * 10**8, True)(core, *operands)
    arrived, grad_weights = share(keep, send, back, core)

    grad_mesh = kernel(
        return_grads,
        shape((1, nodes, width), F32),
        [pltpu.VMEM((half // LANES, halves, LANES), F32)],
        10**9,
    )(
        arrived,
        mesh_send_rows,
        send_grad[groups * halo_slots :],
        recv_grad,
        a_send,
        a_recv,
        cotangent,
    )
    return (mesh_out, grad_mesh, grad_weights)


def solution(mesh):
    torus = Mesh(
        mesh.devices.reshape(8, 8, 2, mesh.shape["sample"]),
        ("graph_0", "graph_1", "graph_2", "sample"),
    )
    in_specs = (
        P("sample", GRAPH, None),
        P("sample", GRAPH, None),
        P(None, GRAPH),
        P(),
        P(),
        P(),
        P(),
        P(),
        P(),
        P("sample", GRAPH, None),
        P(GRAPH, None, None),
        P(GRAPH, None),
        P(GRAPH),
        P(GRAPH),
        P(GRAPH, None, None),
        P(GRAPH),
        P(GRAPH),
    )
    out_specs = (P("sample", GRAPH, None), P("sample", GRAPH, None), P(GRAPH, None))
    return jax.shard_map(
        on_device, mesh=torus, in_specs=in_specs, out_specs=out_specs, check_vma=False
    )
```

time: 221 us -> 138 us (0.62)
  the two profiles are of different devices: /device:TPU:24 before, /device:TPU:1 now
where the time goes in v1:
time: 138 us; the launch traced here: 137 us
  waiting for transfers between devices  46.9 us (34%)
  blocking collectives  41.4 us (30%)
  starting transfers between devices  30.4 us (22%)
  Pallas kernels  13.6 us (10%)
  local copies, waits for them, and re-layouts  3.64 us (3%)
    all_to_all x3, waiting for transfers between devices, exchange(): return lax.all_to_all(x, axis, split_axis=0, concat_axis=0, tiled=True)  45.2 us
    all_to_all x1, blocking collectives, exchange(): return lax.all_to_all(x, axis, split_axis=0, concat_axis=0, tiled=True)  41.4 us
    all_to_all x3, starting transfers between devices, exchange(): return lax.all_to_all(x, axis, split_axis=0, concat_axis=0, tiled=True)  28.5 us
    pallas_call x9, Pallas kernels, call(): pl.pallas_call(body, out_shape=outs, in_specs=specs, out_specs=jax.tree.m...  13.6 us
    unnamed x36, local copies, waits for them, and re-layouts  3.63 us
  transfers between devices with their start and end apart: 4, of which 4 were waited for; matrix products, arithmetic and copies ran while one was open for 0% of the time, Pallas kernels for 2%

profile of v1, /device:TPU:1, one launch (start us, length us, event | category | flops | bytes accessed | tf_op | source)
XLA Modules:
  0.0 136.9 jit_solution(996782392559772940)
XLA Ops:
  0.6 0.0 copy-start.16
  0.6 0.0 copy-start.12
  0.7 0.0 copy-start.11
  0.7 0.0 copy-start.13
  0.7 0.0 copy-start.10
  0.7 0.8 copy.20.rows_ref
  1.5 0.9 copy-done
  2.5 0.7 copy-done.1
  3.1 1.5 %shard_map.184 = bf16[1024,256]{1,0:T(8,128)(2,1)} custom-call(s32[1,128,8]{2,1,0:T(8,128)S(1)} %copy.20.rows_ref, s32[1,128]{1,0:T(1,128)S(1)} %copy-done.1, bf16[1,512,256]{2,1,0:T(8,128)(2,1)S(1)} %copy-done), custom_call_target="tpu_custom_call" | custom-call | flops 100000000 | bytes 266752 | tf_op jit(solution)/shard_map/pallas_call | solution.py:263
  4.6 18.4 %all-to-all-start = ((bf16[128,8,256]{2,1,0:T(8,128)(2,1)}), bf16[128,8,256]{2,1,0:T(8,128)(2,1)S(1)}, u32[]{:S(2)}, u32[]{:S(2)}) async-start(bf16[128,8,256]{2,1,0:T(8,128)(2,1)} %bitcast), calls=%async_computation | async-start | bytes 1048576 | tf_op jit(solution)/shard_map/all_to_all | solution.py:277
  23.0 0.0 copy-done.16
  23.0 0.1 copy.21.send_rows_ref
  23.1 20.5 %all-to-all-done = bf16[128,8,256]{2,1,0:T(8,128)(2,1)S(1)} async-done(((bf16[128,8,256]{2,1,0:T(8,128)(2,1)}), bf16[128,8,256]{2,1,0:T(8,128)(2,1)S(1)}, u32[]{:S(2)}, u32[]{:S(2)}) %all-to-all-start) | async-done | bytes 524320 | tf_op jit(solution)/shard_map/all_to_all | solution.py:277
  43.6 0.0 copy-done.12
  43.6 0.0 copy-done.11
  43.6 0.0 copy-done.13
  43.6 0.0 copy-done.10
  43.6 0.0 copy-done.2
  43.6 0.0 copy-done.7
  43.6 0.0 copy-done.8
  43.6 0.0 copy-start.3
  43.6 0.0 copy-start.4
  43.7 0.0 copy-start.9
  43.7 0.0 copy-start.14
  43.7 0.0 copy-start.15
  43.7 4.8 %shard_map.185 = (bf16[128,512]{1,0:T(8,128)(2,1)S(1)}, bf16[1024,256]{1,0:T(8,128)(2,1)}) custom-call(bf16[1024,256]{1,0:T(8,128)(2,1)S(1)} %bitcast.23, s32[1,1024]{1,0:T(1,128)S(1)} %bitcast.25, s32[1,1024]{1,0:T(1,128)S(1)} %bitcast.26, bf16[4,1024]{1,0:T(4,128)(2,1)S(1)} %copy-done.10, bf16[256,512]{1,0:T(8,128)(2,1)S(1)} %copy-done.7, ...), custom_call_target="tpu_custom_call" | custom-call | flops 2000000000 | bytes 1464320 | tf_op jit(solution)/shard_map/pallas_call | solution.py:263
  48.4 5.4 %all-to-all-start.1 = ((bf16[128,8,256]{2,1,0:T(8,128)(2,1)}), bf16[128,8,256]{2,1,0:T(8,128)(2,1)S(1)}, u32[]{:S(2)}, u32[]{:S(2)}) async-start(bf16[128,8,256]{2,1,0:T(8,128)(2,1)} %bitcast.4), calls=%async_computation.1 | async-start | bytes 1048576 | tf_op jit(solution)/shard_map/all_to_all | solution.py:277
  53.9 20.6 %all-to-all-done.1 = bf16[128,8,256]{2,1,0:T(8,128)(2,1)S(1)} async-done(((bf16[128,8,256]{2,1,0:T(8,128)(2,1)}), bf16[128,8,256]{2,1,0:T(8,128)(2,1)S(1)}, u32[]{:S(2)}, u32[]{:S(2)}) %all-to-all-start.1) | async-done | bytes 524320 | tf_op jit(solution)/shard_map/all_to_all | solution.py:277
  74.4 0.0 copy-done.3
  74.4 0.0 copy-done.4
  74.4 0.0 copy-done.9
  74.4 0.0 copy-done.14
  74.5 0.0 copy-done.15
  74.5 0.0 copy-start.5
  74.5 1.0 copy-done.5
  75.5 3.0 %shard_map.186 = (bf16[1,128,512]{2,1,0:T(8,128)(2,1)}, bf16[1024,256]{1,0:T(8,128)(2,1)S(1)}, bf16[640,512]{1,0:T(8,128)(2,1)S(1)}, bf16[640,512]{1,0:T(8,128)(...) custom-call(bf16[1024,256]{1,0:T(8,128)(2,1)S(1)} %bitcast.22, ...), custom_call_target="tpu_custom_call" | custom-call | flops 3000000000 | bytes 2363392 | tf_op jit(solution)/shard_map/pallas_call | solution.py:263
  78.5 0.6 shard_map.188
  79.1 1.9 %collective-permute-start = (bf16[1536,256]{1,0:T(8,128)(2,1)S(1)}, bf16[1536,256]{1,0:T(8,128)(2,1)S(1)}, u32[]{:S(2)}, u32[]{:S(2)}) collective-permute-start(bf16[1536,256]{1,0:T(8,128)(2,1)S(1)} %shard_map.188), channel_id=1, source_target_pairs={{0,4},{4,0},{1,5},{5,1},{2,6},{6,2},{3,7},{7,3},{8,12},{12,8},{9,1... | collective-permute-start | bytes 2359304 | tf_op jit(solution)/shard_map/ppermute | solution.py:286
  81.0 0.6 shard_map.187
  81.6 1.7 %collective-permute-done = bf16[1536,256]{1,0:T(8,128)(2,1)S(1)} collective-permute-done((bf16[1536,256]{1,0:T(8,128)(2,1)S(1)}, bf16[1536,256]{1,0:T(8,128)(2,1)S(1)}, u32[]{:S(2)}, u32[]{:S(2)}) %collective-permute-start) | collective-permute-done | bytes 786464 | tf_op jit(solution)/shard_map/ppermute | solution.py:286
  83.3 0.2 shard_map.189
  83.4 41.4 %all_to_all.20 = bf16[128,8,640]{2,1,0:T(8,128)(2,1)S(1)} all-to-all(bf16[128,8,640]{2,1,0:T(8,128)(2,1)S(1)} %bitcast.19), channel_id=1, replica_groups=mesh['graph_0'=8,'graph_1'=8,'graph_2'=2,'sample'=4] {'graph_0','graph_1..., dimensions={0} | all-to-all | bytes 2621440 | tf_op jit(solution)/shard_map/all_to_all | solution.py:277
  124.9 0.8 shard_map.191
  125.7 4.7 %all-to-all-start.3 = ((f32[8,2,8,384]{3,2,1,0:T(8,128)}), f32[8,2,8,384]{3,2,1,0:T(8,128)S(1)}, u32[]{:S(2)}, u32[]{:S(2)}) async-start(f32[8,2,8,384]{3,2,1,0:T(8,128)} %shard_map.191), calls=%async_computation.3 | async-start | bytes 393216 | tf_op jit(solution)/shard_map/all_to_all | solution.py:277
  130.4 0.0 copy-done.6
  130.4 1.7 %shard_map.190 = f32[1,128,512]{2,1,0:T(8,128)} custom-call(bf16[1024,640]{1,0:T(8,128)(2,1)S(1)} %bitcast.18, s32[1,128,4]{2,1,0:T(8,128)S(1)} %copy.21.send_rows_ref, bf16[128,512]{1,0:T(8,128)(2,1)S(1)} %slice.3.send_grad_ref, bf16[128,512]{1,0:T(8,128)(2,1)S(1)} %get-tuple-element.17.recv_grad_ref, bf16[512,512]{1,0:T(8,128)(2,1)S(1)} %copy-done.4, ...), custom_call_target="tpu_custom_call" | custom-call | flops 1000000000 | bytes 2754560 | tf_op jit(solution)/shard_map/pallas_call | solution.py:263
  132.1 4.2 %all-to-all-done.3 = f32[8,2,8,384]{3,2,1,0:T(8,128)S(1)} async-done(((f32[8,2,8,384]{3,2,1,0:T(8,128)}), f32[8,2,8,384]{3,2,1,0:T(8,128)S(1)}, u32[]{:S(2)}, u32[]{:S(2)}) %all-to-all-start.3) | async-done | bytes 196640 | tf_op jit(solution)/shard_map/all_to_all | solution.py:277
  136.3 0.6 shard_map.192
  (7 shorter events, 0.0 us)
Async XLA Ops:
  0.6 22.4 %copy-start.16 = (s32[1,128,4]{1,2,0:T(4,128)S(1)}, s32[1,128,4]{1,2,0:T(4,128)}, u32[]{:S(2)}) copy-start(s32[1,128,4]{1,2,0:T(4,128)} %param.31) | copy-start | bytes 6148
  0.6 42.9 %copy-start.12 = (s32[1024]{0:T(1024)S(1)}, s32[1024]{0:T(1024)}, u32[]{:S(2)}) copy-start(s32[1024]{0:T(1024)} %param.30) | copy-start | bytes 12292
  0.7 42.9 %copy-start.11 = (s32[1024]{0:T(1024)S(1)}, s32[1024]{0:T(1024)}, u32[]{:S(2)}) copy-start(s32[1024]{0:T(1024)} %param.29) | copy-start | bytes 12292
  0.7 42.9 %copy-start.13 = (bf16[4,512]{1,0:T(4,128)(2,1)S(1)}, bf16[4,512]{1,0:T(4,128)(2,1)}, u32[]{:S(2)}) copy-start(bf16[4,512]{1,0:T(4,128)(2,1)} %w_geo_ref.1) | copy-start | bytes 12292
  0.7 42.9 %copy-start.10 = (bf16[4,1024]{1,0:T(4,128)(2,1)S(1)}, bf16[4,1024]{1,0:T(4,128)(2,1)}, u32[]{:S(2)}) copy-start(bf16[4,1024]{1,0:T(4,128)(2,1)} %geometry_ref.1) | copy-start | bytes 24580
  1.5 0.9 copy-start
  2.4 0.7 copy-start.1
  3.1 40.5 %copy-start.2 = (bf16[512,512]{1,0:T(8,128)(2,1)S(1)}, bf16[512,512]{1,0:T(8,128)(2,1)}, u32[]{:S(2)}) copy-start(bf16[512,512]{1,0:T(8,128)(2,1)} %w_g2m_ref.1) | copy-start | bytes 1572868
  3.1 40.5 %copy-start.7 = (bf16[256,512]{1,0:T(8,128)(2,1)S(1)}, bf16[256,512]{1,0:T(8,128)(2,1)}, u32[]{:S(2)}) copy-start(bf16[256,512]{1,0:T(8,128)(2,1)} %w_embed_ref.1) | copy-start | bytes 786436
  3.1 40.5 %copy-start.8 = (bf16[1,128,512]{2,1,0:T(8,128)(2,1)S(1)}, bf16[1,128,512]{2,1,0:T(8,128)(2,1)}, u32[]{:S(2)}) copy-start(bf16[1,128,512]{2,1,0:T(8,128)(2,1)} %init_ref.1) | copy-start | bytes 393220
  4.6 39.0 %all-to-all-start = ((bf16[128,8,256]{2,1,0:T(8,128)(2,1)}), bf16[128,8,256]{2,1,0:T(8,128)(2,1)S(1)}, u32[]{:S(2)}, u32[]{:S(2)}) async-start(bf16[128,8,256]{2,1,0:T(8,128)(2,1)} %bitcast), calls=%async_computation | async-start | bytes 1048576 | tf_op jit(solution)/shard_map/all_to_all | solution.py:277
  43.6 30.8 %copy-start.3 = (bf16[512,512]{1,0:T(8,128)(2,1)S(1)}, bf16[512,512]{1,0:T(8,128)(2,1)}, u32[]{:S(2)}) copy-start(bf16[512,512]{1,0:T(8,128)(2,1)} %b_node_ref.1) | copy-start | bytes 1572868
  43.6 30.8 %copy-start.4 = (bf16[512,512]{1,0:T(8,128)(2,1)S(1)}, bf16[512,512]{1,0:T(8,128)(2,1)}, u32[]{:S(2)}) copy-start(bf16[512,512]{1,0:T(8,128)(2,1)} %a_send_ref.3) | copy-start | bytes 1572868
  43.7 30.8 %copy-start.9 = (bf16[1,128,512]{2,1,0:T(8,128)(2,1)S(1)}, bf16[1,128,512]{2,1,0:T(8,128)(2,1)}, u32[]{:S(2)}) copy-start(bf16[1,128,512]{2,1,0:T(8,128)(2,1)} %cot_ref.3) | copy-start | bytes 393220
  43.7 30.8 %copy-start.14 = (s32[512]{0:T(512)S(1)}, s32[512]{0:T(512)}, u32[]{:S(2)}) copy-start(s32[512]{0:T(512)} %param.32) | copy-start | bytes 6148
  43.7 30.8 %copy-start.15 = (s32[512]{0:T(512)S(1)}, s32[512]{0:T(512)}, u32[]{:S(2)}) copy-start(s32[512]{0:T(512)} %param.33) | copy-start | bytes 6148
  48.4 26.0 %all-to-all-start.1 = ((bf16[128,8,256]{2,1,0:T(8,128)(2,1)}), bf16[128,8,256]{2,1,0:T(8,128)(2,1)S(1)}, u32[]{:S(2)}, u32[]{:S(2)}) async-start(bf16[128,8,256]{2,1,0:T(8,128)(2,1)} %bitcast.4), calls=%async_computation.1 | async-start | bytes 1048576 | tf_op jit(solution)/shard_map/all_to_all | solution.py:277
  74.5 1.0 copy-start.5
  79.1 4.2 %collective-permute-start = (bf16[1536,256]{1,0:T(8,128)(2,1)S(1)}, bf16[1536,256]{1,0:T(8,128)(2,1)S(1)}, u32[]{:S(2)}, u32[]{:S(2)}) collective-permute-start(bf16[1536,256]{1,0:T(8,128)(2,1)S(1)} %shard_map.188), channel_id=1, source_target_pairs={{0,4},{4,0},{1,5},{5,1},{2,6},{6,2},{3,7},{7,3},{8,12},{12,8},{9,1... | collective-permute-start | bytes 2359304 | tf_op jit(solution)/shard_map/ppermute | solution.py:286
  124.9 5.5 %copy-start.6 = (bf16[512,512]{1,0:T(8,128)(2,1)S(1)}, bf16[512,512]{1,0:T(8,128)(2,1)}, u32[]{:S(2)}) copy-start(bf16[512,512]{1,0:T(8,128)(2,1)} %a_recv_ref.3) | copy-start | bytes 1572868
  125.7 10.6 %all-to-all-start.3 = ((f32[8,2,8,384]{3,2,1,0:T(8,128)}), f32[8,2,8,384]{3,2,1,0:T(8,128)S(1)}, u32[]{:S(2)}, u32[]{:S(2)}) async-start(f32[8,2,8,384]{3,2,1,0:T(8,128)} %shard_map.191), calls=%async_computation.3 | async-start | bytes 393216 | tf_op jit(solution)/shard_map/all_to_all | solution.py:277

commit v2 on v1

--- a/solution.py
+++ b/solution.py
@@ -12,6 +12,7 @@
 LANES = 128
 F32 = jnp.float32
 BF16 = jnp.bfloat16
+GRANTS = (60, 40, 40)
 
 
 def dot(left, right):
@@ -40,6 +41,12 @@
 
 def columns_of(row):
     return jnp.transpose(jnp.broadcast_to(row, (LANES, row.shape[1])))
+
+
+def slot_columns(ids):
+    slots, groups = ids.shape
+    turned = jnp.transpose(jnp.concatenate([ids] * (LANES // slots), axis=0))
+    return [jnp.broadcast_to(turned[:, j : j + 1], (groups, LANES)) for j in range(slots)]
 
 
 def select_rows(column, size):
@@ -71,14 +78,24 @@
         spread[k] = in_ref[:, k * LANES : (k + 1) * LANES].astype(spread.dtype)
 
 
-def pick_grid(rows_ref, counts_ref, grid_ref, out_ref, spread):
-    groups, slots = rows_ref.shape[1:]
-    counts = columns_of(counts_ref[...])
-    wanted = rows_ref[0]
+def pick_grid(rows_hbm, counts_hbm, grid_hbm, out_ref, rows, counts, grid, sems, spread):
+    copies = [
+        pltpu.make_async_copy(source, target, sems.at[i])
+        for i, (source, target) in enumerate(
+            ((rows_hbm, rows), (counts_hbm, counts), (grid_hbm, grid))
+        )
+    ]
+    for copy in copies:
+        copy.start()
+    copies[0].wait()
+    copies[1].wait()
+    slots = rows.shape[1]
+    slot = lax.broadcasted_iota(jnp.int32, rows.shape[1:], 0)
+    ids = slot_columns(jnp.where(slot < counts[...], rows[0], -1))
+    chosen = [select_rows(ids[j], grid.shape[1]) for j in range(slots)]
+    copies[2].wait()
     for j in range(slots):
-        row_ids = jnp.where(counts > j, wanted[:, j : j + 1], -1)
-        chosen = dot(select_rows(row_ids, grid_ref.shape[1]), grid_ref[0])
-        strided_store(spread, j, slots, chosen)
+        strided_store(spread, j, slots, dot(chosen[j], grid[0]))
     gather_blocks(spread, out_ref)
 
 
@@ -100,11 +117,9 @@
         total = total + dot(select_columns(receivers_ref[:, span], nodes), message)
     latent = total.astype(BF16)
     latent_ref[...] = latent
-    groups, slots = send_rows_ref.shape[1:]
-    wanted = send_rows_ref[0]
-    for j in range(slots):
-        row_ids = jnp.broadcast_to(wanted[:, j : j + 1], (groups, LANES))
-        split_store(spread, j, slots, dot(select_rows(row_ids, nodes), latent))
+    ids = slot_columns(send_rows_ref[0])
+    for j in range(len(ids)):
+        split_store(spread, j, len(ids), dot(select_rows(ids[j], nodes), latent))
     gather_blocks(spread, halo_ref)
 
 
@@ -124,7 +139,8 @@
 
 
 def process(
-    slots, halo_ref, latent_ref, senders_ref, receivers_ref, a_send_ref, a_recv_ref, b_node_ref, cot_ref,
+    slots, halo_ref, latent_ref, senders_ref, receivers_ref, a_send_ref, a_recv_ref, b_node_ref,
+    cot_ref,
     out_ref, back_ref, table_ref, send_grad_ref, recv_grad_ref, aggregate_ref, d_update_ref, spread,
 ):
     nodes, width = latent_ref.shape
@@ -175,55 +191,51 @@
 
 
 def pack(keep_ref, other_ref, back_ref, out_ref):
-    half = keep_ref.shape[2]
-    mid = half // 2
+    chips, _, half = keep_ref.shape
     tile = back_ref.shape[2]
     out_ref[:, :, :, :half] = back_ref[...]
     for i in range(3):
         rows = slice(i * tile, (i + 1) * tile)
-        total = (keep_ref[:, rows, :] + other_ref[:, rows, :].astype(F32)).astype(BF16)
-        if i == 1:
-            out_ref[:, 0, :, 2 * half :] = total[:, :, :mid]
-            out_ref[:, 1, :, 2 * half :] = total[:, :, mid:]
-        else:
-            out_ref[:, i // 2, :, half : 2 * half] = total
+        total = keep_ref[:, rows, :] + other_ref[:, rows, :].astype(F32)
+        if i != 1:
+            out_ref[:, i // 2, :, half : 2 * half] = total.astype(BF16)
+            continue
+        flat = total.reshape(chips * tile, half)
+        left, right = flat[:, :LANES], flat[:, LANES:]
+        upper = lax.rem(lax.broadcasted_iota(jnp.int32, left.shape, 0), tile) < tile // 2
+        first = jnp.where(upper, left, pltpu.roll(right, tile // 2, 0))
+        second = jnp.where(upper, pltpu.roll(left, chips * tile - tile // 2, 0), right)
+        out_ref[:, 0, :, 2 * half :] = first.astype(BF16).reshape(chips, tile, LANES)
+        out_ref[:, 1, :, 2 * half :] = second.astype(BF16).reshape(chips, tile, LANES)
 
 
 def add_chips(arrived_ref, out_ref):
     chips = arrived_ref.shape[0]
-    skip = arrived_ref.shape[3] - out_ref.shape[3]
+    skip = arrived_ref.shape[3] - out_ref.shape[2]
     total = arrived_ref[0, :, :, skip:].astype(F32)
     for i in range(1, chips):
         total = total + arrived_ref[i, :, :, skip:].astype(F32)
-    for i in range(out_ref.shape[0]):
-        out_ref[i] = total
-
-
-def add_samples(core_ref, arrived_ref, out_ref):
-    samples, _, _, tile, lanes = arrived_ref.shape
+    out_ref[...] = total
+
+
+def add_samples(core_ref, own_ref, next_ref, across_ref, last_ref, out_ref):
+    total = (own_ref[...] + across_ref[...]) + (next_ref[...] + last_ref[...])
+    tile = total.shape[1]
     half = out_ref.shape[1] // 2
-    mid = half // 2
-    total = arrived_ref[0]
-    for i in range(1, samples):
-        total = total + arrived_ref[i]
     extra = tile // 2
-
-    def middle(rows):
-        parts = [total[core, h, rows, half:] for h in range(2) for core in range(2)]
-        return jnp.concatenate(parts, axis=1)
-
-    def whole(core):
-        return jnp.concatenate([total[core, h, :, :half] for h in range(2)], axis=1)
+    whole = jnp.concatenate([total[h, :, :half] for h in range(2)], axis=1)
+    parts = [total[h, k * extra : (k + 1) * extra, half:] for h in range(2) for k in range(2)]
+    middle = jnp.concatenate(parts, axis=1)
 
     @pl.when(core_ref[0] == 0)
     def _():
-        out_ref[:tile, :] = whole(0)
-        out_ref[tile:, :] = middle(slice(0, extra))
+        out_ref[:tile, :] = whole
+        out_ref[tile:, :] = middle
 
     @pl.when(core_ref[0] == 1)
     def _():
-        out_ref[:extra, :] = middle(slice(extra, tile))
-        out_ref[extra:, :] = whole(1)
+        out_ref[:extra, :] = middle
+        out_ref[extra:, :] = whole
 
 
 def return_grads(
@@ -231,14 +243,13 @@
     out_ref, spread,
 ):
     nodes = recv_grad_ref.shape[0]
-    groups, slots = send_rows_ref.shape[1:]
+    slots, groups = send_rows_ref.shape[1:]
     scatter_blocks(spread, back_ref)
     total = send_grad_ref[...].astype(F32)
     wanted = send_rows_ref[0]
     for j in range(slots):
-        row_ids = jnp.broadcast_to(wanted[:, j : j + 1], (groups, LANES))
         arrived = split_load(spread, j, slots, groups).astype(BF16)
-        total = total + inner_rows(select_rows(row_ids, nodes), arrived)
+        total = total + dot(select_columns(wanted[j : j + 1], nodes), arrived)
     high = total.astype(BF16)
     rest = total - high.astype(F32)
     low = rest.astype(BF16)
@@ -254,11 +265,12 @@
     return jax.ShapeDtypeStruct(dims, dtype)
 
 
-def kernel(body, outs, scratch, flops, smem_first=False):
+def kernel(body, outs, scratch, flops, first=0, space=None, grant=24):
     def call(*operands):
-        specs = [pl.BlockSpec(memory_space=pltpu.VMEM) for _ in operands]
-        if smem_first:
-            specs[0] = pl.BlockSpec(memory_space=pltpu.SMEM)
+        specs = [
+            pl.BlockSpec(memory_space=space if i < first else pltpu.VMEM)
+            for i in range(len(operands))
+        ]
         moved = sum(x.size * x.dtype.itemsize for x in operands)
         return pl.pallas_call(
             body,
@@ -266,7 +278,7 @@
             in_specs=specs,
             out_specs=jax.tree.map(lambda _: pl.BlockSpec(memory_space=pltpu.VMEM), outs),
             scratch_shapes=scratch,
-            compiler_params=pltpu.CompilerParams(vmem_limit_bytes=24 << 20),
+            compiler_params=pltpu.CompilerParams(vmem_limit_bytes=grant << 20),
             cost_estimate=pl.CostEstimate(flops=flops, bytes_accessed=moved, transcendentals=0),
         )(*operands)
 
@@ -290,13 +302,16 @@
         back.reshape(chips, 2, tile, half),
     )
     arrived = exchange(packed.reshape(2 * chips, tile, lanes), GRAPH)
-    copies = kernel(add_chips, shape((2 * samples, 2, tile, lanes - half), F32), [], 10**7)(
+    own = kernel(add_chips, shape((2, tile, lanes - half), F32), [], 10**7)(
         arrived.reshape(chips, 2, tile, lanes)
     )
-    copies = exchange(copies, ("sample", "graph_2"))
+    others = [
+        lax.ppermute(own, "sample", [((i + step) % samples, i) for i in range(samples)])
+        for step in range(1, samples)
+    ]
     rows = keep.shape[0] // (2 * chips)
-    grad_weights = kernel(add_samples, shape((rows, 2 * half), F32), [], 10**6, True)(
-        core, copies.reshape(samples, 2, 2, tile, lanes - half)
+    grad_weights = kernel(add_samples, shape((rows, 2 * half), F32), [], 10**6, 1, pltpu.SMEM)(
+        core, own, *others
     )
     return arrived.reshape(2 * chips * tile, lanes), grad_weights
 
@@ -329,12 +344,23 @@
     table_rows = groups * halo_slots + nodes
     halves = 2 * groups * halo_slots
 
+    grid_rows = jnp.transpose(g2m_send_rows, (0, 2, 1))
+    mesh_rows = jnp.transpose(mesh_send_rows, (0, 2, 1))
     raw_rows = kernel(
         pick_grid,
         shape((groups * slots, features), BF16),
-        [pltpu.VMEM((features // LANES, groups * slots, LANES), F32)],
+        [
+            pltpu.VMEM(grid_rows.shape, jnp.int32),
+            pltpu.VMEM(g2m_counts.shape, jnp.int32),
+            pltpu.VMEM(grid_in.shape, BF16),
+            pltpu.SemaphoreType.DMA((3,)),
+            pltpu.VMEM((features // LANES, groups * slots, LANES), F32),
+        ],
         10**8,
-    )(g2m_send_rows, g2m_counts, grid_in)
+        3,
+        pltpu.HBM,
+        GRANTS[0],
+    )(grid_rows, g2m_counts, grid_in)
     pieces = exchange(raw_rows.reshape(groups, slots, features), GRAPH)
 
     latent, halo = kernel(
@@ -342,6 +368,7 @@
         (shape((nodes, width), BF16), shape((halves, half), BF16)),
         [pltpu.VMEM((half // LANES, halves, LANES), F32)],
         2 * 10**9,
+        grant=GRANTS[1],
     )(
         pieces.reshape(groups * slots, features),
         g2m_senders[None],
@@ -351,7 +378,7 @@
         w_g2m,
         w_geo,
         mesh_init,
-        mesh_send_rows,
+        mesh_rows,
     )
     halo = exchange(halo.reshape(groups, 2 * halo_slots, half), GRAPH)
 
@@ -368,6 +395,7 @@
         ),
         [pltpu.VMEM((half // LANES, halves, LANES), F32)],
         3 * 10**9,
+        grant=GRANTS[2],
     )(
         halo.reshape(halves, half),
         latent,
@@ -378,10 +406,11 @@
         b_node,
         cotangent,
     )
+
     core = lax.axis_index("graph_2").astype(jnp.int32)[None]
     operands = (table, send_grad, latent, recv_grad, aggregate, d_update)
-    send = kernel(weight_grads, shape((3 * width, half), BF16), [], 5 * 10**8, True)(1 - core, *operands)
-    keep = kernel(weight_grads, shape((3 * width, half), F32), [], 5 * 10**8, True)(core, *operands)
+    send = kernel(weight_grads, shape((3 * width, half), BF16), [], 5 * 10**8, 1, pltpu.SMEM)(1 - core, *operands)
+    keep = kernel(weight_grads, shape((3 * width, half), F32), [], 5 * 10**8, 1, pltpu.SMEM)(core, *operands)
     arrived, grad_weights = share(keep, send, back, core)
 
     grad_mesh = kernel(
@@ -391,7 +420,7 @@
         10**9,
     )(
         arrived,
-        mesh_send_rows,
+        mesh_rows,
         send_grad[groups * halo_slots :],
         recv_grad,
         a_send,

time: 138 us -> 139 us (level)
  waiting for transfers between devices: 46.9 us -> 58.3 us
  starting transfers between devices: 30.4 us -> 23.5 us
  local copies, waits for them, and re-layouts: 3.64 us -> 0.08 us
  blocking collectives: 41.4 us -> 39 us
  Pallas kernels: 13.6 us -> 15.1 us
    all_to_all x3 -> x2, starting transfers between devices: 28.5 us -> 11 us  [exchange(): return lax.all_to_all(x, axis, split_axis=0, concat_axis=0, tiled=True)]
    all_to_all x3 -> x2, waiting for transfers between devices: 45.2 us -> 56.6 us  [exchange(): return lax.all_to_all(x, axis, split_axis=0, concat_axis=0, tiled=True)]
    ppermute x0 -> x3, starting transfers between devices: none -> 10.5 us  [share(): lax.ppermute(own, 'sample', [((i + step) % samples, i) for i in range(sam...]
    unnamed x36 -> x28, local copies, waits for them, and re-layouts: 3.63 us -> 0.07 us
    all_to_all x1, blocking collectives: 41.4 us -> 39 us  [exchange(): return lax.all_to_all(x, axis, split_axis=0, concat_axis=0, tiled=True)]
    pallas_call x9, Pallas kernels: 13.6 us -> 15.1 us  [call(): pl.pallas_call(body, out_shape=outs, in_specs=specs, out_specs=jax.tree.m...]
  transfers between devices with their start and end apart: 4 -> 6, of which waited for: 4 -> 3; matrix products, arithmetic and copies ran while one was open for 0% -> 0% of each run, Pallas kernels for 2% -> 2%
where the time goes in v2:
time: 139 us; the launch traced here: 137 us
  waiting for transfers between devices  58.3 us (42%)
  blocking collectives  39 us (28%)
  starting transfers between devices  23.5 us (17%)
  Pallas kernels  15.1 us (11%)
    all_to_all x2, waiting for transfers between devices, exchange(): return lax.all_to_all(x, axis, split_axis=0, concat_axis=0, tiled=True)  56.6 us
    all_to_all x1, blocking collectives, exchange(): return lax.all_to_all(x, axis, split_axis=0, concat_axis=0, tiled=True)  39 us
    pallas_call x9, Pallas kernels, call(): pl.pallas_call(body, out_shape=outs, in_specs=specs, out_specs=jax.tree.m...  15.1 us
    all_to_all x2, starting transfers between devices, exchange(): return lax.all_to_all(x, axis, split_axis=0, concat_axis=0, tiled=True)  11 us
    ppermute x3, starting transfers between devices, share(): lax.ppermute(own, 'sample', [((i + step) % samples, i) for i in range(sam...  10.5 us
  transfers between devices with their start and end apart: 6, of which 3 were waited for; matrix products, arithmetic and copies ran while one was open for 0% of the time, Pallas kernels for 2%

profile of v2, /device:TPU:1, one launch (start us, length us, event | category | flops | bytes accessed | tf_op | source)
XLA Modules:
  0.0 136.9 jit_solution(1367239468355435801)
XLA Ops:
  0.6 0.0 copy-start.13
  0.6 0.0 copy-start.9
  0.7 0.0 copy-start.8
  0.7 0.0 copy-start.10
  0.7 0.0 copy-start
  0.7 0.0 copy-start.4
  0.7 0.0 copy-start.7
  0.7 0.0 copy-start.5
  0.7 2.5 %shard_map.184 = bf16[1024,256]{1,0:T(8,128)(2,1)} custom-call(s32[1,8,128]{2,1,0:T(8,128)} %bitcast.31, s32[1,128]{1,0:T(1,128)} %counts_hbm.1, bf16[1,512,256]{2,1,0:T(8,128)(2,1)} %grid_hbm.1), custom_call_target="tpu_custom_call" | custom-call | flops 100000000 | bytes 266752 | tf_op jit(solution)/shard_map/pallas_call | solution.py:275
  3.2 39.0 %all_to_all.15 = bf16[128,8,256]{2,1,0:T(8,128)(2,1)S(1)} all-to-all(bf16[128,8,256]{2,1,0:T(8,128)(2,1)} %bitcast.30), channel_id=1, replica_groups=mesh['graph_0'=8,'graph_1'=8,'graph_2'=2,'sample'=4] {'graph_0','graph_1..., dimensions={0} | all-to-all | bytes 1048576 | tf_op jit(solution)/shard_map/all_to_all | solution.py:289
  42.2 0.0 copy-done.13
  42.2 0.0 copy-done.9
  42.2 0.0 copy-done.8
  42.2 0.0 copy-done.10
  42.2 0.0 copy-done
  42.3 0.0 copy-done.4
  42.3 0.0 copy-done.7
  42.3 0.0 copy-done.5
  42.3 0.0 copy-start.1
  42.3 0.0 copy-start.2
  42.3 0.0 copy-start.3
  42.3 0.0 copy-start.6
  42.3 0.0 copy-start.11
  42.3 0.0 copy-start.12
  42.4 4.7 %shard_map.185 = (bf16[128,512]{1,0:T(8,128)(2,1)S(1)}, bf16[1024,256]{1,0:T(8,128)(2,1)}) custom-call(bf16[1024,256]{1,0:T(8,128)(2,1)S(1)} %bitcast.22, s32[1,1024]{1,0:T(1,128)S(1)} %bitcast.24, s32[1,1024]{1,0:T(1,128)S(1)} %bitcast.25, bf16[4,1024]{1,0:T(4,128)(2,1)S(1)} %copy-done.7, bf16[256,512]{1,0:T(8,128)(2,1)S(1)} %copy-done.4, ...), custom_call_target="tpu_custom_call" | custom-call | flops 2000000000 | bytes 1464320 | tf_op jit(solution)/shard_map/pallas_call | solution.py:275
  47.1 5.4 %all-to-all-start.1 = ((bf16[128,8,256]{2,1,0:T(8,128)(2,1)}), bf16[128,8,256]{2,1,0:T(8,128)(2,1)S(1)}, u32[]{:S(2)}, u32[]{:S(2)}) async-start(bf16[128,8,256]{2,1,0:T(8,128)(2,1)} %bitcast.6), calls=%async_computation.1 | async-start | bytes 1048576 | tf_op jit(solution)/shard_map/all_to_all | solution.py:289
  52.5 20.6 %all-to-all-done.1 = bf16[128,8,256]{2,1,0:T(8,128)(2,1)S(1)} async-done(((bf16[128,8,256]{2,1,0:T(8,128)(2,1)}), bf16[128,8,256]{2,1,0:T(8,128)(2,1)S(1)}, u32[]{:S(2)}, u32[]{:S(2)}) %all-to-all-start.1) | async-done | bytes 524320 | tf_op jit(solution)/shard_map/all_to_all | solution.py:289
  73.1 0.0 copy-done.1
  73.1 0.0 copy-done.2
  73.1 0.0 copy-done.3
  73.1 0.0 copy-done.6
  73.1 3.0 %shard_map.186 = (bf16[1,128,512]{2,1,0:T(8,128)(2,1)}, bf16[1024,256]{1,0:T(8,128)(2,1)S(1)}, bf16[640,512]{1,0:T(8,128)(2,1)S(1)}, bf16[640,512]{1,0:T(8,128)(...) custom-call(bf16[1024,256]{1,0:T(8,128)(2,1)S(1)} %bitcast.21, ...), custom_call_target="tpu_custom_call" | custom-call | flops 3000000000 | bytes 2363392 | tf_op jit(solution)/shard_map/pallas_call | solution.py:275
  76.2 0.6 shard_map.188
  76.7 1.9 %collective-permute-start = (bf16[1536,256]{1,0:T(8,128)(2,1)S(1)}, bf16[1536,256]{1,0:T(8,128)(2,1)S(1)}, u32[]{:S(2)}, u32[]{:S(2)}) collective-permute-start(bf16[1536,256]{1,0:T(8,128)(2,1)S(1)} %shard_map.188), channel_id=1, source_target_pairs={{0,4},{4,0},{1,5},{5,1},{2,6},{6,2},{3,7},{7,3},{8,12},{12,8},{9,1... | collective-permute-start | bytes 2359304 | tf_op jit(solution)/shard_map/ppermute | solution.py:298
  78.7 0.6 shard_map.187
  79.2 1.7 %collective-permute-done = bf16[1536,256]{1,0:T(8,128)(2,1)S(1)} collective-permute-done((bf16[1536,256]{1,0:T(8,128)(2,1)S(1)}, bf16[1536,256]{1,0:T(8,128)(2,1)S(1)}, u32[]{:S(2)}, u32[]{:S(2)}) %collective-permute-start) | collective-permute-done | bytes 786464 | tf_op jit(solution)/shard_map/ppermute | solution.py:298
  80.9 1.3 shard_map.189
  82.2 5.6 %all-to-all-start.2 = ((bf16[128,8,640]{2,1,0:T(8,128)(2,1)}), bf16[128,8,640]{2,1,0:T(8,128)(2,1)S(1)}, u32[]{:S(2)}, u32[]{:S(2)}) async-start(bf16[128,8,640]{2,1,0:T(8,128)(2,1)} %bitcast.14), calls=%async_computation.2 | async-start | bytes 2621440 | tf_op jit(solution)/shard_map/all_to_all | solution.py:289
  87.9 36.1 %all-to-all-done.2 = bf16[128,8,640]{2,1,0:T(8,128)(2,1)S(1)} async-done(((bf16[128,8,640]{2,1,0:T(8,128)(2,1)}), bf16[128,8,640]{2,1,0:T(8,128)(2,1)S(1)}, u32[]{:S(2)}, u32[]{:S(2)}) %all-to-all-start.2) | async-done | bytes 1310752 | tf_op jit(solution)/shard_map/all_to_all | solution.py:289
  123.9 0.1 shard_map.191.own_ref
  124.1 3.1 %collective-permute-start.3 = (f32[2,8,384]{2,1,0:T(8,128)S(1)}, f32[2,8,384]{2,1,0:T(8,128)S(1)}, u32[]{:S(2)}, u32[]{:S(2)}) collective-permute-start(f32[2,8,384]{2,1,0:T(8,128)S(1)} %shard_map.191.own_ref), channel_id=1, source_target_pairs={{3,0},{0,1},{1,2},{2,3},{7,4},{4,5},{5,6},{6,7},{11,8},{8,9},{9,10... | collective-permute-start | bytes 73736 | tf_op jit(solution)/shard_map/ppermute | solution.py:309
  127.2 4.4 %collective-permute-start.2 = (f32[2,8,384]{2,1,0:T(8,128)S(1)}, f32[2,8,384]{2,1,0:T(8,128)S(1)}, u32[]{:S(2)}, u32[]{:S(2)}) collective-permute-start(f32[2,8,384]{2,1,0:T(8,128)S(1)} %shard_map.191.own_ref), channel_id=1, source_target_pairs={{2,0},{3,1},{0,2},{1,3},{6,4},{7,5},{4,6},{5,7},{10,8},{11,9},{8,1... | collective-permute-start | bytes 73736 | tf_op jit(solution)/shard_map/ppermute | solution.py:309
  131.6 3.1 %collective-permute-start.1 = (f32[2,8,384]{2,1,0:T(8,128)S(1)}, f32[2,8,384]{2,1,0:T(8,128)S(1)}, u32[]{:S(2)}, u32[]{:S(2)}) collective-permute-start(f32[2,8,384]{2,1,0:T(8,128)S(1)} %shard_map.191.own_ref), channel_id=1, source_target_pairs={{1,0},{2,1},{3,2},{0,3},{5,4},{6,5},{7,6},{4,7},{9,8},{10,9},{11,1... | collective-permute-start | bytes 73736 | tf_op jit(solution)/shard_map/ppermute | solution.py:309
  134.6 1.6 %shard_map.190 = f32[1,128,512]{2,1,0:T(8,128)} custom-call(bf16[1024,640]{1,0:T(8,128)(2,1)S(1)} %bitcast.19, s32[1,4,128]{2,1,0:T(4,128)S(1)} %bitcast.29, bf16[128,512]{1,0:T(8,128)(2,1)S(1)} %slice.3.send_grad_ref, bf16[128,512]{1,0:T(8,128)(2,1)S(1)} %get-tuple-element.17.recv_grad_ref, bf16[512,512]{1,0:T(8,128)(2,1)S(1)} %copy-done.2, ...), custom_call_target="tpu_custom_call" | custom-call | flops 1000000000 | bytes 2754560 | tf_op jit(solution)/shard_map/pallas_call | solution.py:275
  136.2 0.0 collective-permute-done.3.last_ref
  136.2 0.0 collective-permute-done.2.across_ref
  136.2 0.0 collective-permute-done.1.next_ref
  136.2 0.6 shard_map.192
  (3 shorter events, 0.0 us)
Async XLA Ops:
  0.6 41.6 %copy-start.13 = (s32[1,128,4]{1,2,0:T(4,128)S(1)}, s32[1,128,4]{1,2,0:T(4,128)}, u32[]{:S(2)}) copy-start(s32[1,128,4]{1,2,0:T(4,128)} %param.31) | copy-start | bytes 6148
  0.6 41.6 %copy-start.9 = (s32[1024]{0:T(1024)S(1)}, s32[1024]{0:T(1024)}, u32[]{:S(2)}) copy-start(s32[1024]{0:T(1024)} %param.30) | copy-start | bytes 12292
  0.7 41.6 %copy-start.8 = (s32[1024]{0:T(1024)S(1)}, s32[1024]{0:T(1024)}, u32[]{:S(2)}) copy-start(s32[1024]{0:T(1024)} %param.29) | copy-start | bytes 12292
  0.7 41.6 %copy-start.10 = (bf16[4,512]{1,0:T(4,128)(2,1)S(1)}, bf16[4,512]{1,0:T(4,128)(2,1)}, u32[]{:S(2)}) copy-start(bf16[4,512]{1,0:T(4,128)(2,1)} %w_geo_ref.1) | copy-start | bytes 12292
  0.7 41.6 %copy-start = (bf16[512,512]{1,0:T(8,128)(2,1)S(1)}, bf16[512,512]{1,0:T(8,128)(2,1)}, u32[]{:S(2)}) copy-start(bf16[512,512]{1,0:T(8,128)(2,1)} %w_g2m_ref.1) | copy-start | bytes 1572868
  0.7 41.6 %copy-start.4 = (bf16[256,512]{1,0:T(8,128)(2,1)S(1)}, bf16[256,512]{1,0:T(8,128)(2,1)}, u32[]{:S(2)}) copy-start(bf16[256,512]{1,0:T(8,128)(2,1)} %w_embed_ref.1) | copy-start | bytes 786436
  0.7 41.6 %copy-start.7 = (bf16[4,1024]{1,0:T(4,128)(2,1)S(1)}, bf16[4,1024]{1,0:T(4,128)(2,1)}, u32[]{:S(2)}) copy-start(bf16[4,1024]{1,0:T(4,128)(2,1)} %geometry_ref.1) | copy-start | bytes 24580
  0.7 41.6 %copy-start.5 = (bf16[1,128,512]{2,1,0:T(8,128)(2,1)S(1)}, bf16[1,128,512]{2,1,0:T(8,128)(2,1)}, u32[]{:S(2)}) copy-start(bf16[1,128,512]{2,1,0:T(8,128)(2,1)} %init_ref.1) | copy-start | bytes 393220
  42.3 30.8 %copy-start.1 = (bf16[512,512]{1,0:T(8,128)(2,1)S(1)}, bf16[512,512]{1,0:T(8,128)(2,1)}, u32[]{:S(2)}) copy-start(bf16[512,512]{1,0:T(8,128)(2,1)} %b_node_ref.1) | copy-start | bytes 1572868
  42.3 30.8 %copy-start.2 = (bf16[512,512]{1,0:T(8,128)(2,1)S(1)}, bf16[512,512]{1,0:T(8,128)(2,1)}, u32[]{:S(2)}) copy-start(bf16[512,512]{1,0:T(8,128)(2,1)} %a_send_ref.3) | copy-start | bytes 1572868
  42.3 30.8 %copy-start.3 = (bf16[512,512]{1,0:T(8,128)(2,1)S(1)}, bf16[512,512]{1,0:T(8,128)(2,1)}, u32[]{:S(2)}) copy-start(bf16[512,512]{1,0:T(8,128)(2,1)} %a_recv_ref.3) | copy-start | bytes 1572868
  42.3 30.8 %copy-start.6 = (bf16[1,128,512]{2,1,0:T(8,128)(2,1)S(1)}, bf16[1,128,512]{2,1,0:T(8,128)(2,1)}, u32[]{:S(2)}) copy-start(bf16[1,128,512]{2,1,0:T(8,128)(2,1)} %cot_ref.3) | copy-start | bytes 393220
  42.3 30.8 %copy-start.11 = (s32[512]{0:T(512)S(1)}, s32[512]{0:T(512)}, u32[]{:S(2)}) copy-start(s32[512]{0:T(512)} %param.32) | copy-start | bytes 6148
  42.3 30.8 %copy-start.12 = (s32[512]{0:T(512)S(1)}, s32[512]{0:T(512)}, u32[]{:S(2)}) copy-start(s32[512]{0:T(512)} %param.33) | copy-start | bytes 6148
  47.1 26.0 %all-to-all-start.1 = ((bf16[128,8,256]{2,1,0:T(8,128)(2,1)}), bf16[128,8,256]{2,1,0:T(8,128)(2,1)S(1)}, u32[]{:S(2)}, u32[]{:S(2)}) async-start(bf16[128,8,256]{2,1,0:T(8,128)(2,1)} %bitcast.6), calls=%async_computation.1 | async-start | bytes 1048576 | tf_op jit(solution)/shard_map/all_to_all | solution.py:289
  76.7 4.2 %collective-permute-start = (bf16[1536,256]{1,0:T(8,128)(2,1)S(1)}, bf16[1536,256]{1,0:T(8,128)(2,1)S(1)}, u32[]{:S(2)}, u32[]{:S(2)}) collective-permute-start(bf16[1536,256]{1,0:T(8,128)(2,1)S(1)} %shard_map.188), channel_id=1, source_target_pairs={{0,4},{4,0},{1,5},{5,1},{2,6},{6,2},{3,7},{7,3},{8,12},{12,8},{9,1... | collective-permute-start | bytes 2359304 | tf_op jit(solution)/shard_map/ppermute | solution.py:298
  82.2 41.7 %all-to-all-start.2 = ((bf16[128,8,640]{2,1,0:T(8,128)(2,1)}), bf16[128,8,640]{2,1,0:T(8,128)(2,1)S(1)}, u32[]{:S(2)}, u32[]{:S(2)}) async-start(bf16[128,8,640]{2,1,0:T(8,128)(2,1)} %bitcast.14), calls=%async_computation.2 | async-start | bytes 2621440 | tf_op jit(solution)/shard_map/all_to_all | solution.py:289
  124.1 12.1 %collective-permute-start.3 = (f32[2,8,384]{2,1,0:T(8,128)S(1)}, f32[2,8,384]{2,1,0:T(8,128)S(1)}, u32[]{:S(2)}, u32[]{:S(2)}) collective-permute-start(f32[2,8,384]{2,1,0:T(8,128)S(1)} %shard_map.191.own_ref), channel_id=1, source_target_pairs={{3,0},{0,1},{1,2},{2,3},{7,4},{4,5},{5,6},{6,7},{11,8},{8,9},{9,10... | collective-permute-start | bytes 73736 | tf_op jit(solution)/shard_map/ppermute | solution.py:309
  127.2 9.0 %collective-permute-start.2 = (f32[2,8,384]{2,1,0:T(8,128)S(1)}, f32[2,8,384]{2,1,0:T(8,128)S(1)}, u32[]{:S(2)}, u32[]{:S(2)}) collective-permute-start(f32[2,8,384]{2,1,0:T(8,128)S(1)} %shard_map.191.own_ref), channel_id=1, source_target_pairs={{2,0},{3,1},{0,2},{1,3},{6,4},{7,5},{4,6},{5,7},{10,8},{11,9},{8,1... | collective-permute-start | bytes 73736 | tf_op jit(solution)/shard_map/ppermute | solution.py:309
  131.6 4.7 %collective-permute-start.1 = (f32[2,8,384]{2,1,0:T(8,128)S(1)}, f32[2,8,384]{2,1,0:T(8,128)S(1)}, u32[]{:S(2)}, u32[]{:S(2)}) collective-permute-start(f32[2,8,384]{2,1,0:T(8,128)S(1)} %shard_map.191.own_ref), channel_id=1, source_target_pairs={{1,0},{2,1},{3,2},{0,3},{5,4},{6,5},{7,6},{4,7},{9,8},{10,9},{11,1... | collective-permute-start | bytes 73736 | tf_op jit(solution)/shard_map/ppermute | solution.py:309

commit v3 on v2

--- a/solution.py
+++ b/solution.py
@@ -105,16 +105,19 @@
 ):
     edges = senders_ref.shape[1]
     nodes, width = latent_ref.shape
-    step = 256
-    total = init_ref[0].astype(F32)
-    for start in range(0, edges, step):
-        span = slice(start, start + step)
-        chosen = select_rows(columns_of(senders_ref[:, span]), pieces_ref.shape[0])
-        raw = dot(chosen, pieces_ref[...]).astype(BF16)
-        embedded = silu(dot(raw, w_embed_ref[...])).astype(BF16)
-        geo_part = inner_rows(geometry_ref[:, span], w_geo_ref[...])
-        message = silu(dot(embedded, w_g2m_ref[...]) + geo_part).astype(BF16)
-        total = total + dot(select_columns(receivers_ref[:, span], nodes), message)
+    inputs = geometry_ref.shape[0]
+    geometry = geometry_ref[...].astype(F32)
+    blank = jnp.zeros((LANES - inputs, edges), F32)
+    geometry = jnp.transpose(jnp.concatenate([geometry, blank], axis=0)).astype(BF16)
+    blank = jnp.zeros((LANES - inputs, width), F32)
+    weights = [w_g2m_ref[...].astype(F32), w_geo_ref[...].astype(F32), blank]
+    weights = jnp.concatenate(weights, axis=0).astype(BF16)
+    chosen = select_rows(columns_of(senders_ref[...]), pieces_ref.shape[0])
+    raw = dot(chosen, pieces_ref[...]).astype(BF16)
+    embedded = silu(dot(raw, w_embed_ref[...])).astype(BF16)
+    message = silu(dot(jnp.concatenate([embedded, geometry], axis=1), weights)).astype(BF16)
+    gather = select_columns(receivers_ref[...], nodes)
+    total = init_ref[0].astype(F32) + dot(gather, message)
     latent = total.astype(BF16)
     latent_ref[...] = latent
     ids = slot_columns(send_rows_ref[0])
@@ -179,11 +182,12 @@
 
 
 def weight_grads(
-    half_ref, table_ref, send_grad_ref, latent_ref, recv_grad_ref, aggregate_ref, d_update_ref, out_ref
+    mine, sibling_ref, table_ref, send_grad_ref, latent_ref, recv_grad_ref, aggregate_ref, d_update_ref, out_ref
 ):
     half = out_ref.shape[1]
     width = latent_ref.shape[1]
-    columns = pl.ds(pl.multiple_of(half_ref[0] * half, half), half)
+    core = 1 - sibling_ref[0] if mine else sibling_ref[0]
+    columns = pl.ds(pl.multiple_of(core * half, half), half)
     pairs = ((table_ref, send_grad_ref), (latent_ref, recv_grad_ref), (aggregate_ref, d_update_ref))
     for i, (left, right) in enumerate(pairs):
         product = inner_rows(left[...], right[:, columns])
@@ -218,8 +222,12 @@
     out_ref[...] = total
 
 
-def add_samples(core_ref, own_ref, next_ref, across_ref, last_ref, out_ref):
-    total = (own_ref[...] + across_ref[...]) + (next_ref[...] + last_ref[...])
+def add_pair(own_ref, other_ref, out_ref):
+    out_ref[...] = own_ref[...] + other_ref[...]
+
+
+def add_samples(sibling_ref, own_ref, other_ref, out_ref):
+    total = own_ref[...] + other_ref[...]
     tile = total.shape[1]
     half = out_ref.shape[1] // 2
     extra = tile // 2
@@ -227,12 +235,12 @@
     parts = [total[h, k * extra : (k + 1) * extra, half:] for h in range(2) for k in range(2)]
     middle = jnp.concatenate(parts, axis=1)
 
-    @pl.when(core_ref[0] == 0)
+    @pl.when(sibling_ref[0] == 1)
     def _():
         out_ref[:tile, :] = whole
         out_ref[tile:, :] = middle
 
-    @pl.when(core_ref[0] == 1)
+    @pl.when(sibling_ref[0] == 0)
     def _():
         out_ref[:extra, :] = middle
         out_ref[extra:, :] = whole
@@ -245,7 +253,7 @@
     nodes = recv_grad_ref.shape[0]
     slots, groups = send_rows_ref.shape[1:]
     scatter_blocks(spread, back_ref)
-    total = send_grad_ref[...].astype(F32)
+    total = send_grad_ref[slots * groups :, :].astype(F32)
     wanted = send_rows_ref[0]
     for j in range(slots):
         arrived = split_load(spread, j, slots, groups).astype(BF16)
@@ -289,7 +297,7 @@
     return lax.all_to_all(x, axis, split_axis=0, concat_axis=0, tiled=True)
 
 
-def share(keep, send, back, core):
+def share(keep, send, back, sibling):
     half = keep.shape[1]
     tile = 8
     chips = lax.axis_size("graph_0") * lax.axis_size("graph_1")
@@ -305,13 +313,12 @@
     own = kernel(add_chips, shape((2, tile, lanes - half), F32), [], 10**7)(
         arrived.reshape(chips, 2, tile, lanes)
     )
-    others = [
-        lax.ppermute(own, "sample", [((i + step) % samples, i) for i in range(samples)])
-        for step in range(1, samples)
-    ]
+    other = lax.ppermute(own, "sample", [(i, i ^ 1) for i in range(samples)])
+    own = kernel(add_pair, shape(own.shape, F32), [], 10**6)(own, other)
+    other = lax.ppermute(own, "sample", [(i, samples - 1 - i) for i in range(samples)])
     rows = keep.shape[0] // (2 * chips)
     grad_weights = kernel(add_samples, shape((rows, 2 * half), F32), [], 10**6, 1, pltpu.SMEM)(
-        core, own, *others
+        sibling, own, other
     )
     return arrived.reshape(2 * chips * tile, lanes), grad_weights
 
@@ -344,6 +351,8 @@
     table_rows = groups * halo_slots + nodes
     halves = 2 * groups * halo_slots
 
+    sibling = 1 - lax.axis_index("graph_2").astype(jnp.int32)[None]
+    sibling, g2m_counts = lax.optimization_barrier((sibling, g2m_counts))
     grid_rows = jnp.transpose(g2m_send_rows, (0, 2, 1))
     mesh_rows = jnp.transpose(mesh_send_rows, (0, 2, 1))
     raw_rows = kernel(
@@ -407,11 +416,10 @@
         cotangent,
     )
 
-    core = lax.axis_index("graph_2").astype(jnp.int32)[None]
     operands = (table, send_grad, latent, recv_grad, aggregate, d_update)
-    send = kernel(weight_grads, shape((3 * width, half), BF16), [], 5 * 10**8, 1, pltpu.SMEM)(1 - core, *operands)
-    keep = kernel(weight_grads, shape((3 * width, half), F32), [], 5 * 10**8, 1, pltpu.SMEM)(core, *operands)
-    arrived, grad_weights = share(keep, send, back, core)
+    send = kernel(functools.partial(weight_grads, False), shape((3 * width, half), BF16), [], 5 * 10**8, 1, pltpu.SMEM)(sibling, *operands)
+    keep = kernel(functools.partial(weight_grads, True), shape((3 * width, half), F32), [], 5 * 10**8, 1, pltpu.SMEM)(sibling, *operands)
+    arrived, grad_weights = share(keep, send, back, sibling)
 
     grad_mesh = kernel(
         return_grads,
@@ -421,7 +429,7 @@
     )(
         arrived,
         mesh_rows,
-        send_grad[groups * halo_slots :],
+        send_grad,
         recv_grad,
         a_send,
         a_recv,

time: 139 us -> 134 us (0.964)
  blocking collectives: 39 us -> 106 us
  waiting for transfers between devices: 58.3 us -> 3.14 us
  starting transfers between devices: 23.5 us -> 9.41 us
  Pallas kernels: 15.1 us -> 12.5 us
    all_to_all x1 -> x3, blocking collectives: 39 us -> 106 us  [exchange(): return lax.all_to_all(x, axis, split_axis=0, concat_axis=0, tiled=True)]
    all_to_all x2 -> x0, waiting for transfers between devices: 56.6 us -> none  [exchange(): return lax.all_to_all(x, axis, split_axis=0, concat_axis=0, tiled=True)]
    all_to_all x2 -> x0, starting transfers between devices: 11 us -> none  [exchange(): return lax.all_to_all(x, axis, split_axis=0, concat_axis=0, tiled=True)]
    ppermute x3 -> x2, starting transfers between devices: 10.5 us -> 7.49 us  [the longest x1 4.38 us: share(): lax.ppermute(own, 'sample', [(i, samples - 1 - i) for i in range(samples)])]
    pallas_call x9 -> x10, Pallas kernels: 15.1 us -> 12.5 us  [call(): pl.pallas_call(body, out_shape=outs, in_specs=specs, out_specs=jax.tree.m...]
    ppermute x3 -> x2, waiting for transfers between devices: 0.01 us -> 1.45 us  [the longest x1 1.45 us: share(): other = lax.ppermute(own, 'sample', [(i, i ^ 1) for i in range(samples)])]
  transfers between devices with their start and end apart: 6 -> 3, of which waited for: 3 -> 2; matrix products, arithmetic and copies ran while one was open for 0% -> 0% of each run, Pallas kernels for 2% -> 2%
where the time goes in v3:
time: 134 us; the launch traced here: 132 us
  blocking collectives  106 us (79%)
  Pallas kernels  12.5 us (9%)
  starting transfers between devices  9.41 us (7%)
  waiting for transfers between devices  3.14 us (2%)
    all_to_all x3, blocking collectives, exchange(): return lax.all_to_all(x, axis, split_axis=0, concat_axis=0, tiled=True)  106 us
    pallas_call x10, Pallas kernels, call(): pl.pallas_call(body, out_shape=outs, in_specs=specs, out_specs=jax.tree.m...  12.5 us
    ppermute x1, starting transfers between devices, share(): lax.ppermute(own, 'sample', [(i, samples - 1 - i) for i in range(samples)])  4.38 us
    ppermute x1, starting transfers between devices, share(): other = lax.ppermute(own, 'sample', [(i, i ^ 1) for i in range(samples)])  3.11 us
  transfers between devices with their start and end apart: 3, of which 2 were waited for; matrix products, arithmetic and copies ran while one was open for 0% of the time, Pallas kernels for 2%

profile of v3, /device:TPU:1, one launch (start us, length us, event | category | flops | bytes accessed | tf_op | source)
XLA Modules:
  0.0 132.1 jit_solution(308628943562039213)
XLA Ops:
  0.6 0.0 copy-start.13
  0.6 0.0 copy-start.9
  0.7 0.0 copy-start.8
  0.7 0.0 copy-start.10
  0.7 0.0 copy-start
  0.7 0.0 copy-start.4
  0.7 0.0 copy-start.7
  0.7 0.0 copy-start.5
  0.7 2.5 %shard_map.184 = bf16[1024,256]{1,0:T(8,128)(2,1)} custom-call(s32[1,8,128]{2,1,0:T(8,128)} %bitcast.33, s32[1,128]{1,0:T(1,128)} %counts_hbm, bf16[1,512,256]{2,1,0:T(8,128)(2,1)} %grid_hbm.1), custom_call_target="tpu_custom_call" | custom-call | flops 100000000 | bytes 266752 | tf_op jit(solution)/shard_map/pallas_call | solution.py:283
  3.2 39.0 %all_to_all.15 = bf16[128,8,256]{2,1,0:T(8,128)(2,1)S(1)} all-to-all(bf16[128,8,256]{2,1,0:T(8,128)(2,1)} %bitcast.32), channel_id=1, replica_groups=mesh['graph_0'=8,'graph_1'=8,'graph_2'=2,'sample'=4] {'graph_0','graph_1..., dimensions={0} | all-to-all | bytes 1048576 | tf_op jit(solution)/shard_map/all_to_all | solution.py:297
  42.2 0.0 copy-done.13
  42.2 0.0 copy-done.9
  42.2 0.0 copy-done.8
  42.2 0.0 copy-done.10
  42.3 0.0 copy-done
  42.3 0.0 copy-done.4
  42.3 0.0 copy-done.7
  42.3 0.0 copy-done.5
  42.3 0.0 copy-start.1
  42.3 0.0 copy-start.2
  42.3 0.0 copy-start.3
  42.3 0.0 copy-start.6
  42.3 0.0 copy-start.11
  42.4 0.0 copy-start.12
  42.4 3.3 %shard_map.185 = (bf16[128,512]{1,0:T(8,128)(2,1)S(1)}, bf16[1024,256]{1,0:T(8,128)(2,1)S(1)}) custom-call(bf16[1024,256]{1,0:T(8,128)(2,1)S(1)} %bitcast.23, s32[1,1024]{1,0:T(1,128)S(1)} %bitcast.26, s32[1,1024]{1,0:T(1,128)S(1)} %bitcast.27, bf16[4,1024]{1,0:T(4,128)(2,1)S(1)} %copy-done.7, bf16[256,512]{1,0:T(8,128)(2,1)S(1)} %copy-done.4, ...), custom_call_target="tpu_custom_call" | custom-call | flops 2000000000 | bytes 1464320 | tf_op jit(solution)/shard_map/pallas_call | solution.py:283
  45.7 25.8 %all_to_all.16 = bf16[128,8,256]{2,1,0:T(8,128)(2,1)S(1)} all-to-all(bf16[128,8,256]{2,1,0:T(8,128)(2,1)S(1)} %bitcast.24), channel_id=1, replica_groups=mesh['graph_0'=8,'graph_1'=8,'graph_2'=2,'sample'=4] {'graph_0','graph_1..., dimensions={0} | all-to-all | bytes 1048576 | tf_op jit(solution)/shard_map/all_to_all | solution.py:297
  71.4 0.0 copy-done.1
  71.4 0.0 copy-done.2
  71.4 0.0 copy-done.3
  71.4 0.0 copy-done.6
  71.5 0.0 copy-done.11
  71.5 0.0 copy-done.12
  71.5 3.0 %shard_map.186 = (bf16[1,128,512]{2,1,0:T(8,128)(2,1)}, bf16[1024,256]{1,0:T(8,128)(2,1)S(1)}, bf16[640,512]{1,0:T(8,128)(2,1)S(1)}, bf16[640,512]{1,0:T(8,128)(...) custom-call(bf16[1024,256]{1,0:T(8,128)(2,1)S(1)} %bitcast.22, ...), custom_call_target="tpu_custom_call" | custom-call | flops 3000000000 | bytes 2363392 | tf_op jit(solution)/shard_map/pallas_call | solution.py:283
  74.5 0.6 shard_map.188
  75.1 1.9 %collective-permute-start = (bf16[1536,256]{1,0:T(8,128)(2,1)S(1)}, bf16[1536,256]{1,0:T(8,128)(2,1)S(1)}, u32[]{:S(2)}, u32[]{:S(2)}) collective-permute-start(bf16[1536,256]{1,0:T(8,128)(2,1)S(1)} %shard_map.188), channel_id=1, source_target_pairs={{0,4},{4,0},{1,5},{5,1},{2,6},{6,2},{3,7},{7,3},{8,12},{12,8},{9,1... | collective-permute-start | bytes 2359304 | tf_op jit(solution)/shard_map/ppermute | solution.py:306
  77.0 0.6 shard_map.187
  77.6 1.7 %collective-permute-done = bf16[1536,256]{1,0:T(8,128)(2,1)S(1)} collective-permute-done((bf16[1536,256]{1,0:T(8,128)(2,1)S(1)}, bf16[1536,256]{1,0:T(8,128)(2,1)S(1)}, u32[]{:S(2)}, u32[]{:S(2)}) %collective-permute-start) | collective-permute-done | bytes 786464 | tf_op jit(solution)/shard_map/ppermute | solution.py:306
  79.3 0.3 shard_map.189
  79.5 41.3 %all_to_all.17 = bf16[128,8,640]{2,1,0:T(8,128)(2,1)S(1)} all-to-all(bf16[128,8,640]{2,1,0:T(8,128)(2,1)S(1)} %bitcast.20), channel_id=1, replica_groups=mesh['graph_0'=8,'graph_1'=8,'graph_2'=2,'sample'=4] {'graph_0','graph_1..., dimensions={0} | all-to-all | bytes 2621440 | tf_op jit(solution)/shard_map/all_to_all | solution.py:297
  120.8 0.1 shard_map.191.own_ref
  120.9 3.1 %collective-permute-start.1 = (f32[2,8,384]{2,1,0:T(8,128)S(1)}, f32[2,8,384]{2,1,0:T(8,128)S(1)}, u32[]{:S(2)}, u32[]{:S(2)}) collective-permute-start(f32[2,8,384]{2,1,0:T(8,128)S(1)} %shard_map.191.own_ref), channel_id=1, source_target_pairs={{0,1},{1,0},{2,3},{3,2},{4,5},{5,4},{6,7},{7,6},{8,9},{9,8},{10,11... | collective-permute-start | bytes 73736 | tf_op jit(solution)/shard_map/ppermute | solution.py:316
  124.0 1.4 %collective-permute-done.1.other_ref = f32[2,8,384]{2,1,0:T(8,128)S(1)} collective-permute-done((f32[2,8,384]{2,1,0:T(8,128)S(1)}, f32[2,8,384]{2,1,0:T(8,128)S(1)}, u32[]{:S(2)}, u32[]{:S(2)}) %collective-permute-start.1) | collective-permute-done | bytes 24608 | tf_op jit(solution)/shard_map/ppermute | solution.py:316
  125.5 4.4 %collective-permute-start.2 = (f32[2,8,384]{2,1,0:T(8,128)S(1)}, f32[2,8,384]{2,1,0:T(8,128)S(1)}, u32[]{:S(2)}, u32[]{:S(2)}) collective-permute-start(f32[2,8,384]{2,1,0:T(8,128)S(1)} %shard_map.192.own_ref), channel_id=1, source_target_pairs={{0,3},{1,2},{2,1},{3,0},{4,7},{5,6},{6,5},{7,4},{8,11},{9,10},{10,... | collective-permute-start | bytes 73736 | tf_op jit(solution)/shard_map/ppermute | solution.py:318
  129.9 1.6 %shard_map.190 = f32[1,128,512]{2,1,0:T(8,128)} custom-call(bf16[1024,640]{1,0:T(8,128)(2,1)S(1)} %bitcast.19, s32[1,4,128]{2,1,0:T(4,128)S(1)} %bitcast.31, bf16[640,512]{1,0:T(8,128)(2,1)S(1)} %get-tuple-element.20.send_grad_ref, bf16[128,512]{1,0:T(8,128)(2,1)S(1)} %get-tuple-element.21.recv_grad_ref, bf16[512,512]{1,0:T(8,128)(2,1)S(1)} %copy-done.2, ...), custom_call_target="tpu_custom_call" | custom-call | flops 1000000000 | bytes 3278848 | tf_op jit(solution)/shard_map/pallas_call | solution.py:283
  131.5 0.0 collective-permute-done.2.other_ref
  131.5 0.6 shard_map.193
  (1 shorter events, 0.0 us)
Async XLA Ops:
  0.6 41.6 %copy-start.13 = (s32[1,128,4]{1,2,0:T(4,128)S(1)}, s32[1,128,4]{1,2,0:T(4,128)}, u32[]{:S(2)}) copy-start(s32[1,128,4]{1,2,0:T(4,128)} %param.31) | copy-start | bytes 6148
  0.6 41.6 %copy-start.9 = (s32[1024]{0:T(1024)S(1)}, s32[1024]{0:T(1024)}, u32[]{:S(2)}) copy-start(s32[1024]{0:T(1024)} %param.30) | copy-start | bytes 12292
  0.7 41.6 %copy-start.8 = (s32[1024]{0:T(1024)S(1)}, s32[1024]{0:T(1024)}, u32[]{:S(2)}) copy-start(s32[1024]{0:T(1024)} %param.29) | copy-start | bytes 12292
  0.7 41.6 %copy-start.10 = (bf16[4,512]{1,0:T(4,128)(2,1)S(1)}, bf16[4,512]{1,0:T(4,128)(2,1)}, u32[]{:S(2)}) copy-start(bf16[4,512]{1,0:T(4,128)(2,1)} %w_geo_ref.1) | copy-start | bytes 12292
  0.7 41.6 %copy-start = (bf16[512,512]{1,0:T(8,128)(2,1)S(1)}, bf16[512,512]{1,0:T(8,128)(2,1)}, u32[]{:S(2)}) copy-start(bf16[512,512]{1,0:T(8,128)(2,1)} %w_g2m_ref.1) | copy-start | bytes 1572868
  0.7 41.6 %copy-start.4 = (bf16[256,512]{1,0:T(8,128)(2,1)S(1)}, bf16[256,512]{1,0:T(8,128)(2,1)}, u32[]{:S(2)}) copy-start(bf16[256,512]{1,0:T(8,128)(2,1)} %w_embed_ref.1) | copy-start | bytes 786436
  0.7 41.6 %copy-start.7 = (bf16[4,1024]{1,0:T(4,128)(2,1)S(1)}, bf16[4,1024]{1,0:T(4,128)(2,1)}, u32[]{:S(2)}) copy-start(bf16[4,1024]{1,0:T(4,128)(2,1)} %geometry_ref.1) | copy-start | bytes 24580
  0.7 41.6 %copy-start.5 = (bf16[1,128,512]{2,1,0:T(8,128)(2,1)S(1)}, bf16[1,128,512]{2,1,0:T(8,128)(2,1)}, u32[]{:S(2)}) copy-start(bf16[1,128,512]{2,1,0:T(8,128)(2,1)} %init_ref.1) | copy-start | bytes 393220
  42.3 29.1 %copy-start.1 = (bf16[512,512]{1,0:T(8,128)(2,1)S(1)}, bf16[512,512]{1,0:T(8,128)(2,1)}, u32[]{:S(2)}) copy-start(bf16[512,512]{1,0:T(8,128)(2,1)} %b_node_ref.1) | copy-start | bytes 1572868
  42.3 29.1 %copy-start.2 = (bf16[512,512]{1,0:T(8,128)(2,1)S(1)}, bf16[512,512]{1,0:T(8,128)(2,1)}, u32[]{:S(2)}) copy-start(bf16[512,512]{1,0:T(8,128)(2,1)} %a_send_ref.3) | copy-start | bytes 1572868
  42.3 29.1 %copy-start.3 = (bf16[512,512]{1,0:T(8,128)(2,1)S(1)}, bf16[512,512]{1,0:T(8,128)(2,1)}, u32[]{:S(2)}) copy-start(bf16[512,512]{1,0:T(8,128)(2,1)} %a_recv_ref.3) | copy-start | bytes 1572868
  42.3 29.1 %copy-start.6 = (bf16[1,128,512]{2,1,0:T(8,128)(2,1)S(1)}, bf16[1,128,512]{2,1,0:T(8,128)(2,1)}, u32[]{:S(2)}) copy-start(bf16[1,128,512]{2,1,0:T(8,128)(2,1)} %cot_ref.3) | copy-start | bytes 393220
  42.3 29.1 %copy-start.11 = (s32[512]{0:T(512)S(1)}, s32[512]{0:T(512)}, u32[]{:S(2)}) copy-start(s32[512]{0:T(512)} %param.32) | copy-start | bytes 6148
  42.4 29.1 %copy-start.12 = (s32[512]{0:T(512)S(1)}, s32[512]{0:T(512)}, u32[]{:S(2)}) copy-start(s32[512]{0:T(512)} %param.33) | copy-start | bytes 6148
  75.1 4.2 %collective-permute-start = (bf16[1536,256]{1,0:T(8,128)(2,1)S(1)}, bf16[1536,256]{1,0:T(8,128)(2,1)S(1)}, u32[]{:S(2)}, u32[]{:S(2)}) collective-permute-start(bf16[1536,256]{1,0:T(8,128)(2,1)S(1)} %shard_map.188), channel_id=1, source_target_pairs={{0,4},{4,0},{1,5},{5,1},{2,6},{6,2},{3,7},{7,3},{8,12},{12,8},{9,1... | collective-permute-start | bytes 2359304 | tf_op jit(solution)/shard_map/ppermute | solution.py:306
  120.9 4.6 %collective-permute-start.1 = (f32[2,8,384]{2,1,0:T(8,128)S(1)}, f32[2,8,384]{2,1,0:T(8,128)S(1)}, u32[]{:S(2)}, u32[]{:S(2)}) collective-permute-start(f32[2,8,384]{2,1,0:T(8,128)S(1)} %shard_map.191.own_ref), channel_id=1, source_target_pairs={{0,1},{1,0},{2,3},{3,2},{4,5},{5,4},{6,7},{7,6},{8,9},{9,8},{10,11... | collective-permute-start | bytes 73736 | tf_op jit(solution)/shard_map/ppermute | solution.py:316
  125.5 6.0 %collective-permute-start.2 = (f32[2,8,384]{2,1,0:T(8,128)S(1)}, f32[2,8,384]{2,1,0:T(8,128)S(1)}, u32[]{:S(2)}, u32[]{:S(2)}) collective-permute-start(f32[2,8,384]{2,1,0:T(8,128)S(1)} %shard_map.192.own_ref), channel_id=1, source_target_pairs={{0,3},{1,2},{2,1},{3,0},{4,7},{5,6},{6,5},{7,4},{8,11},{9,10},{10,... | collective-permute-start | bytes 73736 | tf_op jit(solution)/shard_map/ppermute | solution.py:318

commit v4 on v3

--- a/solution.py
+++ b/solution.py
@@ -92,10 +92,12 @@
     slots = rows.shape[1]
     slot = lax.broadcasted_iota(jnp.int32, rows.shape[1:], 0)
     ids = slot_columns(jnp.where(slot < counts[...], rows[0], -1))
-    chosen = [select_rows(ids[j], grid.shape[1]) for j in range(slots)]
+    chosen = jnp.concatenate([select_rows(column, grid.shape[1]) for column in ids], axis=0)
     copies[2].wait()
+    picked = dot(chosen, grid[0])
+    groups = rows.shape[2]
     for j in range(slots):
-        strided_store(spread, j, slots, dot(chosen[j], grid[0]))
+        strided_store(spread, j, slots, picked[j * groups : (j + 1) * groups])
     gather_blocks(spread, out_ref)
 
 
@@ -121,8 +123,10 @@
     latent = total.astype(BF16)
     latent_ref[...] = latent
     ids = slot_columns(send_rows_ref[0])
+    picked = dot(jnp.concatenate([select_rows(column, nodes) for column in ids], axis=0), latent)
+    groups = send_rows_ref.shape[2]
     for j in range(len(ids)):
-        split_store(spread, j, len(ids), dot(select_rows(ids[j], nodes), latent))
+        split_store(spread, j, len(ids), picked[j * groups : (j + 1) * groups])
     gather_blocks(spread, halo_ref)
 
 
@@ -141,10 +145,25 @@
     return jnp.concatenate(blocks, axis=1)
 
 
+def weight_grads(
+    mine, sibling_ref, table_ref, send_grad_ref, latent_ref, recv_grad_ref, aggregate_ref,
+    d_update_ref, out_ref,
+):
+    half = out_ref.shape[1]
+    width = latent_ref.shape[1]
+    core = 1 - sibling_ref[0] if mine else sibling_ref[0]
+    columns = pl.ds(pl.multiple_of(core * half, half), half)
+    pairs = ((table_ref, send_grad_ref), (latent_ref, recv_grad_ref), (aggregate_ref, d_update_ref))
+    for i, (left, right) in enumerate(pairs):
+        product = inner_rows(left[...], right[:, columns])
+        out_ref[i * width : (i + 1) * width, :] = product.astype(out_ref.dtype)
+
+
 def process(
-    slots, halo_ref, latent_ref, senders_ref, receivers_ref, a_send_ref, a_recv_ref, b_node_ref,
+    slots, sibling_ref, halo_ref, latent_ref, senders_ref, receivers_ref, a_send_ref, a_recv_ref, b_node_ref,
     cot_ref,
-    out_ref, back_ref, table_ref, send_grad_ref, recv_grad_ref, aggregate_ref, d_update_ref, spread,
+    out_ref, back_ref, table_ref, send_grad_ref, recv_grad_ref, aggregate_ref, d_update_ref, send_ref,
+    spread,
 ):
     nodes, width = latent_ref.shape
     rows = table_ref.shape[0]
@@ -162,7 +181,8 @@
     gather = select_columns(receivers, nodes)
     sent = dot(select_rows(columns_of(ids), rows), table_ref[...]).astype(BF16)
     own = dot(receive, latent).astype(BF16)
-    pre_act = dot(sent, a_send_ref[...]) + dot(own, a_recv_ref[...])
+    weights = jnp.concatenate([a_send_ref[...], a_recv_ref[...]], axis=0)
+    pre_act = dot(jnp.concatenate([sent, own], axis=1), weights)
     gate = logistic(pre_act)
     aggregate = dot(gather, (pre_act * gate).astype(BF16)).astype(BF16)
     aggregate_ref[...] = aggregate
@@ -173,25 +193,17 @@
     d_update_ref[...] = d_update
     d_aggregate = times_transposed(d_update, b_node_ref[...]).astype(BF16)
     d_pre = (dot(receive, d_aggregate) * slope_from(pre_act, gate)).astype(BF16)
-    recv_grad_ref[...] = dot(gather, d_pre).astype(BF16)
-    send_grad = dot(select_columns(ids, rows), d_pre)
+    sums = dot(jnp.concatenate([select_columns(ids, rows), gather], axis=0), d_pre)
+    recv_grad_ref[...] = sums[rows:].astype(BF16)
+    send_grad = sums[:rows]
     send_grad_ref[...] = send_grad.astype(BF16)
     for j in range(slots):
         split_store(spread, j, slots, send_grad[j * groups : (j + 1) * groups])
     gather_blocks(spread, back_ref)
-
-
-def weight_grads(
-    mine, sibling_ref, table_ref, send_grad_ref, latent_ref, recv_grad_ref, aggregate_ref, d_update_ref, out_ref
-):
-    half = out_ref.shape[1]
-    width = latent_ref.shape[1]
-    core = 1 - sibling_ref[0] if mine else sibling_ref[0]
-    columns = pl.ds(pl.multiple_of(core * half, half), half)
-    pairs = ((table_ref, send_grad_ref), (latent_ref, recv_grad_ref), (aggregate_ref, d_update_ref))
-    for i, (left, right) in enumerate(pairs):
-        product = inner_rows(left[...], right[:, columns])
-        out_ref[i * width : (i + 1) * width, :] = product.astype(out_ref.dtype)
+    weight_grads(
+        False, sibling_ref, table_ref, send_grad_ref, latent_ref, recv_grad_ref, aggregate_ref,
+        d_update_ref, send_ref,
+    )
 
 
 def pack(keep_ref, other_ref, back_ref, out_ref):
@@ -215,19 +227,18 @@
 
 def add_chips(arrived_ref, out_ref):
     chips = arrived_ref.shape[0]
-    skip = arrived_ref.shape[3] - out_ref.shape[2]
+    skip = arrived_ref.shape[3] - out_ref.shape[3]
     total = arrived_ref[0, :, :, skip:].astype(F32)
     for i in range(1, chips):
         total = total + arrived_ref[i, :, :, skip:].astype(F32)
-    out_ref[...] = total
-
-
-def add_pair(own_ref, other_ref, out_ref):
-    out_ref[...] = own_ref[...] + other_ref[...]
-
-
-def add_samples(sibling_ref, own_ref, other_ref, out_ref):
-    total = own_ref[...] + other_ref[...]
+    for i in range(out_ref.shape[0]):
+        out_ref[i] = total
+
+
+def add_samples(sibling_ref, arrived_ref, out_ref):
+    total = arrived_ref[0]
+    for i in range(1, arrived_ref.shape[0]):
+        total = total + arrived_ref[i]
     tile = total.shape[1]
     half = out_ref.shape[1] // 2
     extra = tile // 2
@@ -253,11 +264,11 @@
     nodes = recv_grad_ref.shape[0]
     slots, groups = send_rows_ref.shape[1:]
     scatter_blocks(spread, back_ref)
-    total = send_grad_ref[slots * groups :, :].astype(F32)
     wanted = send_rows_ref[0]
-    for j in range(slots):
-        arrived = split_load(spread, j, slots, groups).astype(BF16)
-        total = total + dot(select_columns(wanted[j : j + 1], nodes), arrived)
+    arrived = [split_load(spread, j, slots, groups).astype(BF16) for j in range(slots)]
+    chosen = [select_columns(wanted[j : j + 1], nodes) for j in range(slots)]
+    total = dot(jnp.concatenate(chosen, axis=1), jnp.concatenate(arrived, axis=0))
+    total = total + send_grad_ref[slots * groups :, :].astype(F32)
     high = total.astype(BF16)
     rest = total - high.astype(F32)
     low = rest.astype(BF16)
@@ -310,15 +321,13 @@
         back.reshape(chips, 2, tile, half),
     )
     arrived = exchange(packed.reshape(2 * chips, tile, lanes), GRAPH)
-    own = kernel(add_chips, shape((2, tile, lanes - half), F32), [], 10**7)(
+    copies = kernel(add_chips, shape((samples, 2, tile, lanes - half), F32), [], 10**7)(
         arrived.reshape(chips, 2, tile, lanes)
     )
-    other = lax.ppermute(own, "sample", [(i, i ^ 1) for i in range(samples)])
-    own = kernel(add_pair, shape(own.shape, F32), [], 10**6)(own, other)
-    other = lax.ppermute(own, "sample", [(i, samples - 1 - i) for i in range(samples)])
+    copies = exchange(copies, "sample")
     rows = keep.shape[0] // (2 * chips)
     grad_weights = kernel(add_samples, shape((rows, 2 * half), F32), [], 10**6, 1, pltpu.SMEM)(
-        sibling, own, other
+        sibling, copies
     )
     return arrived.reshape(2 * chips * tile, lanes), grad_weights
 
@@ -391,7 +400,7 @@
     )
     halo = exchange(halo.reshape(groups, 2 * halo_slots, half), GRAPH)
 
-    mesh_out, back, table, send_grad, recv_grad, aggregate, d_update = kernel(
+    mesh_out, back, table, send_grad, recv_grad, aggregate, d_update, send = kernel(
         functools.partial(process, halo_slots),
         (
             shape((1, nodes, width), BF16),
@@ -401,11 +410,15 @@
             shape((nodes, width), BF16),
             shape((nodes, width), BF16),
             shape((nodes, width), BF16),
+            shape((3 * width, half), BF16),
         ),
         [pltpu.VMEM((half // LANES, halves, LANES), F32)],
         3 * 10**9,
-        grant=GRANTS[2],
+        1,
+        pltpu.SMEM,
+        GRANTS[2],
     )(
+        sibling,
         halo.reshape(halves, half),
         latent,
         mesh_senders[None],
@@ -417,7 +430,6 @@
     )
 
     operands = (table, send_grad, latent, recv_grad, aggregate, d_update)
-    send = kernel(functools.partial(weight_grads, False), shape((3 * width, half), BF16), [], 5 * 10**8, 1, pltpu.SMEM)(sibling, *operands)
     keep = kernel(functools.partial(weight_grads, True), shape((3 * width, half), F32), [], 5 * 10**8, 1, pltpu.SMEM)(sibling, *operands)
     arrived, grad_weights = share(keep, send, back, sibling)
 

time: 134 us -> 133 us (level)
  starting transfers between devices: 9.41 us -> 5.91 us
  waiting for transfers between devices: 3.14 us -> 4.77 us
    ppermute x2 -> x0, starting transfers between devices: 7.49 us -> none  [the longest x1 4.38 us: share(): lax.ppermute(own, 'sample', [(i, samples - 1 - i) for i in range(samples)])]
    all_to_all x0 -> x1, starting transfers between devices: none -> 4.01 us  [exchange(): return lax.all_to_all(x, axis, split_axis=0, concat_axis=0, tiled=True)]
    all_to_all x0 -> x1, waiting for transfers between devices: none -> 3.08 us  [exchange(): return lax.all_to_all(x, axis, split_axis=0, concat_axis=0, tiled=True)]
    ppermute x2 -> x0, waiting for transfers between devices: 1.45 us -> none  [the longest x1 1.45 us: share(): other = lax.ppermute(own, 'sample', [(i, i ^ 1) for i in range(samples)])]
    pallas_call x10 -> x8, Pallas kernels: 12.5 us -> 13.3 us  [call(): pl.pallas_call(body, out_shape=outs, in_specs=specs, out_specs=jax.tree.m...]
  transfers between devices with their start and end apart: 3 -> 2, of which waited for: 2 -> 2; matrix products, arithmetic and copies ran while one was open for 0% -> 0% of each run, Pallas kernels for 2% -> 2%
where the time goes in v4:
time: 133 us; the launch traced here: 131 us
  blocking collectives  106 us (80%)
  Pallas kernels  13.3 us (10%)
  starting transfers between devices  5.91 us (4%)
  waiting for transfers between devices  4.77 us (4%)
    all_to_all x3, blocking collectives, exchange(): return lax.all_to_all(x, axis, split_axis=0, concat_axis=0, tiled=True)  106 us
    pallas_call x8, Pallas kernels, call(): pl.pallas_call(body, out_shape=outs, in_specs=specs, out_specs=jax.tree.m...  13.3 us
    all_to_all x1, starting transfers between devices, exchange(): return lax.all_to_all(x, axis, split_axis=0, concat_axis=0, tiled=True)  4.01 us
    all_to_all x1, waiting for transfers between devices, exchange(): return lax.all_to_all(x, axis, split_axis=0, concat_axis=0, tiled=True)  3.08 us
  transfers between devices with their start and end apart: 2, of which 2 were waited for; matrix products, arithmetic and copies ran while one was open for 0% of the time, Pallas kernels for 2%

profile of v4, /device:TPU:1, one launch (start us, length us, event | category | flops | bytes accessed | tf_op | source)
XLA Modules:
  0.0 131.0 jit_solution(15931524639200634338)
XLA Ops:
  0.6 0.0 copy-start.13
  0.6 0.0 copy-start.9
  0.7 0.0 copy-start.8
  0.7 0.0 copy-start.10
  0.7 0.0 copy-start
  0.7 0.0 copy-start.4
  0.7 0.0 copy-start.7
  0.7 0.0 copy-start.5
  0.7 2.5 %shard_map.184 = bf16[1024,256]{1,0:T(8,128)(2,1)} custom-call(s32[1,8,128]{2,1,0:T(8,128)} %bitcast.33, s32[1,128]{1,0:T(1,128)} %counts_hbm, bf16[1,512,256]{2,1,0:T(8,128)(2,1)} %grid_hbm.1), custom_call_target="tpu_custom_call" | custom-call | flops 100000000 | bytes 266752 | tf_op jit(solution)/shard_map/pallas_call | solution.py:294
  3.2 39.0 %all_to_all.20 = bf16[128,8,256]{2,1,0:T(8,128)(2,1)S(1)} all-to-all(bf16[128,8,256]{2,1,0:T(8,128)(2,1)} %bitcast.32), channel_id=1, replica_groups=mesh['graph_0'=8,'graph_1'=8,'graph_2'=2,'sample'=4] {'graph_0','graph_1..., dimensions={0} | all-to-all | bytes 1048576 | tf_op jit(solution)/shard_map/all_to_all | solution.py:308
  42.2 0.0 copy-done.13
  42.3 0.0 copy-done.9
  42.3 0.0 copy-done.8
  42.3 0.0 copy-done.10
  42.3 0.0 copy-done
  42.3 0.0 copy-done.4
  42.3 0.0 copy-done.7
  42.3 0.0 copy-done.5
  42.3 0.0 copy-start.1
  42.3 0.0 copy-start.2
  42.3 0.0 copy-start.3
  42.3 0.0 copy-start.6
  42.4 0.0 copy-start.11
  42.4 0.0 copy-start.12
  42.4 3.2 %shard_map.185 = (bf16[128,512]{1,0:T(8,128)(2,1)S(1)}, bf16[1024,256]{1,0:T(8,128)(2,1)S(1)}) custom-call(bf16[1024,256]{1,0:T(8,128)(2,1)S(1)} %bitcast.23, s32[1,1024]{1,0:T(1,128)S(1)} %bitcast.26, s32[1,1024]{1,0:T(1,128)S(1)} %bitcast.27, bf16[4,1024]{1,0:T(4,128)(2,1)S(1)} %copy-done.7, bf16[256,512]{1,0:T(8,128)(2,1)S(1)} %copy-done.4, ...), custom_call_target="tpu_custom_call" | custom-call | flops 2000000000 | bytes 1464320 | tf_op jit(solution)/shard_map/pallas_call | solution.py:294
  45.6 25.8 %all_to_all.21 = bf16[128,8,256]{2,1,0:T(8,128)(2,1)S(1)} all-to-all(bf16[128,8,256]{2,1,0:T(8,128)(2,1)S(1)} %bitcast.24), channel_id=1, replica_groups=mesh['graph_0'=8,'graph_1'=8,'graph_2'=2,'sample'=4] {'graph_0','graph_1..., dimensions={0} | all-to-all | bytes 1048576 | tf_op jit(solution)/shard_map/all_to_all | solution.py:308
  71.4 0.0 copy-done.1
  71.4 0.0 copy-done.2
  71.4 0.0 copy-done.3
  71.4 0.0 copy-done.6
  71.4 0.0 copy-done.11
  71.4 0.0 copy-done.12
  71.4 3.8 %shard_map.186 = (bf16[1,128,512]{2,1,0:T(8,128)(2,1)}, bf16[1024,256]{1,0:T(8,128)(2,1)S(1)}, bf16[640,512]{1,0:T(8,128)(2,1)S(1)}, bf16[640,512]{1,0:T(8,128)(...) custom-call(s32[1]{0:T(128)} %bitcast.sibling_ref, ...), custom_call_target="tpu_custom_call" | custom-call | flops 3000000000 | bytes 2363396 | tf_op jit(solution)/shard_map/pallas_call | solution.py:294
  75.2 1.9 %collective-permute-start = (bf16[1536,256]{1,0:T(8,128)(2,1)S(1)}, bf16[1536,256]{1,0:T(8,128)(2,1)S(1)}, u32[]{:S(2)}, u32[]{:S(2)}) collective-permute-start(bf16[1536,256]{1,0:T(8,128)(2,1)S(1)} %get-tuple-element.25), channel_id=1, source_target_pairs={{0,4},{4,0},{1,5},{5,1},{2,6},{6,2},{3,7},{7,3},{8,12},{12,8},{9,1... | collective-permute-start | bytes 2359304 | tf_op jit(solution)/shard_map/ppermute | solution.py:317
  77.1 0.6 shard_map.187
  77.7 1.7 %collective-permute-done = bf16[1536,256]{1,0:T(8,128)(2,1)S(1)} collective-permute-done((bf16[1536,256]{1,0:T(8,128)(2,1)S(1)}, bf16[1536,256]{1,0:T(8,128)(2,1)S(1)}, u32[]{:S(2)}, u32[]{:S(2)}) %collective-permute-start) | collective-permute-done | bytes 786464 | tf_op jit(solution)/shard_map/ppermute | solution.py:317
  79.4 0.3 shard_map.188
  79.6 41.3 %all_to_all.22 = bf16[128,8,640]{2,1,0:T(8,128)(2,1)S(1)} all-to-all(bf16[128,8,640]{2,1,0:T(8,128)(2,1)S(1)} %bitcast.20), channel_id=1, replica_groups=mesh['graph_0'=8,'graph_1'=8,'graph_2'=2,'sample'=4] {'graph_0','graph_1..., dimensions={0} | all-to-all | bytes 2621440 | tf_op jit(solution)/shard_map/all_to_all | solution.py:308
  120.9 0.8 shard_map.190
  121.7 4.0 %all-to-all-start.3 = ((f32[4,2,8,384]{3,2,1,0:T(8,128)}), f32[4,2,8,384]{3,2,1,0:T(8,128)S(1)}, u32[]{:S(2)}, u32[]{:S(2)}) async-start(f32[4,2,8,384]{3,2,1,0:T(8,128)} %shard_map.190), calls=%async_computation.3 | async-start | bytes 196608 | tf_op jit(solution)/shard_map/all_to_all | solution.py:308
  125.7 1.6 %shard_map.189 = f32[1,128,512]{2,1,0:T(8,128)} custom-call(bf16[1024,640]{1,0:T(8,128)(2,1)S(1)} %bitcast.19, s32[1,4,128]{2,1,0:T(4,128)S(1)} %bitcast.31, bf16[640,512]{1,0:T(8,128)(2,1)S(1)} %get-tuple-element.21.send_grad_ref, bf16[128,512]{1,0:T(8,128)(2,1)S(1)} %get-tuple-element.22.recv_grad_ref, bf16[512,512]{1,0:T(8,128)(2,1)S(1)} %copy-done.2, ...), custom_call_target="tpu_custom_call" | custom-call | flops 1000000000 | bytes 3278848 | tf_op jit(solution)/shard_map/pallas_call | solution.py:294
  127.3 3.1 %all-to-all-done.3.arrived_ref = f32[4,2,8,384]{3,2,1,0:T(8,128)S(1)} async-done(((f32[4,2,8,384]{3,2,1,0:T(8,128)}), f32[4,2,8,384]{3,2,1,0:T(8,128)S(1)}, u32[]{:S(2)}, u32[]{:S(2)}) %all-to-all-start.3) | async-done | bytes 98336 | tf_op jit(solution)/shard_map/all_to_all | solution.py:308
  130.4 0.6 shard_map.191
Async XLA Ops:
  0.6 41.6 %copy-start.13 = (s32[1,128,4]{1,2,0:T(4,128)S(1)}, s32[1,128,4]{1,2,0:T(4,128)}, u32[]{:S(2)}) copy-start(s32[1,128,4]{1,2,0:T(4,128)} %param.31) | copy-start | bytes 6148
  0.6 41.6 %copy-start.9 = (s32[1024]{0:T(1024)S(1)}, s32[1024]{0:T(1024)}, u32[]{:S(2)}) copy-start(s32[1024]{0:T(1024)} %param.30) | copy-start | bytes 12292
  0.7 41.6 %copy-start.8 = (s32[1024]{0:T(1024)S(1)}, s32[1024]{0:T(1024)}, u32[]{:S(2)}) copy-start(s32[1024]{0:T(1024)} %param.29) | copy-start | bytes 12292
  0.7 41.6 %copy-start.10 = (bf16[4,512]{1,0:T(4,128)(2,1)S(1)}, bf16[4,512]{1,0:T(4,128)(2,1)}, u32[]{:S(2)}) copy-start(bf16[4,512]{1,0:T(4,128)(2,1)} %w_geo_ref.1) | copy-start | bytes 12292
  0.7 41.6 %copy-start = (bf16[512,512]{1,0:T(8,128)(2,1)S(1)}, bf16[512,512]{1,0:T(8,128)(2,1)}, u32[]{:S(2)}) copy-start(bf16[512,512]{1,0:T(8,128)(2,1)} %w_g2m_ref.1) | copy-start | bytes 1572868
  0.7 41.6 %copy-start.4 = (bf16[256,512]{1,0:T(8,128)(2,1)S(1)}, bf16[256,512]{1,0:T(8,128)(2,1)}, u32[]{:S(2)}) copy-start(bf16[256,512]{1,0:T(8,128)(2,1)} %w_embed_ref.1) | copy-start | bytes 786436
  0.7 41.6 %copy-start.7 = (bf16[4,1024]{1,0:T(4,128)(2,1)S(1)}, bf16[4,1024]{1,0:T(4,128)(2,1)}, u32[]{:S(2)}) copy-start(bf16[4,1024]{1,0:T(4,128)(2,1)} %geometry_ref.1) | copy-start | bytes 24580
  0.7 41.6 %copy-start.5 = (bf16[1,128,512]{2,1,0:T(8,128)(2,1)S(1)}, bf16[1,128,512]{2,1,0:T(8,128)(2,1)}, u32[]{:S(2)}) copy-start(bf16[1,128,512]{2,1,0:T(8,128)(2,1)} %init_ref.1) | copy-start | bytes 393220
  42.3 29.1 %copy-start.1 = (bf16[512,512]{1,0:T(8,128)(2,1)S(1)}, bf16[512,512]{1,0:T(8,128)(2,1)}, u32[]{:S(2)}) copy-start(bf16[512,512]{1,0:T(8,128)(2,1)} %b_node_ref.1) | copy-start | bytes 1572868
  42.3 29.1 %copy-start.2 = (bf16[512,512]{1,0:T(8,128)(2,1)S(1)}, bf16[512,512]{1,0:T(8,128)(2,1)}, u32[]{:S(2)}) copy-start(bf16[512,512]{1,0:T(8,128)(2,1)} %a_send_ref.3) | copy-start | bytes 1572868
  42.3 29.0 %copy-start.3 = (bf16[512,512]{1,0:T(8,128)(2,1)S(1)}, bf16[512,512]{1,0:T(8,128)(2,1)}, u32[]{:S(2)}) copy-start(bf16[512,512]{1,0:T(8,128)(2,1)} %a_recv_ref.3) | copy-start | bytes 1572868
  42.3 29.0 %copy-start.6 = (bf16[1,128,512]{2,1,0:T(8,128)(2,1)S(1)}, bf16[1,128,512]{2,1,0:T(8,128)(2,1)}, u32[]{:S(2)}) copy-start(bf16[1,128,512]{2,1,0:T(8,128)(2,1)} %cot_ref.3) | copy-start | bytes 393220
  42.4 29.0 %copy-start.11 = (s32[512]{0:T(512)S(1)}, s32[512]{0:T(512)}, u32[]{:S(2)}) copy-start(s32[512]{0:T(512)} %param.32) | copy-start | bytes 6148
  42.4 29.0 %copy-start.12 = (s32[512]{0:T(512)S(1)}, s32[512]{0:T(512)}, u32[]{:S(2)}) copy-start(s32[512]{0:T(512)} %param.33) | copy-start | bytes 6148
  75.2 4.2 %collective-permute-start = (bf16[1536,256]{1,0:T(8,128)(2,1)S(1)}, bf16[1536,256]{1,0:T(8,128)(2,1)S(1)}, u32[]{:S(2)}, u32[]{:S(2)}) collective-permute-start(bf16[1536,256]{1,0:T(8,128)(2,1)S(1)} %get-tuple-element.25), channel_id=1, source_target_pairs={{0,4},{4,0},{1,5},{5,1},{2,6},{6,2},{3,7},{7,3},{8,12},{12,8},{9,1... | collective-permute-start | bytes 2359304 | tf_op jit(solution)/shard_map/ppermute | solution.py:317
  121.7 8.7 %all-to-all-start.3 = ((f32[4,2,8,384]{3,2,1,0:T(8,128)}), f32[4,2,8,384]{3,2,1,0:T(8,128)S(1)}, u32[]{:S(2)}, u32[]{:S(2)}) async-start(f32[4,2,8,384]{3,2,1,0:T(8,128)} %shard_map.190), calls=%async_computation.3 | async-start | bytes 196608 | tf_op jit(solution)/shard_map/all_to_all | solution.py:308

commit v5 on v4

--- a/solution.py
+++ b/solution.py
@@ -28,7 +28,7 @@
 
 
 def logistic(v):
-    return 0.5 * jnp.tanh(0.5 * v) + 0.5
+    return 1.0 / (1.0 + jnp.exp(-v))
 
 
 def silu(v):
@@ -308,7 +308,7 @@
     return lax.all_to_all(x, axis, split_axis=0, concat_axis=0, tiled=True)
 
 
-def share(keep, send, back, sibling):
+def share(keep, send, back, core):
     half = keep.shape[1]
     tile = 8
     chips = lax.axis_size("graph_0") * lax.axis_size("graph_1")
@@ -321,13 +321,14 @@
         back.reshape(chips, 2, tile, half),
     )
     arrived = exchange(packed.reshape(2 * chips, tile, lanes), GRAPH)
+    arrived, core = lax.optimization_barrier((arrived, core))
     copies = kernel(add_chips, shape((samples, 2, tile, lanes - half), F32), [], 10**7)(
         arrived.reshape(chips, 2, tile, lanes)
     )
     copies = exchange(copies, "sample")
     rows = keep.shape[0] // (2 * chips)
     grad_weights = kernel(add_samples, shape((rows, 2 * half), F32), [], 10**6, 1, pltpu.SMEM)(
-        sibling, copies
+        1 - core, copies
     )
     return arrived.reshape(2 * chips * tile, lanes), grad_weights
 
@@ -360,8 +361,8 @@
     table_rows = groups * halo_slots + nodes
     halves = 2 * groups * halo_slots
 
-    sibling = 1 - lax.axis_index("graph_2").astype(jnp.int32)[None]
-    sibling, g2m_counts = lax.optimization_barrier((sibling, g2m_counts))
+    core = lax.axis_index("graph_2").astype(jnp.int32)[None]
+    core, g2m_counts = lax.optimization_barrier((core, g2m_counts))
     grid_rows = jnp.transpose(g2m_send_rows, (0, 2, 1))
     mesh_rows = jnp.transpose(mesh_send_rows, (0, 2, 1))
     raw_rows = kernel(
@@ -399,6 +400,8 @@
         mesh_rows,
     )
     halo = exchange(halo.reshape(groups, 2 * halo_slots, half), GRAPH)
+    halo, core = lax.optimization_barrier((halo, core))
+    sibling = 1 - core
 
     mesh_out, back, table, send_grad, recv_grad, aggregate, d_update, send = kernel(
         functools.partial(process, halo_slots),
@@ -431,7 +434,7 @@
 
     operands = (table, send_grad, latent, recv_grad, aggregate, d_update)
     keep = kernel(functools.partial(weight_grads, True), shape((3 * width, half), F32), [], 5 * 10**8, 1, pltpu.SMEM)(sibling, *operands)
-    arrived, grad_weights = share(keep, send, back, sibling)
+    arrived, grad_weights = share(keep, send, back, core)
 
     grad_mesh = kernel(
         return_grads,

time: 133 us -> 133 us (level)
  no operation moved by 1% of the time
where the time goes in v5:
time: 133 us; the launch traced here: 131 us
  blocking collectives  106 us (80%)
  Pallas kernels  13.4 us (10%)
  starting transfers between devices  5.91 us (4%)
  waiting for transfers between devices  4.76 us (4%)
    all_to_all x3, blocking collectives, exchange(): return lax.all_to_all(x, axis, split_axis=0, concat_axis=0, tiled=True)  106 us
    pallas_call x8, Pallas kernels, call(): pl.pallas_call(body, out_shape=outs, in_specs=specs, out_specs=jax.tree.m...  13.4 us
    all_to_all x1, starting transfers between devices, exchange(): return lax.all_to_all(x, axis, split_axis=0, concat_axis=0, tiled=True)  4 us
    all_to_all x1, waiting for transfers between devices, exchange(): return lax.all_to_all(x, axis, split_axis=0, concat_axis=0, tiled=True)  3.07 us
  transfers between devices with their start and end apart: 2, of which 2 were waited for; matrix products, arithmetic and copies ran while one was open for 0% of the time, Pallas kernels for 2%

profile of v5, /device:TPU:1, one launch (start us, length us, event | category | flops | bytes accessed | tf_op | source)
XLA Modules:
  0.0 131.1 jit_solution(15487605360933414229)
XLA Ops:
  0.6 0.0 copy-start.13
  0.6 0.0 copy-start.9
  0.7 0.0 copy-start.8
  0.7 0.0 copy-start.10
  0.7 0.0 copy-start
  0.7 0.0 copy-start.4
  0.7 0.0 copy-start.7
  0.7 0.0 copy-start.5
  0.7 2.5 %shard_map.184 = bf16[1024,256]{1,0:T(8,128)(2,1)} custom-call(s32[1,8,128]{2,1,0:T(8,128)} %bitcast.33, s32[1,128]{1,0:T(1,128)} %counts_hbm, bf16[1,512,256]{2,1,0:T(8,128)(2,1)} %grid_hbm.1), custom_call_target="tpu_custom_call" | custom-call | flops 100000000 | bytes 266752 | tf_op jit(solution)/shard_map/pallas_call | solution.py:294
  3.2 39.0 %all_to_all.20 = bf16[128,8,256]{2,1,0:T(8,128)(2,1)S(1)} all-to-all(bf16[128,8,256]{2,1,0:T(8,128)(2,1)} %bitcast.32), channel_id=1, replica_groups=mesh['graph_0'=8,'graph_1'=8,'graph_2'=2,'sample'=4] {'graph_0','graph_1..., dimensions={0} | all-to-all | bytes 1048576 | tf_op jit(solution)/shard_map/all_to_all | solution.py:308
  42.2 0.0 copy-done.13
  42.3 0.0 copy-done.9
  42.3 0.0 copy-done.8
  42.3 0.0 copy-done.10
  42.3 0.0 copy-done
  42.3 0.0 copy-done.4
  42.3 0.0 copy-done.7
  42.3 0.0 copy-done.5
  42.3 0.0 copy-start.1
  42.3 0.0 copy-start.2
  42.3 0.0 copy-start.3
  42.3 0.0 copy-start.6
  42.4 0.0 copy-start.11
  42.4 0.0 copy-start.12
  42.4 3.2 %shard_map.185 = (bf16[128,512]{1,0:T(8,128)(2,1)S(1)}, bf16[1024,256]{1,0:T(8,128)(2,1)S(1)}) custom-call(bf16[1024,256]{1,0:T(8,128)(2,1)S(1)} %bitcast.23, s32[1,1024]{1,0:T(1,128)S(1)} %bitcast.26, s32[1,1024]{1,0:T(1,128)S(1)} %bitcast.27, bf16[4,1024]{1,0:T(4,128)(2,1)S(1)} %copy-done.7, bf16[256,512]{1,0:T(8,128)(2,1)S(1)} %copy-done.4, ...), custom_call_target="tpu_custom_call" | custom-call | flops 2000000000 | bytes 1464320 | tf_op jit(solution)/shard_map/pallas_call | solution.py:294
  45.6 25.8 %all_to_all.21 = bf16[128,8,256]{2,1,0:T(8,128)(2,1)S(1)} all-to-all(bf16[128,8,256]{2,1,0:T(8,128)(2,1)S(1)} %bitcast.24), channel_id=1, replica_groups=mesh['graph_0'=8,'graph_1'=8,'graph_2'=2,'sample'=4] {'graph_0','graph_1..., dimensions={0} | all-to-all | bytes 1048576 | tf_op jit(solution)/shard_map/all_to_all | solution.py:308
  71.4 0.0 copy-done.1
  71.4 0.0 copy-done.2
  71.4 0.0 copy-done.3
  71.4 0.0 copy-done.6
  71.4 0.0 copy-done.11
  71.4 0.0 copy-done.12
  71.4 3.8 %shard_map.186 = (bf16[1,128,512]{2,1,0:T(8,128)(2,1)}, bf16[1024,256]{1,0:T(8,128)(2,1)S(1)}, bf16[640,512]{1,0:T(8,128)(2,1)S(1)}, bf16[640,512]{1,0:T(8,128)(...) custom-call(s32[1]{0:T(128)S(6)} %sub.6.sibling_ref, ...), custom_call_target="tpu_custom_call" | custom-call | flops 3000000000 | bytes 2363396 | tf_op jit(solution)/shard_map/pallas_call | solution.py:294
  75.3 1.9 %collective-permute-start = (bf16[1536,256]{1,0:T(8,128)(2,1)S(1)}, bf16[1536,256]{1,0:T(8,128)(2,1)S(1)}, u32[]{:S(2)}, u32[]{:S(2)}) collective-permute-start(bf16[1536,256]{1,0:T(8,128)(2,1)S(1)} %get-tuple-element.31), channel_id=1, source_target_pairs={{0,4},{4,0},{1,5},{5,1},{2,6},{6,2},{3,7},{7,3},{8,12},{12,8},{9,1... | collective-permute-start | bytes 2359304 | tf_op jit(solution)/shard_map/ppermute | solution.py:317
  77.2 0.6 shard_map.187
  77.7 1.7 %collective-permute-done = bf16[1536,256]{1,0:T(8,128)(2,1)S(1)} collective-permute-done((bf16[1536,256]{1,0:T(8,128)(2,1)S(1)}, bf16[1536,256]{1,0:T(8,128)(2,1)S(1)}, u32[]{:S(2)}, u32[]{:S(2)}) %collective-permute-start) | collective-permute-done | bytes 786464 | tf_op jit(solution)/shard_map/ppermute | solution.py:317
  79.4 0.3 shard_map.188
  79.7 41.3 %all_to_all.22 = bf16[128,8,640]{2,1,0:T(8,128)(2,1)S(1)} all-to-all(bf16[128,8,640]{2,1,0:T(8,128)(2,1)S(1)} %bitcast.20), channel_id=1, replica_groups=mesh['graph_0'=8,'graph_1'=8,'graph_2'=2,'sample'=4] {'graph_0','graph_1..., dimensions={0} | all-to-all | bytes 2621440 | tf_op jit(solution)/shard_map/all_to_all | solution.py:308
  121.0 0.8 shard_map.190
  121.8 4.0 %all-to-all-start.3 = ((f32[4,2,8,384]{3,2,1,0:T(8,128)}), f32[4,2,8,384]{3,2,1,0:T(8,128)S(1)}, u32[]{:S(2)}, u32[]{:S(2)}) async-start(f32[4,2,8,384]{3,2,1,0:T(8,128)} %shard_map.190), calls=%async_computation.3 | async-start | bytes 196608 | tf_op jit(solution)/shard_map/all_to_all | solution.py:308
  125.8 1.6 %shard_map.189 = f32[1,128,512]{2,1,0:T(8,128)} custom-call(bf16[1024,640]{1,0:T(8,128)(2,1)S(1)} %bitcast.19, s32[1,4,128]{2,1,0:T(4,128)S(1)} %bitcast.31, bf16[640,512]{1,0:T(8,128)(2,1)S(1)} %get-tuple-element.27.send_grad_ref, bf16[128,512]{1,0:T(8,128)(2,1)S(1)} %get-tuple-element.28.recv_grad_ref, bf16[512,512]{1,0:T(8,128)(2,1)S(1)} %copy-done.2, ...), custom_call_target="tpu_custom_call" | custom-call | flops 1000000000 | bytes 3278848 | tf_op jit(solution)/shard_map/pallas_call | solution.py:294
  127.4 3.1 %all-to-all-done.3.arrived_ref = f32[4,2,8,384]{3,2,1,0:T(8,128)S(1)} async-done(((f32[4,2,8,384]{3,2,1,0:T(8,128)}), f32[4,2,8,384]{3,2,1,0:T(8,128)S(1)}, u32[]{:S(2)}, u32[]{:S(2)}) %all-to-all-start.3) | async-done | bytes 98336 | tf_op jit(solution)/shard_map/all_to_all | solution.py:308
  130.4 0.6 shard_map.191
Async XLA Ops:
  0.6 41.6 %copy-start.13 = (s32[1,128,4]{1,2,0:T(4,128)S(1)}, s32[1,128,4]{1,2,0:T(4,128)}, u32[]{:S(2)}) copy-start(s32[1,128,4]{1,2,0:T(4,128)} %param.31) | copy-start | bytes 6148
  0.6 41.6 %copy-start.9 = (s32[1024]{0:T(1024)S(1)}, s32[1024]{0:T(1024)}, u32[]{:S(2)}) copy-start(s32[1024]{0:T(1024)} %param.30) | copy-start | bytes 12292
  0.7 41.6 %copy-start.8 = (s32[1024]{0:T(1024)S(1)}, s32[1024]{0:T(1024)}, u32[]{:S(2)}) copy-start(s32[1024]{0:T(1024)} %param.29) | copy-start | bytes 12292
  0.7 41.6 %copy-start.10 = (bf16[4,512]{1,0:T(4,128)(2,1)S(1)}, bf16[4,512]{1,0:T(4,128)(2,1)}, u32[]{:S(2)}) copy-start(bf16[4,512]{1,0:T(4,128)(2,1)} %w_geo_ref.1) | copy-start | bytes 12292
  0.7 41.6 %copy-start = (bf16[512,512]{1,0:T(8,128)(2,1)S(1)}, bf16[512,512]{1,0:T(8,128)(2,1)}, u32[]{:S(2)}) copy-start(bf16[512,512]{1,0:T(8,128)(2,1)} %w_g2m_ref.1) | copy-start | bytes 1572868
  0.7 41.6 %copy-start.4 = (bf16[256,512]{1,0:T(8,128)(2,1)S(1)}, bf16[256,512]{1,0:T(8,128)(2,1)}, u32[]{:S(2)}) copy-start(bf16[256,512]{1,0:T(8,128)(2,1)} %w_embed_ref.1) | copy-start | bytes 786436
  0.7 41.6 %copy-start.7 = (bf16[4,1024]{1,0:T(4,128)(2,1)S(1)}, bf16[4,1024]{1,0:T(4,128)(2,1)}, u32[]{:S(2)}) copy-start(bf16[4,1024]{1,0:T(4,128)(2,1)} %geometry_ref.1) | copy-start | bytes 24580
  0.7 41.6 %copy-start.5 = (bf16[1,128,512]{2,1,0:T(8,128)(2,1)S(1)}, bf16[1,128,512]{2,1,0:T(8,128)(2,1)}, u32[]{:S(2)}) copy-start(bf16[1,128,512]{2,1,0:T(8,128)(2,1)} %init_ref.1) | copy-start | bytes 393220
  42.3 29.1 %copy-start.1 = (bf16[512,512]{1,0:T(8,128)(2,1)S(1)}, bf16[512,512]{1,0:T(8,128)(2,1)}, u32[]{:S(2)}) copy-start(bf16[512,512]{1,0:T(8,128)(2,1)} %b_node_ref.1) | copy-start | bytes 1572868
  42.3 29.1 %copy-start.2 = (bf16[512,512]{1,0:T(8,128)(2,1)S(1)}, bf16[512,512]{1,0:T(8,128)(2,1)}, u32[]{:S(2)}) copy-start(bf16[512,512]{1,0:T(8,128)(2,1)} %a_send_ref.3) | copy-start | bytes 1572868
  42.3 29.1 %copy-start.3 = (bf16[512,512]{1,0:T(8,128)(2,1)S(1)}, bf16[512,512]{1,0:T(8,128)(2,1)}, u32[]{:S(2)}) copy-start(bf16[512,512]{1,0:T(8,128)(2,1)} %a_recv_ref.3) | copy-start | bytes 1572868
  42.3 29.1 %copy-start.6 = (bf16[1,128,512]{2,1,0:T(8,128)(2,1)S(1)}, bf16[1,128,512]{2,1,0:T(8,128)(2,1)}, u32[]{:S(2)}) copy-start(bf16[1,128,512]{2,1,0:T(8,128)(2,1)} %cot_ref.3) | copy-start | bytes 393220
  42.4 29.1 %copy-start.11 = (s32[512]{0:T(512)S(1)}, s32[512]{0:T(512)}, u32[]{:S(2)}) copy-start(s32[512]{0:T(512)} %param.32) | copy-start | bytes 6148
  42.4 29.1 %copy-start.12 = (s32[512]{0:T(512)S(1)}, s32[512]{0:T(512)}, u32[]{:S(2)}) copy-start(s32[512]{0:T(512)} %param.33) | copy-start | bytes 6148
  75.3 4.2 %collective-permute-start = (bf16[1536,256]{1,0:T(8,128)(2,1)S(1)}, bf16[1536,256]{1,0:T(8,128)(2,1)S(1)}, u32[]{:S(2)}, u32[]{:S(2)}) collective-permute-start(bf16[1536,256]{1,0:T(8,128)(2,1)S(1)} %get-tuple-element.31), channel_id=1, source_target_pairs={{0,4},{4,0},{1,5},{5,1},{2,6},{6,2},{3,7},{7,3},{8,12},{12,8},{9,1... | collective-permute-start | bytes 2359304 | tf_op jit(solution)/shard_map/ppermute | solution.py:317
  121.8 8.7 %all-to-all-start.3 = ((f32[4,2,8,384]{3,2,1,0:T(8,128)}), f32[4,2,8,384]{3,2,1,0:T(8,128)S(1)}, u32[]{:S(2)}, u32[]{:S(2)}) async-start(f32[4,2,8,384]{3,2,1,0:T(8,128)} %shard_map.190), calls=%async_computation.3 | async-start | bytes 196608 | tf_op jit(solution)/shard_map/all_to_all | solution.py:308

commit v6 on v5

--- a/solution.py
+++ b/solution.py
@@ -206,6 +206,23 @@
     )
 
 
+def keep_grads(
+    sibling_ref, table_ref, send_grad_ref, latent_ref, recv_grad_ref, aggregate_ref, d_update_ref,
+    a_send_ref, a_recv_ref, cot_ref, keep_ref, local_ref,
+):
+    weight_grads(
+        True, sibling_ref, table_ref, send_grad_ref, latent_ref, recv_grad_ref, aggregate_ref,
+        d_update_ref, keep_ref,
+    )
+    nodes = latent_ref.shape[0]
+    own_rows = send_grad_ref[send_grad_ref.shape[0] - nodes :, :]
+    local_ref[...] = (
+        cot_ref[0].astype(F32)
+        + times_transposed(recv_grad_ref[...], a_recv_ref[...])
+        + times_transposed(own_rows, a_send_ref[...])
+    )
+
+
 def pack(keep_ref, other_ref, back_ref, out_ref):
     chips, _, half = keep_ref.shape
     tile = back_ref.shape[2]
@@ -257,27 +274,27 @@
         out_ref[extra:, :] = whole
 
 
-def return_grads(
-    back_ref, send_rows_ref, send_grad_ref, recv_grad_ref, a_send_ref, a_recv_ref, cot_ref,
-    out_ref, spread,
-):
-    nodes = recv_grad_ref.shape[0]
+def return_grads(back_ref, send_rows_ref, a_send_ref, local_ref, out_ref, spread):
+    nodes = local_ref.shape[0]
     slots, groups = send_rows_ref.shape[1:]
     scatter_blocks(spread, back_ref)
     wanted = send_rows_ref[0]
     arrived = [split_load(spread, j, slots, groups).astype(BF16) for j in range(slots)]
     chosen = [select_columns(wanted[j : j + 1], nodes) for j in range(slots)]
     total = dot(jnp.concatenate(chosen, axis=1), jnp.concatenate(arrived, axis=0))
-    total = total + send_grad_ref[slots * groups :, :].astype(F32)
     high = total.astype(BF16)
     rest = total - high.astype(F32)
     low = rest.astype(BF16)
     a_send = a_send_ref[...]
-    out_ref[0] = (
-        cot_ref[0].astype(F32)
-        + times_transposed(recv_grad_ref[...], a_recv_ref[...])
-        + (times_transposed(high, a_send) + times_transposed(low, a_send))
-    )
+    out_ref[0] = local_ref[...] + (times_transposed(high, a_send) + times_transposed(low, a_send))
+
+
+def finish(
+    sibling_ref, copies_ref, back_ref, send_rows_ref, a_send_ref, local_ref, weights_ref, mesh_ref,
+    spread,
+):
+    add_samples(sibling_ref, copies_ref, weights_ref)
+    return_grads(back_ref, send_rows_ref, a_send_ref, local_ref, mesh_ref, spread)
 
 
 def shape(dims, dtype):
@@ -321,16 +338,12 @@
         back.reshape(chips, 2, tile, half),
     )
     arrived = exchange(packed.reshape(2 * chips, tile, lanes), GRAPH)
-    arrived, core = lax.optimization_barrier((arrived, core))
     copies = kernel(add_chips, shape((samples, 2, tile, lanes - half), F32), [], 10**7)(
         arrived.reshape(chips, 2, tile, lanes)
     )
     copies = exchange(copies, "sample")
-    rows = keep.shape[0] // (2 * chips)
-    grad_weights = kernel(add_samples, shape((rows, 2 * half), F32), [], 10**6, 1, pltpu.SMEM)(
-        1 - core, copies
-    )
-    return arrived.reshape(2 * chips * tile, lanes), grad_weights
+    copies, core = lax.optimization_barrier((copies, core))
+    return arrived.reshape(2 * chips * tile, lanes), copies, 1 - core
 
 
 def on_device(
@@ -433,23 +446,23 @@
     )
 
     operands = (table, send_grad, latent, recv_grad, aggregate, d_update)
-    keep = kernel(functools.partial(weight_grads, True), shape((3 * width, half), F32), [], 5 * 10**8, 1, pltpu.SMEM)(sibling, *operands)
-    arrived, grad_weights = share(keep, send, back, core)
-
-    grad_mesh = kernel(
-        return_grads,
-        shape((1, nodes, width), F32),
+    keep, local = kernel(
+        keep_grads,
+        (shape((3 * width, half), F32), shape((nodes, width), F32)),
+        [],
+        7 * 10**8,
+        1,
+        pltpu.SMEM,
+    )(sibling, *operands, a_send, a_recv, cotangent)
+    arrived, copies, sibling = share(keep, send, back, core)
+    grad_weights, grad_mesh = kernel(
+        finish,
+        (shape((3 * width // groups, width), F32), shape((1, nodes, width), F32)),
         [pltpu.VMEM((half // LANES, halves, LANES), F32)],
         10**9,
-    )(
-        arrived,
-        mesh_rows,
-        send_grad,
-        recv_grad,
-        a_send,
-        a_recv,
-        cotangent,
-    )
+        1,
+        pltpu.SMEM,
+    )(sibling, copies, arrived, mesh_rows, a_send, local)
     return (mesh_out, grad_mesh, grad_weights)
 
 

time: 133 us -> 133 us (level)
  blocking collectives: 106 us -> 115 us
  starting transfers between devices: 5.91 us -> 1.91 us
  waiting for transfers between devices: 4.76 us -> 1.45 us
    all_to_all x3 -> x4, blocking collectives: 106 us -> 115 us  [exchange(): return lax.all_to_all(x, axis, split_axis=0, concat_axis=0, tiled=True)]
    all_to_all x1 -> x0, starting transfers between devices: 4 us -> none  [exchange(): return lax.all_to_all(x, axis, split_axis=0, concat_axis=0, tiled=True)]
    all_to_all x1 -> x0, waiting for transfers between devices: 3.07 us -> none  [exchange(): return lax.all_to_all(x, axis, split_axis=0, concat_axis=0, tiled=True)]
    pallas_call x8 -> x7, Pallas kernels: 13.4 us -> 12.2 us  [call(): pl.pallas_call(body, out_shape=outs, in_specs=specs, out_specs=jax.tree.m...]
  transfers between devices with their start and end apart: 2 -> 1, of which waited for: 2 -> 1; matrix products, arithmetic and copies ran while one was open for 0% -> 0% of each run, Pallas kernels for 2% -> 1%
where the time goes in v6:
time: 133 us; the launch traced here: 131 us
  blocking collectives  115 us (86%)
  Pallas kernels  12.2 us (9%)
  starting transfers between devices  1.91 us (1%)
  waiting for transfers between devices  1.45 us (1%)
    all_to_all x4, blocking collectives, exchange(): return lax.all_to_all(x, axis, split_axis=0, concat_axis=0, tiled=True)  115 us
    pallas_call x7, Pallas kernels, call(): pl.pallas_call(body, out_shape=outs, in_specs=specs, out_specs=jax.tree.m...  12.2 us
  transfers between devices with their start and end apart: 1, of which 1 were waited for; matrix products, arithmetic and copies ran while one was open for 0% of the time, Pallas kernels for 1%

profile of v6, /device:TPU:1, one launch (start us, length us, event | category | flops | bytes accessed | tf_op | source)
XLA Modules:
  0.0 131.1 jit_solution(7359628289292722381)
XLA Ops:
  0.6 0.0 copy-start.13
  0.6 0.0 copy-start.9
  0.7 0.0 copy-start.8
  0.7 0.0 copy-start.10
  0.7 0.0 copy-start.3
  0.7 0.0 copy-start.5
  0.7 0.0 copy-start.7
  0.7 0.0 copy-start.6
  0.7 2.5 %shard_map.184 = bf16[1024,256]{1,0:T(8,128)(2,1)} custom-call(s32[1,8,128]{2,1,0:T(8,128)} %bitcast.33, s32[1,128]{1,0:T(1,128)} %counts_hbm, bf16[1,512,256]{2,1,0:T(8,128)(2,1)} %grid_hbm.1), custom_call_target="tpu_custom_call" | custom-call | flops 100000000 | bytes 266752 | tf_op jit(solution)/shard_map/pallas_call | solution.py:311
  3.2 39.0 %all_to_all.20 = bf16[128,8,256]{2,1,0:T(8,128)(2,1)S(1)} all-to-all(bf16[128,8,256]{2,1,0:T(8,128)(2,1)} %bitcast.32), channel_id=1, replica_groups=mesh['graph_0'=8,'graph_1'=8,'graph_2'=2,'sample'=4] {'graph_0','graph_1..., dimensions={0} | all-to-all | bytes 1048576 | tf_op jit(solution)/shard_map/all_to_all | solution.py:325
  42.2 0.0 copy-done.13
  42.3 0.0 copy-done.9
  42.3 0.0 copy-done.8
  42.3 0.0 copy-done.10
  42.3 0.0 copy-done.3
  42.3 0.0 copy-done.5
  42.3 0.0 copy-done.7
  42.3 0.0 copy-done.6
  42.3 0.0 copy-start
  42.3 0.0 copy-start.1
  42.3 0.0 copy-start.2
  42.3 0.0 copy-start.4
  42.4 0.0 copy-start.11
  42.4 0.0 copy-start.12
  42.4 3.2 %shard_map.185 = (bf16[128,512]{1,0:T(8,128)(2,1)S(1)}, bf16[1024,256]{1,0:T(8,128)(2,1)S(1)}) custom-call(bf16[1024,256]{1,0:T(8,128)(2,1)S(1)} %bitcast.23, s32[1,1024]{1,0:T(1,128)S(1)} %bitcast.26, s32[1,1024]{1,0:T(1,128)S(1)} %bitcast.27, bf16[4,1024]{1,0:T(4,128)(2,1)S(1)} %copy-done.7, bf16[256,512]{1,0:T(8,128)(2,1)S(1)} %copy-done.5, ...), custom_call_target="tpu_custom_call" | custom-call | flops 2000000000 | bytes 1464320 | tf_op jit(solution)/shard_map/pallas_call | solution.py:311
  45.6 25.8 %all_to_all.21 = bf16[128,8,256]{2,1,0:T(8,128)(2,1)S(1)} all-to-all(bf16[128,8,256]{2,1,0:T(8,128)(2,1)S(1)} %bitcast.24), channel_id=1, replica_groups=mesh['graph_0'=8,'graph_1'=8,'graph_2'=2,'sample'=4] {'graph_0','graph_1..., dimensions={0} | all-to-all | bytes 1048576 | tf_op jit(solution)/shard_map/all_to_all | solution.py:325
  71.4 0.0 copy-done
  71.4 0.0 copy-done.1
  71.4 0.0 copy-done.2
  71.4 0.0 copy-done.4
  71.4 0.0 copy-done.11
  71.4 0.0 copy-done.12
  71.4 3.8 %shard_map.186 = (bf16[1,128,512]{2,1,0:T(8,128)(2,1)}, bf16[1024,256]{1,0:T(8,128)(2,1)S(1)}, bf16[640,512]{1,0:T(8,128)(2,1)S(1)}, bf16[640,512]{1,0:T(8,128)(...) custom-call(s32[1]{0:T(128)S(6)} %sub.6.sibling_ref, ...), custom_call_target="tpu_custom_call" | custom-call | flops 3000000000 | bytes 2363396 | tf_op jit(solution)/shard_map/pallas_call | solution.py:311
  75.3 1.9 %collective-permute-start = (bf16[1536,256]{1,0:T(8,128)(2,1)S(1)}, bf16[1536,256]{1,0:T(8,128)(2,1)S(1)}, u32[]{:S(2)}, u32[]{:S(2)}) collective-permute-start(bf16[1536,256]{1,0:T(8,128)(2,1)S(1)} %get-tuple-element.36), channel_id=1, source_target_pairs={{0,4},{4,0},{1,5},{5,1},{2,6},{6,2},{3,7},{7,3},{8,12},{12,8},{9,1... | collective-permute-start | bytes 2359304 | tf_op jit(solution)/shard_map/ppermute | solution.py:334
  77.2 0.8 shard_map.187
  78.0 1.4 %collective-permute-done = bf16[1536,256]{1,0:T(8,128)(2,1)S(1)} collective-permute-done((bf16[1536,256]{1,0:T(8,128)(2,1)S(1)}, bf16[1536,256]{1,0:T(8,128)(2,1)S(1)}, u32[]{:S(2)}, u32[]{:S(2)}) %collective-permute-start) | collective-permute-done | bytes 786464 | tf_op jit(solution)/shard_map/ppermute | solution.py:334
  79.4 0.3 shard_map.188
  79.7 41.3 %all_to_all.22 = bf16[128,8,640]{2,1,0:T(8,128)(2,1)S(1)} all-to-all(bf16[128,8,640]{2,1,0:T(8,128)(2,1)S(1)} %bitcast.19), channel_id=1, replica_groups=mesh['graph_0'=8,'graph_1'=8,'graph_2'=2,'sample'=4] {'graph_0','graph_1..., dimensions={0} | all-to-all | bytes 2621440 | tf_op jit(solution)/shard_map/all_to_all | solution.py:325
  121.0 0.1 shard_map.189
  121.1 8.4 %all_to_all.23.copies_ref = f32[4,2,8,384]{3,2,1,0:T(8,128)S(1)} all-to-all(f32[4,2,8,384]{3,2,1,0:T(8,128)S(1)} %shard_map.189), channel_id=1, replica_groups=mesh['graph_0'=8,'graph_1'=8,'graph_2'=2,'sample'=4] {'sample'}, dimensions={0} | all-to-all | bytes 196608 | tf_op jit(solution)/shard_map/all_to_all | solution.py:325
  129.6 1.5 %shard_map.190 = (f32[12,512]{1,0:T(8,128)}, f32[1,128,512]{2,1,0:T(8,128)}) custom-call(s32[1]{0:T(128)S(6)} %sub.7.sibling_ref, f32[4,2,8,384]{3,2,1,0:T(8,128)S(1)} %all_to_all.23.copies_ref, bf16[1024,640]{1,0:T(8,128)(2,1)S(1)} %bitcast.18, s32[1,4,128]{2,1,0:T(4,128)S(1)} %bitcast.31, bf16[512,512]{1,0:T(8,128)(2,1)S(1)} %copy-done.1, ...), custom_call_target="tpu_custom_call" | custom-call | flops 1000000000 | bytes 2197508 | tf_op jit(solution)/shard_map/pallas_call | solution.py:311
Async XLA Ops:
  0.6 41.6 %copy-start.13 = (s32[1,128,4]{1,2,0:T(4,128)S(1)}, s32[1,128,4]{1,2,0:T(4,128)}, u32[]{:S(2)}) copy-start(s32[1,128,4]{1,2,0:T(4,128)} %param.31) | copy-start | bytes 6148
  0.6 41.6 %copy-start.9 = (s32[1024]{0:T(1024)S(1)}, s32[1024]{0:T(1024)}, u32[]{:S(2)}) copy-start(s32[1024]{0:T(1024)} %param.30) | copy-start | bytes 12292
  0.7 41.6 %copy-start.8 = (s32[1024]{0:T(1024)S(1)}, s32[1024]{0:T(1024)}, u32[]{:S(2)}) copy-start(s32[1024]{0:T(1024)} %param.29) | copy-start | bytes 12292
  0.7 41.6 %copy-start.10 = (bf16[4,512]{1,0:T(4,128)(2,1)S(1)}, bf16[4,512]{1,0:T(4,128)(2,1)}, u32[]{:S(2)}) copy-start(bf16[4,512]{1,0:T(4,128)(2,1)} %w_geo_ref.1) | copy-start | bytes 12292
  0.7 41.6 %copy-start.3 = (bf16[512,512]{1,0:T(8,128)(2,1)S(1)}, bf16[512,512]{1,0:T(8,128)(2,1)}, u32[]{:S(2)}) copy-start(bf16[512,512]{1,0:T(8,128)(2,1)} %w_g2m_ref.1) | copy-start | bytes 1572868
  0.7 41.6 %copy-start.5 = (bf16[256,512]{1,0:T(8,128)(2,1)S(1)}, bf16[256,512]{1,0:T(8,128)(2,1)}, u32[]{:S(2)}) copy-start(bf16[256,512]{1,0:T(8,128)(2,1)} %w_embed_ref.1) | copy-start | bytes 786436
  0.7 41.6 %copy-start.7 = (bf16[4,1024]{1,0:T(4,128)(2,1)S(1)}, bf16[4,1024]{1,0:T(4,128)(2,1)}, u32[]{:S(2)}) copy-start(bf16[4,1024]{1,0:T(4,128)(2,1)} %geometry_ref.1) | copy-start | bytes 24580
  0.7 41.6 %copy-start.6 = (bf16[1,128,512]{2,1,0:T(8,128)(2,1)S(1)}, bf16[1,128,512]{2,1,0:T(8,128)(2,1)}, u32[]{:S(2)}) copy-start(bf16[1,128,512]{2,1,0:T(8,128)(2,1)} %init_ref.1) | copy-start | bytes 393220
  42.3 29.1 %copy-start = (bf16[512,512]{1,0:T(8,128)(2,1)S(1)}, bf16[512,512]{1,0:T(8,128)(2,1)}, u32[]{:S(2)}) copy-start(bf16[512,512]{1,0:T(8,128)(2,1)} %a_recv_ref.3) | copy-start | bytes 1572868
  42.3 29.1 %copy-start.1 = (bf16[512,512]{1,0:T(8,128)(2,1)S(1)}, bf16[512,512]{1,0:T(8,128)(2,1)}, u32[]{:S(2)}) copy-start(bf16[512,512]{1,0:T(8,128)(2,1)} %a_send_ref.5) | copy-start | bytes 1572868
  42.3 29.1 %copy-start.2 = (bf16[1,128,512]{2,1,0:T(8,128)(2,1)S(1)}, bf16[1,128,512]{2,1,0:T(8,128)(2,1)}, u32[]{:S(2)}) copy-start(bf16[1,128,512]{2,1,0:T(8,128)(2,1)} %cot_ref.3) | copy-start | bytes 393220
  42.3 29.1 %copy-start.4 = (bf16[512,512]{1,0:T(8,128)(2,1)S(1)}, bf16[512,512]{1,0:T(8,128)(2,1)}, u32[]{:S(2)}) copy-start(bf16[512,512]{1,0:T(8,128)(2,1)} %b_node_ref.1) | copy-start | bytes 1572868
  42.4 29.1 %copy-start.11 = (s32[512]{0:T(512)S(1)}, s32[512]{0:T(512)}, u32[]{:S(2)}) copy-start(s32[512]{0:T(512)} %param.32) | copy-start | bytes 6148
  42.4 29.1 %copy-start.12 = (s32[512]{0:T(512)S(1)}, s32[512]{0:T(512)}, u32[]{:S(2)}) copy-start(s32[512]{0:T(512)} %param.33) | copy-start | bytes 6148
  75.3 4.2 %collective-permute-start = (bf16[1536,256]{1,0:T(8,128)(2,1)S(1)}, bf16[1536,256]{1,0:T(8,128)(2,1)S(1)}, u32[]{:S(2)}, u32[]{:S(2)}) collective-permute-start(bf16[1536,256]{1,0:T(8,128)(2,1)S(1)} %get-tuple-element.36), channel_id=1, source_target_pairs={{0,4},{4,0},{1,5},{5,1},{2,6},{6,2},{3,7},{7,3},{8,12},{12,8},{9,1... | collective-permute-start | bytes 2359304 | tf_op jit(solution)/shard_map/ppermute | solution.py:334

commit v7 on v6

--- a/solution.py
+++ b/solution.py
@@ -224,60 +224,64 @@
 
 
 def pack(keep_ref, other_ref, back_ref, out_ref):
-    chips, _, half = keep_ref.shape
+    half = keep_ref.shape[2]
     tile = back_ref.shape[2]
-    out_ref[:, :, :, :half] = back_ref[...]
+    for i in range(2):
+        out_ref[:, :, i * half : (i + 1) * half] = back_ref[:, i]
     for i in range(3):
         rows = slice(i * tile, (i + 1) * tile)
         total = keep_ref[:, rows, :] + other_ref[:, rows, :].astype(F32)
-        if i != 1:
-            out_ref[:, i // 2, :, half : 2 * half] = total.astype(BF16)
-            continue
-        flat = total.reshape(chips * tile, half)
-        left, right = flat[:, :LANES], flat[:, LANES:]
-        upper = lax.rem(lax.broadcasted_iota(jnp.int32, left.shape, 0), tile) < tile // 2
-        first = jnp.where(upper, left, pltpu.roll(right, tile // 2, 0))
-        second = jnp.where(upper, pltpu.roll(left, chips * tile - tile // 2, 0), right)
-        out_ref[:, 0, :, 2 * half :] = first.astype(BF16).reshape(chips, tile, LANES)
-        out_ref[:, 1, :, 2 * half :] = second.astype(BF16).reshape(chips, tile, LANES)
-
-
-def add_chips(arrived_ref, out_ref):
-    chips = arrived_ref.shape[0]
-    skip = arrived_ref.shape[3] - out_ref.shape[3]
-    total = arrived_ref[0, :, :, skip:].astype(F32)
-    for i in range(1, chips):
-        total = total + arrived_ref[i, :, :, skip:].astype(F32)
-    for i in range(out_ref.shape[0]):
-        out_ref[i] = total
+        out_ref[:, :, (2 + i) * half : (3 + i) * half] = total.astype(BF16)
+
+
+def add_chips(sibling_ref, arrived_ref, copies_ref, theirs_ref):
+    samples, _, rows, half = copies_ref.shape
+    tile = rows // 2
+    columns = pl.ds(pl.multiple_of(sibling_ref[0] * half, half), half)
+    theirs_ref[...] = arrived_ref[:, columns]
+    total = arrived_ref[:tile, 2 * half :].astype(F32)
+    for i in range(1, arrived_ref.shape[0] // tile):
+        total = total + arrived_ref[i * tile : (i + 1) * tile, 2 * half :].astype(F32)
+    tiles = [total[:, i * half : (i + 1) * half] for i in range(3)]
+    for i in range(samples):
+        for core in range(2):
+            copies_ref[i, core, :tile, :] = tiles[core]
+            copies_ref[i, core, tile:, :] = tiles[core + 1]
 
 
 def add_samples(sibling_ref, arrived_ref, out_ref):
     total = arrived_ref[0]
     for i in range(1, arrived_ref.shape[0]):
         total = total + arrived_ref[i]
-    tile = total.shape[1]
-    half = out_ref.shape[1] // 2
-    extra = tile // 2
-    whole = jnp.concatenate([total[h, :, :half] for h in range(2)], axis=1)
-    parts = [total[h, k * extra : (k + 1) * extra, half:] for h in range(2) for k in range(2)]
-    middle = jnp.concatenate(parts, axis=1)
+    whole = jnp.concatenate([total[0], total[1]], axis=1)
+    rows = out_ref.shape[0]
 
     @pl.when(sibling_ref[0] == 1)
     def _():
-        out_ref[:tile, :] = whole
-        out_ref[tile:, :] = middle
+        out_ref[...] = whole[:rows]
 
     @pl.when(sibling_ref[0] == 0)
     def _():
-        out_ref[:extra, :] = middle
-        out_ref[extra:, :] = whole
-
-
-def return_grads(back_ref, send_rows_ref, a_send_ref, local_ref, out_ref, spread):
+        out_ref[...] = whole[whole.shape[0] - rows :]
+
+
+def interleave(sibling_ref, arrived_ref, other_ref, spread):
+    half = other_ref.shape[1]
+    tile = 8
+    columns = pl.ds(pl.multiple_of((1 - sibling_ref[0]) * half, half), half)
+    mine = arrived_ref[:, columns].astype(F32)
+    other = other_ref[...].astype(F32)
+    first = sibling_ref[0] == 1
+    pair = jnp.where(first, mine, other), jnp.where(first, other, mine)
+    for k in range(spread.shape[0]):
+        lanes = slice(k * LANES, (k + 1) * LANES)
+        parts = [part[:, lanes].reshape(-1, 1, tile, LANES) for part in pair]
+        spread[k] = jnp.concatenate(parts, axis=1).reshape(-1, LANES)
+
+
+def return_grads(send_rows_ref, a_send_ref, local_ref, out_ref, spread):
     nodes = local_ref.shape[0]
     slots, groups = send_rows_ref.shape[1:]
-    scatter_blocks(spread, back_ref)
     wanted = send_rows_ref[0]
     arrived = [split_load(spread, j, slots, groups).astype(BF16) for j in range(slots)]
     chosen = [select_columns(wanted[j : j + 1], nodes) for j in range(slots)]
@@ -290,11 +294,12 @@
 
 
 def finish(
-    sibling_ref, copies_ref, back_ref, send_rows_ref, a_send_ref, local_ref, weights_ref, mesh_ref,
-    spread,
+    sibling_ref, copies_ref, arrived_ref, other_ref, send_rows_ref, a_send_ref, local_ref,
+    weights_ref, mesh_ref, spread,
 ):
     add_samples(sibling_ref, copies_ref, weights_ref)
-    return_grads(back_ref, send_rows_ref, a_send_ref, local_ref, mesh_ref, spread)
+    interleave(sibling_ref, arrived_ref, other_ref, spread)
+    return_grads(send_rows_ref, a_send_ref, local_ref, mesh_ref, spread)
 
 
 def shape(dims, dtype):
@@ -330,20 +335,27 @@
     tile = 8
     chips = lax.axis_size("graph_0") * lax.axis_size("graph_1")
     samples = lax.axis_size("sample")
-    lanes = 2 * half + half // 2
-    other = lax.ppermute(send, "graph_2", [(0, 1), (1, 0)])
-    packed = kernel(pack, shape((chips, 2, tile, lanes), BF16), [], 10**7)(
+    swap = [(0, 1), (1, 0)]
+    other = lax.ppermute(send, "graph_2", swap)
+    packed = kernel(pack, shape((chips, tile, 5 * half), BF16), [], 10**7)(
         keep.reshape(chips, -1, half),
         other.reshape(chips, -1, half),
         back.reshape(chips, 2, tile, half),
     )
-    arrived = exchange(packed.reshape(2 * chips, tile, lanes), GRAPH)
-    copies = kernel(add_chips, shape((samples, 2, tile, lanes - half), F32), [], 10**7)(
-        arrived.reshape(chips, 2, tile, lanes)
-    )
-    copies = exchange(copies, "sample")
-    copies, core = lax.optimization_barrier((copies, core))
-    return arrived.reshape(2 * chips * tile, lanes), copies, 1 - core
+    arrived = exchange(packed, ("graph_0", "graph_1"))
+    arrived, core = lax.optimization_barrier((arrived.reshape(chips * tile, 5 * half), core))
+    sibling = 1 - core
+    copies, theirs = kernel(
+        add_chips,
+        (shape((samples, 2, 2 * tile, half), F32), shape((chips * tile, half), BF16)),
+        [],
+        10**7,
+        1,
+        pltpu.SMEM,
+    )(sibling, arrived)
+    theirs = lax.ppermute(theirs, "graph_2", swap)
+    copies = exchange(copies.reshape(2 * samples, 2 * tile, half), ("sample", "graph_2"))
+    return arrived, theirs, copies.reshape(samples, 2, 2 * tile, half), sibling
 
 
 def on_device(
@@ -454,7 +466,7 @@
         1,
         pltpu.SMEM,
     )(sibling, *operands, a_send, a_recv, cotangent)
-    arrived, copies, sibling = share(keep, send, back, core)
+    arrived, theirs, copies, sibling = share(keep, send, back, core)
     grad_weights, grad_mesh = kernel(
         finish,
         (shape((3 * width // groups, width), F32), shape((1, nodes, width), F32)),
@@ -462,7 +474,7 @@
         10**9,
         1,
         pltpu.SMEM,
-    )(sibling, copies, arrived, mesh_rows, a_send, local)
+    )(sibling, copies, arrived, theirs, mesh_rows, a_send, local)
     return (mesh_out, grad_mesh, grad_weights)
 
 

time: 133 us -> 134 us (level); the launches traced: 131 us -> 133 us
  starting transfers between devices: 1.91 us -> 7.13 us
  blocking collectives: 115 us -> 112 us
    ppermute x1 -> x2, starting transfers between devices: 1.91 us -> 7.13 us  [the longest x1 5.22 us: share(): theirs = lax.ppermute(theirs, 'graph_2', swap)]
    all_to_all x4, blocking collectives: 115 us -> 112 us  [exchange(): return lax.all_to_all(x, axis, split_axis=0, concat_axis=0, tiled=True)]
  transfers between devices with their start and end apart: 1 -> 2, of which waited for: 1 -> 1; matrix products, arithmetic and copies ran while one was open for 0% -> 0% of each run, Pallas kernels for 1% -> 1%
where the time goes in v7:
time: 134 us; the launch traced here: 133 us
  blocking collectives  112 us (84%)
  Pallas kernels  12.2 us (9%)
  starting transfers between devices  7.13 us (5%)
  waiting for transfers between devices  1.45 us (1%)
    all_to_all x4, blocking collectives, exchange(): return lax.all_to_all(x, axis, split_axis=0, concat_axis=0, tiled=True)  112 us
    pallas_call x7, Pallas kernels, call(): pl.pallas_call(body, out_shape=outs, in_specs=specs, out_specs=jax.tree.m...  12.2 us
    ppermute x1, starting transfers between devices, share(): theirs = lax.ppermute(theirs, 'graph_2', swap)  5.22 us
  transfers between devices with their start and end apart: 2, of which 1 were waited for; matrix products, arithmetic and copies ran while one was open for 0% of the time, Pallas kernels for 1%

profile of v7, /device:TPU:1, one launch (start us, length us, event | category | flops | bytes accessed | tf_op | source)
XLA Modules:
  0.0 133.5 jit_solution(3671205373188705102)
XLA Ops:
  0.6 0.0 copy-start.13
  0.6 0.0 copy-start.9
  0.7 0.0 copy-start.8
  0.7 0.0 copy-start.10
  0.7 0.0 copy-start.3
  0.7 0.0 copy-start.5
  0.7 0.0 copy-start.7
  0.7 0.0 copy-start.6
  0.7 2.5 %shard_map.184 = bf16[1024,256]{1,0:T(8,128)(2,1)} custom-call(s32[1,8,128]{2,1,0:T(8,128)} %bitcast.34, s32[1,128]{1,0:T(1,128)} %counts_hbm, bf16[1,512,256]{2,1,0:T(8,128)(2,1)} %grid_hbm.1), custom_call_target="tpu_custom_call" | custom-call | flops 100000000 | bytes 266752 | tf_op jit(solution)/shard_map/pallas_call | solution.py:316
  3.2 39.0 %all_to_all.20 = bf16[128,8,256]{2,1,0:T(8,128)(2,1)S(1)} all-to-all(bf16[128,8,256]{2,1,0:T(8,128)(2,1)} %bitcast.33), channel_id=1, replica_groups=mesh['graph_0'=8,'graph_1'=8,'graph_2'=2,'sample'=4] {'graph_0','graph_1..., dimensions={0} | all-to-all | bytes 1048576 | tf_op jit(solution)/shard_map/all_to_all | solution.py:330
  42.2 0.0 copy-done.13
  42.2 0.0 copy-done.9
  42.2 0.0 copy-done.8
  42.2 0.0 copy-done.10
  42.3 0.0 copy-done.3
  42.3 0.0 copy-done.5
  42.3 0.0 copy-done.7
  42.3 0.0 copy-done.6
  42.3 0.0 copy-start
  42.3 0.0 copy-start.1
  42.3 0.0 copy-start.2
  42.3 0.0 copy-start.4
  42.3 0.0 copy-start.11
  42.4 0.0 copy-start.12
  42.4 3.2 %shard_map.185 = (bf16[128,512]{1,0:T(8,128)(2,1)S(1)}, bf16[1024,256]{1,0:T(8,128)(2,1)S(1)}) custom-call(bf16[1024,256]{1,0:T(8,128)(2,1)S(1)} %bitcast.22, s32[1,1024]{1,0:T(1,128)S(1)} %bitcast.27, s32[1,1024]{1,0:T(1,128)S(1)} %bitcast.28, bf16[4,1024]{1,0:T(4,128)(2,1)S(1)} %copy-done.7, bf16[256,512]{1,0:T(8,128)(2,1)S(1)} %copy-done.5, ...), custom_call_target="tpu_custom_call" | custom-call | flops 2000000000 | bytes 1464320 | tf_op jit(solution)/shard_map/pallas_call | solution.py:316
  45.6 25.8 %all_to_all.21 = bf16[128,8,256]{2,1,0:T(8,128)(2,1)S(1)} all-to-all(bf16[128,8,256]{2,1,0:T(8,128)(2,1)S(1)} %bitcast.23), channel_id=1, replica_groups=mesh['graph_0'=8,'graph_1'=8,'graph_2'=2,'sample'=4] {'graph_0','graph_1..., dimensions={0} | all-to-all | bytes 1048576 | tf_op jit(solution)/shard_map/all_to_all | solution.py:330
  71.4 0.0 copy-done
  71.4 0.0 copy-done.1
  71.4 0.0 copy-done.2
  71.4 0.0 copy-done.4
  71.4 0.0 copy-done.11
  71.4 0.0 copy-done.12
  71.4 3.9 %shard_map.186 = (bf16[1,128,512]{2,1,0:T(8,128)(2,1)}, bf16[1024,256]{1,0:T(8,128)(2,1)S(1)}, bf16[640,512]{1,0:T(8,128)(2,1)S(1)}, bf16[640,512]{1,0:T(8,128)(...) custom-call(s32[1]{0:T(128)S(6)} %sub.6.sibling_ref, ...), custom_call_target="tpu_custom_call" | custom-call | flops 3000000000 | bytes 2363396 | tf_op jit(solution)/shard_map/pallas_call | solution.py:316
  75.3 1.9 %collective-permute-start = (bf16[1536,256]{1,0:T(8,128)(2,1)S(1)}, bf16[1536,256]{1,0:T(8,128)(2,1)S(1)}, u32[]{:S(2)}, u32[]{:S(2)}) collective-permute-start(bf16[1536,256]{1,0:T(8,128)(2,1)S(1)} %get-tuple-element.38), channel_id=1, source_target_pairs={{0,4},{4,0},{1,5},{5,1},{2,6},{6,2},{3,7},{7,3},{8,12},{12,8},{9,1... | collective-permute-start | bytes 2359304 | tf_op jit(solution)/shard_map/ppermute | solution.py:339
  77.2 0.8 shard_map.187
  78.0 1.4 %collective-permute-done = bf16[1536,256]{1,0:T(8,128)(2,1)S(1)} collective-permute-done((bf16[1536,256]{1,0:T(8,128)(2,1)S(1)}, bf16[1536,256]{1,0:T(8,128)(2,1)S(1)}, u32[]{:S(2)}, u32[]{:S(2)}) %collective-permute-start) | collective-permute-done | bytes 786464 | tf_op jit(solution)/shard_map/ppermute | solution.py:339
  79.5 0.2 shard_map.188
  79.7 37.4 %all_to_all.22 = bf16[64,8,1280]{2,1,0:T(8,128)(2,1)S(1)} all-to-all(bf16[64,8,1280]{2,1,0:T(8,128)(2,1)S(1)} %shard_map.188), channel_id=1, replica_groups=mesh['graph_0'=8,'graph_1'=8,'graph_2'=2,'sample'=4] {'graph_0','graph_1'}, dimensions={0} | all-to-all | bytes 2621440 | tf_op jit(solution)/shard_map/all_to_all | solution.py:330
  117.1 0.2 shard_map.189
  117.2 5.2 %collective-permute-start.1 = (bf16[512,256]{1,0:T(8,128)(2,1)S(1)}, bf16[512,256]{1,0:T(8,128)(2,1)S(1)}, u32[]{:S(2)}, u32[]{:S(2)}) collective-permute-start(bf16[512,256]{1,0:T(8,128)(2,1)S(1)} %get-tuple-element.43), channel_id=1, source_target_pairs={{0,4},{4,0},{1,5},{5,1},{2,6},{6,2},{3,7},{7,3},{8,12},{12,8},{9,1... | collective-permute-start | bytes 786440 | tf_op jit(solution)/shard_map/ppermute | solution.py:356
  122.5 9.5 %all_to_all.23 = f32[8,16,256]{2,1,0:T(8,128)S(1)} all-to-all(f32[8,16,256]{2,1,0:T(8,128)S(1)} %bitcast.26), channel_id=1, replica_groups=mesh['graph_0'=8,'graph_1'=8,'graph_2'=2,'sample'=4] {'sample','graph_2'}, dimensions={0} | all-to-all | bytes 262144 | tf_op jit(solution)/shard_map/all_to_all | solution.py:330
  132.0 0.0 collective-permute-done.1.other_ref
  132.0 1.5 %shard_map.190 = (f32[12,512]{1,0:T(8,128)}, f32[1,128,512]{2,1,0:T(8,128)}) custom-call(s32[1]{0:T(128)S(6)} %sub.7.sibling_ref, f32[4,2,16,256]{3,2,1,0:T(8,128)S(1)} %bitcast.25, bf16[512,1280]{1,0:T(8,128)(2,1)S(1)} %bitcast.18, bf16[512,256]{1,0:T(8,128)(2,1)S(1)} %collective-permute-done.1.other_ref, s32[1,4,128]{2,1,0:T(4,128)S(1)} %bitcast.32, ...), custom_call_target="tpu_custom_call" | custom-call | flops 1000000000 | bytes 2492420 | tf_op jit(solution)/shard_map/pallas_call | solution.py:316
Async XLA Ops:
  0.6 41.6 %copy-start.13 = (s32[1,128,4]{1,2,0:T(4,128)S(1)}, s32[1,128,4]{1,2,0:T(4,128)}, u32[]{:S(2)}) copy-start(s32[1,128,4]{1,2,0:T(4,128)} %param.31) | copy-start | bytes 6148
  0.6 41.6 %copy-start.9 = (s32[1024]{0:T(1024)S(1)}, s32[1024]{0:T(1024)}, u32[]{:S(2)}) copy-start(s32[1024]{0:T(1024)} %param.30) | copy-start | bytes 12292
  0.7 41.6 %copy-start.8 = (s32[1024]{0:T(1024)S(1)}, s32[1024]{0:T(1024)}, u32[]{:S(2)}) copy-start(s32[1024]{0:T(1024)} %param.29) | copy-start | bytes 12292
  0.7 41.6 %copy-start.10 = (bf16[4,512]{1,0:T(4,128)(2,1)S(1)}, bf16[4,512]{1,0:T(4,128)(2,1)}, u32[]{:S(2)}) copy-start(bf16[4,512]{1,0:T(4,128)(2,1)} %w_geo_ref.1) | copy-start | bytes 12292
  0.7 41.6 %copy-start.3 = (bf16[512,512]{1,0:T(8,128)(2,1)S(1)}, bf16[512,512]{1,0:T(8,128)(2,1)}, u32[]{:S(2)}) copy-start(bf16[512,512]{1,0:T(8,128)(2,1)} %w_g2m_ref.1) | copy-start | bytes 1572868
  0.7 41.6 %copy-start.5 = (bf16[256,512]{1,0:T(8,128)(2,1)S(1)}, bf16[256,512]{1,0:T(8,128)(2,1)}, u32[]{:S(2)}) copy-start(bf16[256,512]{1,0:T(8,128)(2,1)} %w_embed_ref.1) | copy-start | bytes 786436
  0.7 41.6 %copy-start.7 = (bf16[4,1024]{1,0:T(4,128)(2,1)S(1)}, bf16[4,1024]{1,0:T(4,128)(2,1)}, u32[]{:S(2)}) copy-start(bf16[4,1024]{1,0:T(4,128)(2,1)} %geometry_ref.1) | copy-start | bytes 24580
  0.7 41.6 %copy-start.6 = (bf16[1,128,512]{2,1,0:T(8,128)(2,1)S(1)}, bf16[1,128,512]{2,1,0:T(8,128)(2,1)}, u32[]{:S(2)}) copy-start(bf16[1,128,512]{2,1,0:T(8,128)(2,1)} %init_ref.1) | copy-start | bytes 393220
  42.3 29.1 %copy-start = (bf16[512,512]{1,0:T(8,128)(2,1)S(1)}, bf16[512,512]{1,0:T(8,128)(2,1)}, u32[]{:S(2)}) copy-start(bf16[512,512]{1,0:T(8,128)(2,1)} %a_recv_ref.3) | copy-start | bytes 1572868
  42.3 29.1 %copy-start.1 = (bf16[512,512]{1,0:T(8,128)(2,1)S(1)}, bf16[512,512]{1,0:T(8,128)(2,1)}, u32[]{:S(2)}) copy-start(bf16[512,512]{1,0:T(8,128)(2,1)} %a_send_ref.5) | copy-start | bytes 1572868
  42.3 29.1 %copy-start.2 = (bf16[1,128,512]{2,1,0:T(8,128)(2,1)S(1)}, bf16[1,128,512]{2,1,0:T(8,128)(2,1)}, u32[]{:S(2)}) copy-start(bf16[1,128,512]{2,1,0:T(8,128)(2,1)} %cot_ref.3) | copy-start | bytes 393220
  42.3 29.1 %copy-start.4 = (bf16[512,512]{1,0:T(8,128)(2,1)S(1)}, bf16[512,512]{1,0:T(8,128)(2,1)}, u32[]{:S(2)}) copy-start(bf16[512,512]{1,0:T(8,128)(2,1)} %b_node_ref.1) | copy-start | bytes 1572868
  42.3 29.1 %copy-start.11 = (s32[512]{0:T(512)S(1)}, s32[512]{0:T(512)}, u32[]{:S(2)}) copy-start(s32[512]{0:T(512)} %param.32) | copy-start | bytes 6148
  42.4 29.1 %copy-start.12 = (s32[512]{0:T(512)S(1)}, s32[512]{0:T(512)}, u32[]{:S(2)}) copy-start(s32[512]{0:T(512)} %param.33) | copy-start | bytes 6148
  75.3 4.2 %collective-permute-start = (bf16[1536,256]{1,0:T(8,128)(2,1)S(1)}, bf16[1536,256]{1,0:T(8,128)(2,1)S(1)}, u32[]{:S(2)}, u32[]{:S(2)}) collective-permute-start(bf16[1536,256]{1,0:T(8,128)(2,1)S(1)} %get-tuple-element.38), channel_id=1, source_target_pairs={{0,4},{4,0},{1,5},{5,1},{2,6},{6,2},{3,7},{7,3},{8,12},{12,8},{9,1... | collective-permute-start | bytes 2359304 | tf_op jit(solution)/shard_map/ppermute | solution.py:339
  117.2 14.7 %collective-permute-start.1 = (bf16[512,256]{1,0:T(8,128)(2,1)S(1)}, bf16[512,256]{1,0:T(8,128)(2,1)S(1)}, u32[]{:S(2)}, u32[]{:S(2)}) collective-permute-start(bf16[512,256]{1,0:T(8,128)(2,1)S(1)} %get-tuple-element.43), channel_id=1, source_target_pairs={{0,4},{4,0},{1,5},{5,1},{2,6},{6,2},{3,7},{7,3},{8,12},{12,8},{9,1... | collective-permute-start | bytes 786440 | tf_op jit(solution)/shard_map/ppermute | solution.py:356

commit v8 on v5

--- a/solution.py
+++ b/solution.py
@@ -160,10 +160,9 @@
 
 
 def process(
-    slots, sibling_ref, halo_ref, latent_ref, senders_ref, receivers_ref, a_send_ref, a_recv_ref, b_node_ref,
+    slots, halo_ref, latent_ref, senders_ref, receivers_ref, a_send_ref, a_recv_ref, b_node_ref,
     cot_ref,
-    out_ref, back_ref, table_ref, send_grad_ref, recv_grad_ref, aggregate_ref, d_update_ref, send_ref,
-    spread,
+    out_ref, back_ref, table_ref, send_grad_ref, recv_grad_ref, aggregate_ref, d_update_ref, spread,
 ):
     nodes, width = latent_ref.shape
     rows = table_ref.shape[0]
@@ -200,10 +199,6 @@
     for j in range(slots):
         split_store(spread, j, slots, send_grad[j * groups : (j + 1) * groups])
     gather_blocks(spread, back_ref)
-    weight_grads(
-        False, sibling_ref, table_ref, send_grad_ref, latent_ref, recv_grad_ref, aggregate_ref,
-        d_update_ref, send_ref,
-    )
 
 
 def pack(keep_ref, other_ref, back_ref, out_ref):
@@ -403,7 +398,7 @@
     halo, core = lax.optimization_barrier((halo, core))
     sibling = 1 - core
 
-    mesh_out, back, table, send_grad, recv_grad, aggregate, d_update, send = kernel(
+    mesh_out, back, table, send_grad, recv_grad, aggregate, d_update = kernel(
         functools.partial(process, halo_slots),
         (
             shape((1, nodes, width), BF16),
@@ -413,15 +408,11 @@
             shape((nodes, width), BF16),
             shape((nodes, width), BF16),
             shape((nodes, width), BF16),
-            shape((3 * width, half), BF16),
         ),
         [pltpu.VMEM((half // LANES, halves, LANES), F32)],
         3 * 10**9,
-        1,
-        pltpu.SMEM,
-        GRANTS[2],
+        grant=GRANTS[2],
     )(
-        sibling,
         halo.reshape(halves, half),
         latent,
         mesh_senders[None],
@@ -433,6 +424,7 @@
     )
 
     operands = (table, send_grad, latent, recv_grad, aggregate, d_update)
+    send = kernel(functools.partial(weight_grads, False), shape((3 * width, half), BF16), [], 5 * 10**8, 1, pltpu.SMEM)(sibling, *operands)
     keep = kernel(functools.partial(weight_grads, True), shape((3 * width, half), F32), [], 5 * 10**8, 1, pltpu.SMEM)(sibling, *operands)
     arrived, grad_weights = share(keep, send, back, core)
 

time: 133 us -> 133 us (level)
    pallas_call x8 -> x9, Pallas kernels: 13.4 us -> 13.1 us  [call(): pl.pallas_call(body, out_shape=outs, in_specs=specs, out_specs=jax.tree.m...]
where the time goes in v8:
time: 133 us; the launch traced here: 131 us
  blocking collectives  106 us (80%)
  Pallas kernels  13.1 us (10%)
  starting transfers between devices  5.93 us (4%)
  waiting for transfers between devices  4.76 us (4%)
    all_to_all x3, blocking collectives, exchange(): return lax.all_to_all(x, axis, split_axis=0, concat_axis=0, tiled=True)  106 us
    pallas_call x9, Pallas kernels, call(): pl.pallas_call(body, out_shape=outs, in_specs=specs, out_specs=jax.tree.m...  13.1 us
    all_to_all x1, starting transfers between devices, exchange(): return lax.all_to_all(x, axis, split_axis=0, concat_axis=0, tiled=True)  4.01 us
    all_to_all x1, waiting for transfers between devices, exchange(): return lax.all_to_all(x, axis, split_axis=0, concat_axis=0, tiled=True)  3.07 us
  transfers between devices with their start and end apart: 2, of which 2 were waited for; matrix products, arithmetic and copies ran while one was open for 0% of the time, Pallas kernels for 2%

profile of v8, /device:TPU:1, one launch (start us, length us, event | category | flops | bytes accessed | tf_op | source)
XLA Modules:
  0.0 130.8 jit_solution(6517154162576956707)
XLA Ops:
  0.6 0.0 copy-start.13
  0.6 0.0 copy-start.9
  0.7 0.0 copy-start.8
  0.7 0.0 copy-start.10
  0.7 0.0 copy-start
  0.7 0.0 copy-start.4
  0.7 0.0 copy-start.7
  0.7 0.0 copy-start.5
  0.7 2.5 %shard_map.184 = bf16[1024,256]{1,0:T(8,128)(2,1)} custom-call(s32[1,8,128]{2,1,0:T(8,128)} %bitcast.33, s32[1,128]{1,0:T(1,128)} %counts_hbm, bf16[1,512,256]{2,1,0:T(8,128)(2,1)} %grid_hbm.1), custom_call_target="tpu_custom_call" | custom-call | flops 100000000 | bytes 266752 | tf_op jit(solution)/shard_map/pallas_call | solution.py:289
  3.2 39.0 %all_to_all.20 = bf16[128,8,256]{2,1,0:T(8,128)(2,1)S(1)} all-to-all(bf16[128,8,256]{2,1,0:T(8,128)(2,1)} %bitcast.32), channel_id=1, replica_groups=mesh['graph_0'=8,'graph_1'=8,'graph_2'=2,'sample'=4] {'graph_0','graph_1..., dimensions={0} | all-to-all | bytes 1048576 | tf_op jit(solution)/shard_map/all_to_all | solution.py:303
  42.2 0.0 copy-done.13
  42.3 0.0 copy-done.9
  42.3 0.0 copy-done.8
  42.3 0.0 copy-done.10
  42.3 0.0 copy-done
  42.3 0.0 copy-done.4
  42.3 0.0 copy-done.7
  42.3 0.0 copy-done.5
  42.3 0.0 copy-start.1
  42.3 0.0 copy-start.2
  42.3 0.0 copy-start.3
  42.3 0.0 copy-start.6
  42.4 0.0 copy-start.11
  42.4 0.0 copy-start.12
  42.4 3.2 %shard_map.185 = (bf16[128,512]{1,0:T(8,128)(2,1)S(1)}, bf16[1024,256]{1,0:T(8,128)(2,1)S(1)}) custom-call(bf16[1024,256]{1,0:T(8,128)(2,1)S(1)} %bitcast.23, s32[1,1024]{1,0:T(1,128)S(1)} %bitcast.26, s32[1,1024]{1,0:T(1,128)S(1)} %bitcast.27, bf16[4,1024]{1,0:T(4,128)(2,1)S(1)} %copy-done.7, bf16[256,512]{1,0:T(8,128)(2,1)S(1)} %copy-done.4, ...), custom_call_target="tpu_custom_call" | custom-call | flops 2000000000 | bytes 1464320 | tf_op jit(solution)/shard_map/pallas_call | solution.py:289
  45.6 25.8 %all_to_all.21 = bf16[128,8,256]{2,1,0:T(8,128)(2,1)S(1)} all-to-all(bf16[128,8,256]{2,1,0:T(8,128)(2,1)S(1)} %bitcast.24), channel_id=1, replica_groups=mesh['graph_0'=8,'graph_1'=8,'graph_2'=2,'sample'=4] {'graph_0','graph_1..., dimensions={0} | all-to-all | bytes 1048576 | tf_op jit(solution)/shard_map/all_to_all | solution.py:303
  71.4 0.0 copy-done.1
  71.4 0.0 copy-done.2
  71.4 0.0 copy-done.3
  71.4 0.0 copy-done.6
  71.4 0.0 copy-done.11
  71.4 0.0 copy-done.12
  71.4 3.0 %shard_map.186 = (bf16[1,128,512]{2,1,0:T(8,128)(2,1)}, bf16[1024,256]{1,0:T(8,128)(2,1)S(1)}, bf16[640,512]{1,0:T(8,128)(2,1)S(1)}, bf16[640,512]{1,0:T(8,128)(...) custom-call(bf16[1024,256]{1,0:T(8,128)(2,1)S(1)} %bitcast.22, ...), custom_call_target="tpu_custom_call" | custom-call | flops 3000000000 | bytes 2363392 | tf_op jit(solution)/shard_map/pallas_call | solution.py:289
  74.5 0.6 shard_map.188
  75.0 1.9 %collective-permute-start = (bf16[1536,256]{1,0:T(8,128)(2,1)S(1)}, bf16[1536,256]{1,0:T(8,128)(2,1)S(1)}, u32[]{:S(2)}, u32[]{:S(2)}) collective-permute-start(bf16[1536,256]{1,0:T(8,128)(2,1)S(1)} %shard_map.188), channel_id=1, source_target_pairs={{0,4},{4,0},{1,5},{5,1},{2,6},{6,2},{3,7},{7,3},{8,12},{12,8},{9,1... | collective-permute-start | bytes 2359304 | tf_op jit(solution)/shard_map/ppermute | solution.py:312
  77.0 0.6 shard_map.187
  77.5 1.7 %collective-permute-done = bf16[1536,256]{1,0:T(8,128)(2,1)S(1)} collective-permute-done((bf16[1536,256]{1,0:T(8,128)(2,1)S(1)}, bf16[1536,256]{1,0:T(8,128)(2,1)S(1)}, u32[]{:S(2)}, u32[]{:S(2)}) %collective-permute-start) | collective-permute-done | bytes 786464 | tf_op jit(solution)/shard_map/ppermute | solution.py:312
  79.2 0.3 shard_map.189
  79.5 41.3 %all_to_all.22 = bf16[128,8,640]{2,1,0:T(8,128)(2,1)S(1)} all-to-all(bf16[128,8,640]{2,1,0:T(8,128)(2,1)S(1)} %bitcast.20), channel_id=1, replica_groups=mesh['graph_0'=8,'graph_1'=8,'graph_2'=2,'sample'=4] {'graph_0','graph_1..., dimensions={0} | all-to-all | bytes 2621440 | tf_op jit(solution)/shard_map/all_to_all | solution.py:303
  120.7 0.8 shard_map.191
  121.5 4.0 %all-to-all-start.3 = ((f32[4,2,8,384]{3,2,1,0:T(8,128)}), f32[4,2,8,384]{3,2,1,0:T(8,128)S(1)}, u32[]{:S(2)}, u32[]{:S(2)}) async-start(f32[4,2,8,384]{3,2,1,0:T(8,128)} %shard_map.191), calls=%async_computation.3 | async-start | bytes 196608 | tf_op jit(solution)/shard_map/all_to_all | solution.py:303
  125.5 1.6 %shard_map.190 = f32[1,128,512]{2,1,0:T(8,128)} custom-call(bf16[1024,640]{1,0:T(8,128)(2,1)S(1)} %bitcast.19, s32[1,4,128]{2,1,0:T(4,128)S(1)} %bitcast.31, bf16[640,512]{1,0:T(8,128)(2,1)S(1)} %get-tuple-element.26.send_grad_ref, bf16[128,512]{1,0:T(8,128)(2,1)S(1)} %get-tuple-element.27.recv_grad_ref, bf16[512,512]{1,0:T(8,128)(2,1)S(1)} %copy-done.2, ...), custom_call_target="tpu_custom_call" | custom-call | flops 1000000000 | bytes 3278848 | tf_op jit(solution)/shard_map/pallas_call | solution.py:289
  127.1 3.1 %all-to-all-done.3.arrived_ref = f32[4,2,8,384]{3,2,1,0:T(8,128)S(1)} async-done(((f32[4,2,8,384]{3,2,1,0:T(8,128)}), f32[4,2,8,384]{3,2,1,0:T(8,128)S(1)}, u32[]{:S(2)}, u32[]{:S(2)}) %all-to-all-start.3) | async-done | bytes 98336 | tf_op jit(solution)/shard_map/all_to_all | solution.py:303
  130.2 0.6 shard_map.192
Async XLA Ops:
  0.6 41.6 %copy-start.13 = (s32[1,128,4]{1,2,0:T(4,128)S(1)}, s32[1,128,4]{1,2,0:T(4,128)}, u32[]{:S(2)}) copy-start(s32[1,128,4]{1,2,0:T(4,128)} %param.31) | copy-start | bytes 6148
  0.6 41.6 %copy-start.9 = (s32[1024]{0:T(1024)S(1)}, s32[1024]{0:T(1024)}, u32[]{:S(2)}) copy-start(s32[1024]{0:T(1024)} %param.30) | copy-start | bytes 12292
  0.7 41.6 %copy-start.8 = (s32[1024]{0:T(1024)S(1)}, s32[1024]{0:T(1024)}, u32[]{:S(2)}) copy-start(s32[1024]{0:T(1024)} %param.29) | copy-start | bytes 12292
  0.7 41.6 %copy-start.10 = (bf16[4,512]{1,0:T(4,128)(2,1)S(1)}, bf16[4,512]{1,0:T(4,128)(2,1)}, u32[]{:S(2)}) copy-start(bf16[4,512]{1,0:T(4,128)(2,1)} %w_geo_ref.1) | copy-start | bytes 12292
  0.7 41.6 %copy-start = (bf16[512,512]{1,0:T(8,128)(2,1)S(1)}, bf16[512,512]{1,0:T(8,128)(2,1)}, u32[]{:S(2)}) copy-start(bf16[512,512]{1,0:T(8,128)(2,1)} %w_g2m_ref.1) | copy-start | bytes 1572868
  0.7 41.6 %copy-start.4 = (bf16[256,512]{1,0:T(8,128)(2,1)S(1)}, bf16[256,512]{1,0:T(8,128)(2,1)}, u32[]{:S(2)}) copy-start(bf16[256,512]{1,0:T(8,128)(2,1)} %w_embed_ref.1) | copy-start | bytes 786436
  0.7 41.6 %copy-start.7 = (bf16[4,1024]{1,0:T(4,128)(2,1)S(1)}, bf16[4,1024]{1,0:T(4,128)(2,1)}, u32[]{:S(2)}) copy-start(bf16[4,1024]{1,0:T(4,128)(2,1)} %geometry_ref.1) | copy-start | bytes 24580
  0.7 41.6 %copy-start.5 = (bf16[1,128,512]{2,1,0:T(8,128)(2,1)S(1)}, bf16[1,128,512]{2,1,0:T(8,128)(2,1)}, u32[]{:S(2)}) copy-start(bf16[1,128,512]{2,1,0:T(8,128)(2,1)} %init_ref.1) | copy-start | bytes 393220
  42.3 29.1 %copy-start.1 = (bf16[512,512]{1,0:T(8,128)(2,1)S(1)}, bf16[512,512]{1,0:T(8,128)(2,1)}, u32[]{:S(2)}) copy-start(bf16[512,512]{1,0:T(8,128)(2,1)} %b_node_ref.1) | copy-start | bytes 1572868
  42.3 29.1 %copy-start.2 = (bf16[512,512]{1,0:T(8,128)(2,1)S(1)}, bf16[512,512]{1,0:T(8,128)(2,1)}, u32[]{:S(2)}) copy-start(bf16[512,512]{1,0:T(8,128)(2,1)} %a_send_ref.3) | copy-start | bytes 1572868
  42.3 29.1 %copy-start.3 = (bf16[512,512]{1,0:T(8,128)(2,1)S(1)}, bf16[512,512]{1,0:T(8,128)(2,1)}, u32[]{:S(2)}) copy-start(bf16[512,512]{1,0:T(8,128)(2,1)} %a_recv_ref.3) | copy-start | bytes 1572868
  42.3 29.1 %copy-start.6 = (bf16[1,128,512]{2,1,0:T(8,128)(2,1)S(1)}, bf16[1,128,512]{2,1,0:T(8,128)(2,1)}, u32[]{:S(2)}) copy-start(bf16[1,128,512]{2,1,0:T(8,128)(2,1)} %cot_ref.3) | copy-start | bytes 393220
  42.4 29.1 %copy-start.11 = (s32[512]{0:T(512)S(1)}, s32[512]{0:T(512)}, u32[]{:S(2)}) copy-start(s32[512]{0:T(512)} %param.32) | copy-start | bytes 6148
  42.4 29.1 %copy-start.12 = (s32[512]{0:T(512)S(1)}, s32[512]{0:T(512)}, u32[]{:S(2)}) copy-start(s32[512]{0:T(512)} %param.33) | copy-start | bytes 6148
  75.0 4.2 %collective-permute-start = (bf16[1536,256]{1,0:T(8,128)(2,1)S(1)}, bf16[1536,256]{1,0:T(8,128)(2,1)S(1)}, u32[]{:S(2)}, u32[]{:S(2)}) collective-permute-start(bf16[1536,256]{1,0:T(8,128)(2,1)S(1)} %shard_map.188), channel_id=1, source_target_pairs={{0,4},{4,0},{1,5},{5,1},{2,6},{6,2},{3,7},{7,3},{8,12},{12,8},{9,1... | collective-permute-start | bytes 2359304 | tf_op jit(solution)/shard_map/ppermute | solution.py:312
  121.5 8.7 %all-to-all-start.3 = ((f32[4,2,8,384]{3,2,1,0:T(8,128)}), f32[4,2,8,384]{3,2,1,0:T(8,128)S(1)}, u32[]{:S(2)}, u32[]{:S(2)}) async-start(f32[4,2,8,384]{3,2,1,0:T(8,128)} %shard_map.191), calls=%async_computation.3 | async-start | bytes 196608 | tf_op jit(solution)/shard_map/all_to_all | solution.py:303

commit v9 on v6

--- a/solution.py
+++ b/solution.py
@@ -289,14 +289,6 @@
     out_ref[0] = local_ref[...] + (times_transposed(high, a_send) + times_transposed(low, a_send))
 
 
-def finish(
-    sibling_ref, copies_ref, back_ref, send_rows_ref, a_send_ref, local_ref, weights_ref, mesh_ref,
-    spread,
-):
-    add_samples(sibling_ref, copies_ref, weights_ref)
-    return_grads(back_ref, send_rows_ref, a_send_ref, local_ref, mesh_ref, spread)
-
-
 def shape(dims, dtype):
     return jax.ShapeDtypeStruct(dims, dtype)
 
@@ -455,14 +447,15 @@
         pltpu.SMEM,
     )(sibling, *operands, a_send, a_recv, cotangent)
     arrived, copies, sibling = share(keep, send, back, core)
-    grad_weights, grad_mesh = kernel(
-        finish,
-        (shape((3 * width // groups, width), F32), shape((1, nodes, width), F32)),
+    grad_weights = kernel(
+        add_samples, shape((3 * width // groups, width), F32), [], 10**6, 1, pltpu.SMEM
+    )(sibling, copies)
+    grad_mesh = kernel(
+        return_grads,
+        shape((1, nodes, width), F32),
         [pltpu.VMEM((half // LANES, halves, LANES), F32)],
         10**9,
-        1,
-        pltpu.SMEM,
-    )(sibling, copies, arrived, mesh_rows, a_send, local)
+    )(arrived, mesh_rows, a_send, local)
     return (mesh_out, grad_mesh, grad_weights)
 
 

time: 133 us -> 133 us (level)
  blocking collectives: 115 us -> 106 us
  starting transfers between devices: 1.91 us -> 5.92 us
  waiting for transfers between devices: 1.45 us -> 4.65 us
    all_to_all x4 -> x3, blocking collectives: 115 us -> 106 us  [exchange(): return lax.all_to_all(x, axis, split_axis=0, concat_axis=0, tiled=True)]
    all_to_all x0 -> x1, starting transfers between devices: none -> 4.01 us  [exchange(): return lax.all_to_all(x, axis, split_axis=0, concat_axis=0, tiled=True)]
    all_to_all x0 -> x1, waiting for transfers between devices: none -> 3.2 us  [exchange(): return lax.all_to_all(x, axis, split_axis=0, concat_axis=0, tiled=True)]
    pallas_call x7 -> x8, Pallas kernels: 12.2 us -> 13.5 us  [call(): pl.pallas_call(body, out_shape=outs, in_specs=specs, out_specs=jax.tree.m...]
  transfers between devices with their start and end apart: 1 -> 2, of which waited for: 1 -> 2; matrix products, arithmetic and copies ran while one was open for 0% -> 0% of each run, Pallas kernels for 1% -> 2%
where the time goes in v9:
time: 133 us; the launch traced here: 131 us
  blocking collectives  106 us (80%)
  Pallas kernels  13.5 us (10%)
  starting transfers between devices  5.92 us (4%)
  waiting for transfers between devices  4.65 us (3%)
    all_to_all x3, blocking collectives, exchange(): return lax.all_to_all(x, axis, split_axis=0, concat_axis=0, tiled=True)  106 us
    pallas_call x8, Pallas kernels, call(): pl.pallas_call(body, out_shape=outs, in_specs=specs, out_specs=jax.tree.m...  13.5 us
    all_to_all x1, starting transfers between devices, exchange(): return lax.all_to_all(x, axis, split_axis=0, concat_axis=0, tiled=True)  4.01 us
    all_to_all x1, waiting for transfers between devices, exchange(): return lax.all_to_all(x, axis, split_axis=0, concat_axis=0, tiled=True)  3.2 us
  transfers between devices with their start and end apart: 2, of which 2 were waited for; matrix products, arithmetic and copies ran while one was open for 0% of the time, Pallas kernels for 2%

profile of v9, /device:TPU:1, one launch (start us, length us, event | category | flops | bytes accessed | tf_op | source)
XLA Modules:
  0.0 131.0 jit_solution(3401881177176498228)
XLA Ops:
  0.6 0.0 copy-start.13
  0.6 0.0 copy-start.9
  0.7 0.0 copy-start.8
  0.7 0.0 copy-start.10
  0.7 0.0 copy-start.3
  0.7 0.0 copy-start.5
  0.7 0.0 copy-start.7
  0.7 0.0 copy-start.6
  0.7 2.5 %shard_map.184 = bf16[1024,256]{1,0:T(8,128)(2,1)} custom-call(s32[1,8,128]{2,1,0:T(8,128)} %bitcast.33, s32[1,128]{1,0:T(1,128)} %counts_hbm, bf16[1,512,256]{2,1,0:T(8,128)(2,1)} %grid_hbm.1), custom_call_target="tpu_custom_call" | custom-call | flops 100000000 | bytes 266752 | tf_op jit(solution)/shard_map/pallas_call | solution.py:303
  3.2 39.0 %all_to_all.20 = bf16[128,8,256]{2,1,0:T(8,128)(2,1)S(1)} all-to-all(bf16[128,8,256]{2,1,0:T(8,128)(2,1)} %bitcast.32), channel_id=1, replica_groups=mesh['graph_0'=8,'graph_1'=8,'graph_2'=2,'sample'=4] {'graph_0','graph_1..., dimensions={0} | all-to-all | bytes 1048576 | tf_op jit(solution)/shard_map/all_to_all | solution.py:317
  42.2 0.0 copy-done.13
  42.2 0.0 copy-done.9
  42.2 0.0 copy-done.8
  42.3 0.0 copy-done.10
  42.3 0.0 copy-done.3
  42.3 0.0 copy-done.5
  42.3 0.0 copy-done.7
  42.3 0.0 copy-done.6
  42.3 0.0 copy-start
  42.3 0.0 copy-start.1
  42.3 0.0 copy-start.2
  42.3 0.0 copy-start.4
  42.3 0.0 copy-start.11
  42.4 0.0 copy-start.12
  42.4 3.2 %shard_map.185 = (bf16[128,512]{1,0:T(8,128)(2,1)S(1)}, bf16[1024,256]{1,0:T(8,128)(2,1)S(1)}) custom-call(bf16[1024,256]{1,0:T(8,128)(2,1)S(1)} %bitcast.23, s32[1,1024]{1,0:T(1,128)S(1)} %bitcast.26, s32[1,1024]{1,0:T(1,128)S(1)} %bitcast.27, bf16[4,1024]{1,0:T(4,128)(2,1)S(1)} %copy-done.7, bf16[256,512]{1,0:T(8,128)(2,1)S(1)} %copy-done.5, ...), custom_call_target="tpu_custom_call" | custom-call | flops 2000000000 | bytes 1464320 | tf_op jit(solution)/shard_map/pallas_call | solution.py:303
  45.6 25.8 %all_to_all.21 = bf16[128,8,256]{2,1,0:T(8,128)(2,1)S(1)} all-to-all(bf16[128,8,256]{2,1,0:T(8,128)(2,1)S(1)} %bitcast.24), channel_id=1, replica_groups=mesh['graph_0'=8,'graph_1'=8,'graph_2'=2,'sample'=4] {'graph_0','graph_1..., dimensions={0} | all-to-all | bytes 1048576 | tf_op jit(solution)/shard_map/all_to_all | solution.py:317
  71.4 0.0 copy-done
  71.4 0.0 copy-done.1
  71.4 0.0 copy-done.2
  71.4 0.0 copy-done.4
  71.4 0.0 copy-done.11
  71.4 0.0 copy-done.12
  71.4 3.9 %shard_map.186 = (bf16[1,128,512]{2,1,0:T(8,128)(2,1)}, bf16[1024,256]{1,0:T(8,128)(2,1)S(1)}, bf16[640,512]{1,0:T(8,128)(2,1)S(1)}, bf16[640,512]{1,0:T(8,128)(...) custom-call(s32[1]{0:T(128)S(6)} %sub.6.sibling_ref, ...), custom_call_target="tpu_custom_call" | custom-call | flops 3000000000 | bytes 2363396 | tf_op jit(solution)/shard_map/pallas_call | solution.py:303
  75.3 1.9 %collective-permute-start = (bf16[1536,256]{1,0:T(8,128)(2,1)S(1)}, bf16[1536,256]{1,0:T(8,128)(2,1)S(1)}, u32[]{:S(2)}, u32[]{:S(2)}) collective-permute-start(bf16[1536,256]{1,0:T(8,128)(2,1)S(1)} %get-tuple-element.34), channel_id=1, source_target_pairs={{0,4},{4,0},{1,5},{5,1},{2,6},{6,2},{3,7},{7,3},{8,12},{12,8},{9,1... | collective-permute-start | bytes 2359304 | tf_op jit(solution)/shard_map/ppermute | solution.py:326
  77.2 0.8 shard_map.187
  78.0 1.4 %collective-permute-done = bf16[1536,256]{1,0:T(8,128)(2,1)S(1)} collective-permute-done((bf16[1536,256]{1,0:T(8,128)(2,1)S(1)}, bf16[1536,256]{1,0:T(8,128)(2,1)S(1)}, u32[]{:S(2)}, u32[]{:S(2)}) %collective-permute-start) | collective-permute-done | bytes 786464 | tf_op jit(solution)/shard_map/ppermute | solution.py:326
  79.4 0.3 shard_map.188
  79.7 41.3 %all_to_all.22 = bf16[128,8,640]{2,1,0:T(8,128)(2,1)S(1)} all-to-all(bf16[128,8,640]{2,1,0:T(8,128)(2,1)S(1)} %bitcast.19), channel_id=1, replica_groups=mesh['graph_0'=8,'graph_1'=8,'graph_2'=2,'sample'=4] {'graph_0','graph_1..., dimensions={0} | all-to-all | bytes 2621440 | tf_op jit(solution)/shard_map/all_to_all | solution.py:317
  121.0 0.8 shard_map.190
  121.7 4.0 %all-to-all-start.3 = ((f32[4,2,8,384]{3,2,1,0:T(8,128)}), f32[4,2,8,384]{3,2,1,0:T(8,128)S(1)}, u32[]{:S(2)}, u32[]{:S(2)}) async-start(f32[4,2,8,384]{3,2,1,0:T(8,128)} %shard_map.190), calls=%async_computation.3 | async-start | bytes 196608 | tf_op jit(solution)/shard_map/all_to_all | solution.py:317
  125.8 1.5 %shard_map.189 = f32[1,128,512]{2,1,0:T(8,128)} custom-call(bf16[1024,640]{1,0:T(8,128)(2,1)S(1)} %bitcast.18, s32[1,4,128]{2,1,0:T(4,128)S(1)} %bitcast.31, bf16[512,512]{1,0:T(8,128)(2,1)S(1)} %copy-done.1, f32[128,512]{1,0:T(8,128)S(1)} %get-tuple-element.36.local_ref), custom_call_target="tpu_custom_call" | custom-call | flops 1000000000 | bytes 2099200 | tf_op jit(solution)/shard_map/pallas_call | solution.py:303
  127.2 3.2 %all-to-all-done.3.arrived_ref = f32[4,2,8,384]{3,2,1,0:T(8,128)S(1)} async-done(((f32[4,2,8,384]{3,2,1,0:T(8,128)}), f32[4,2,8,384]{3,2,1,0:T(8,128)S(1)}, u32[]{:S(2)}, u32[]{:S(2)}) %all-to-all-start.3) | async-done | bytes 98336 | tf_op jit(solution)/shard_map/all_to_all | solution.py:317
  130.4 0.6 shard_map.191
Async XLA Ops:
  0.6 41.6 %copy-start.13 = (s32[1,128,4]{1,2,0:T(4,128)S(1)}, s32[1,128,4]{1,2,0:T(4,128)}, u32[]{:S(2)}) copy-start(s32[1,128,4]{1,2,0:T(4,128)} %param.31) | copy-start | bytes 6148
  0.6 41.6 %copy-start.9 = (s32[1024]{0:T(1024)S(1)}, s32[1024]{0:T(1024)}, u32[]{:S(2)}) copy-start(s32[1024]{0:T(1024)} %param.30) | copy-start | bytes 12292
  0.7 41.6 %copy-start.8 = (s32[1024]{0:T(1024)S(1)}, s32[1024]{0:T(1024)}, u32[]{:S(2)}) copy-start(s32[1024]{0:T(1024)} %param.29) | copy-start | bytes 12292
  0.7 41.6 %copy-start.10 = (bf16[4,512]{1,0:T(4,128)(2,1)S(1)}, bf16[4,512]{1,0:T(4,128)(2,1)}, u32[]{:S(2)}) copy-start(bf16[4,512]{1,0:T(4,128)(2,1)} %w_geo_ref.1) | copy-start | bytes 12292
  0.7 41.6 %copy-start.3 = (bf16[512,512]{1,0:T(8,128)(2,1)S(1)}, bf16[512,512]{1,0:T(8,128)(2,1)}, u32[]{:S(2)}) copy-start(bf16[512,512]{1,0:T(8,128)(2,1)} %w_g2m_ref.1) | copy-start | bytes 1572868
  0.7 41.6 %copy-start.5 = (bf16[256,512]{1,0:T(8,128)(2,1)S(1)}, bf16[256,512]{1,0:T(8,128)(2,1)}, u32[]{:S(2)}) copy-start(bf16[256,512]{1,0:T(8,128)(2,1)} %w_embed_ref.1) | copy-start | bytes 786436
  0.7 41.6 %copy-start.7 = (bf16[4,1024]{1,0:T(4,128)(2,1)S(1)}, bf16[4,1024]{1,0:T(4,128)(2,1)}, u32[]{:S(2)}) copy-start(bf16[4,1024]{1,0:T(4,128)(2,1)} %geometry_ref.1) | copy-start | bytes 24580
  0.7 41.6 %copy-start.6 = (bf16[1,128,512]{2,1,0:T(8,128)(2,1)S(1)}, bf16[1,128,512]{2,1,0:T(8,128)(2,1)}, u32[]{:S(2)}) copy-start(bf16[1,128,512]{2,1,0:T(8,128)(2,1)} %init_ref.1) | copy-start | bytes 393220
  42.3 29.1 %copy-start = (bf16[512,512]{1,0:T(8,128)(2,1)S(1)}, bf16[512,512]{1,0:T(8,128)(2,1)}, u32[]{:S(2)}) copy-start(bf16[512,512]{1,0:T(8,128)(2,1)} %a_recv_ref.3) | copy-start | bytes 1572868
  42.3 29.1 %copy-start.1 = (bf16[512,512]{1,0:T(8,128)(2,1)S(1)}, bf16[512,512]{1,0:T(8,128)(2,1)}, u32[]{:S(2)}) copy-start(bf16[512,512]{1,0:T(8,128)(2,1)} %a_send_ref.5) | copy-start | bytes 1572868
  42.3 29.1 %copy-start.2 = (bf16[1,128,512]{2,1,0:T(8,128)(2,1)S(1)}, bf16[1,128,512]{2,1,0:T(8,128)(2,1)}, u32[]{:S(2)}) copy-start(bf16[1,128,512]{2,1,0:T(8,128)(2,1)} %cot_ref.3) | copy-start | bytes 393220
  42.3 29.1 %copy-start.4 = (bf16[512,512]{1,0:T(8,128)(2,1)S(1)}, bf16[512,512]{1,0:T(8,128)(2,1)}, u32[]{:S(2)}) copy-start(bf16[512,512]{1,0:T(8,128)(2,1)} %b_node_ref.1) | copy-start | bytes 1572868
  42.3 29.1 %copy-start.11 = (s32[512]{0:T(512)S(1)}, s32[512]{0:T(512)}, u32[]{:S(2)}) copy-start(s32[512]{0:T(512)} %param.32) | copy-start | bytes 6148
  42.4 29.1 %copy-start.12 = (s32[512]{0:T(512)S(1)}, s32[512]{0:T(512)}, u32[]{:S(2)}) copy-start(s32[512]{0:T(512)} %param.33) | copy-start | bytes 6148
  75.3 4.2 %collective-permute-start = (bf16[1536,256]{1,0:T(8,128)(2,1)S(1)}, bf16[1536,256]{1,0:T(8,128)(2,1)S(1)}, u32[]{:S(2)}, u32[]{:S(2)}) collective-permute-start(bf16[1536,256]{1,0:T(8,128)(2,1)S(1)} %get-tuple-element.34), channel_id=1, source_target_pairs={{0,4},{4,0},{1,5},{5,1},{2,6},{6,2},{3,7},{7,3},{8,12},{12,8},{9,1... | collective-permute-start | bytes 2359304 | tf_op jit(solution)/shard_map/ppermute | solution.py:326
  121.7 8.7 %all-to-all-start.3 = ((f32[4,2,8,384]{3,2,1,0:T(8,128)}), f32[4,2,8,384]{3,2,1,0:T(8,128)S(1)}, u32[]{:S(2)}, u32[]{:S(2)}) async-start(f32[4,2,8,384]{3,2,1,0:T(8,128)} %shard_map.190), calls=%async_computation.3 | async-start | bytes 196608 | tf_op jit(solution)/shard_map/all_to_all | solution.py:317
